TPU v7x, 128 devices: a whole 4x4x4 slice. The times are simulated.
128 devices in a mesh: group: 16 (over z, y), inner: 8 (over x, core).
Axes of the slice: x: 4, y: 4, z: 4, core: 2. Of those that a mesh axis runs over, the one named last changes fastest.
Arguments:
- tokens: bfloat16 [16384, 7168], P(('group', 'inner')), may hold values from -6 to 6
- target: int32 [16384], P(('group', 'inner')), may hold values from 0 to 16, as said below
- gate_scale: float32 [16384], P(('group', 'inner')), may hold values from 0.25 to 2.5
- gate_weight: bfloat16 [16, 7168, 2048], P('group', None, 'inner'), may hold values from -0.0625 to 0.0625
- up_weight: bfloat16 [16, 7168, 2048], P('group', None, 'inner'), may hold values from -0.0625 to 0.0625
- down_weight: bfloat16 [16, 2048, 7168], P('group', 'inner'), may hold values from -0.125 to 0.125
Outputs:
- routed_out: bfloat16 [16384, 7168], P(('group', 'inner'))
Inputs may be any that keep to these rules, and one draw needn't show every extreme that they name: 16 means that the token uses no expert of this round. Among the 128 tokens of one device at most 10 target any one group, and in every device some group is targeted by exactly 10 of them.
All inputs are finite; a program needn't handle non-finite values.
Results may differ from a plain program's by a relative error of at most 0.0095.
Values may be sent and summed in bfloat16 or wider, within the bound.
A program may use at most 192 MiB of HBM per device.

v0:
```python
import jax
import jax.numpy as jnp
from jax import lax
from jax.sharding import PartitionSpec as P


def expert_part(rows_in, gate_mat, up_mat, down_mat):
    gate_pre = jnp.dot(rows_in, gate_mat, preferred_element_type=jnp.float32)
    up_pre = jnp.dot(rows_in, up_mat, preferred_element_type=jnp.float32)
    hidden = (jax.nn.silu(gate_pre) * up_pre).astype(jnp.bfloat16)
    return jnp.dot(hidden, down_mat, preferred_element_type=jnp.float32)


def body(tokens, target, gate_scale, gate_weight, up_weight, down_weight):
    groups = lax.axis_size("group")
    inner_size = lax.axis_size("inner")
    tok_count = tokens.shape[0]
    model_width = tokens.shape[1]
    capacity = tok_count * 5 // (4 * groups)
    slot_count = groups * capacity
    onehot = (target[:, None] == jnp.arange(groups, dtype=jnp.int32)[None, :]).astype(jnp.int32)
    rank_in = jnp.sum((jnp.cumsum(onehot, axis=0) - onehot) * onehot, axis=1)
    slot_of = jnp.where(target < groups, target * capacity + rank_in, slot_count)
    dispatch = (slot_of[None, :] == jnp.arange(slot_count, dtype=jnp.int32)[:, None]).astype(
        jnp.bfloat16
    )
    outbound = jnp.dot(dispatch, tokens, preferred_element_type=jnp.float32).astype(jnp.bfloat16)
    gate_mat = gate_weight[0]
    up_mat = up_weight[0]
    down_mat = down_weight[0]
    copies = jnp.broadcast_to(
        outbound.reshape(groups, 1, capacity, model_width),
        (groups, inner_size, capacity, model_width),
    )
    copies = copies.reshape(groups * inner_size, capacity, model_width)
    received = lax.all_to_all(copies, ("group", "inner"), split_axis=0, concat_axis=0, tiled=True)
    partial_value = expert_part(received.reshape(-1, model_width), gate_mat, up_mat, down_mat)
    partial_value = partial_value.astype(jnp.bfloat16).reshape(received.shape)
    returned = lax.all_to_all(
        partial_value, ("group", "inner"), split_axis=0, concat_axis=0, tiled=True
    )
    summed = jnp.sum(
        returned.reshape(groups, inner_size, capacity, model_width).astype(jnp.float32), axis=1
    )
    back_rows = summed.astype(jnp.bfloat16).reshape(slot_count, model_width)
    expert_out = lax.dot_general(
        dispatch, back_rows, (((0,), (0,)), ((), ())), preferred_element_type=jnp.float32
    )
    return (gate_scale[:, None] * expert_out).astype(jnp.bfloat16)


def solution(mesh):
    in_specs = (
        P(("group", "inner"), None),
        P(("group", "inner")),
        P(("group", "inner")),
        P("group", None, "inner"),
        P("group", None, "inner"),
        P("group", "inner", None),
    )
    out_specs = P(("group", "inner"), None)
    return jax.shard_map(body, mesh=mesh, in_specs=in_specs, out_specs=out_specs, check_vma=False)
```

profile of v0, /device:TPU:0, one launch (start us, length us, event | category | flops | bytes accessed | tf_op | source)
XLA Modules:
  0.0 796.5 jit_solution(6565377100137666943)
XLA Ops:
  0.0 0.0 copy-start
  0.0 0.9 fusion.18
  0.9 0.2 reduce_window_sum.11
  1.1 0.8 select_reduce_fusion
  1.9 0.7 compare_select_fusion
  2.6 0.0 copy-done
  2.6 2.1 convolution_convert_fusion.1
  4.7 4.5 broadcast_in_dim.9
  9.2 11.0 %broadcast_in_dim.18 = bf16[16,8,10,7168]{3,2,1,0:T(8,128)(2,1)} broadcast(bf16[16,10,7168]{2,1,0:T(8,128)(2,1)} %broadcast_in_dim.9), dimensions={0,2,3} | broadcast | bytes 20643840 | tf_op jit(solution)/shard_map/broadcast_in_dim | solution.py:31
  20.2 333.8 %all_to_all.10 = bf16[128,10,7168]{2,1,0:T(8,128)(2,1)} all-to-all(bf16[128,10,7168]{2,1,0:T(8,128)(2,1)} %bitcast.22), channel_id=1, replica_groups=mesh['group'=16,'inner'=8] {'group','inner'}, dimensions={0} | all-to-all | bytes 36700160 | tf_op jit(solution)/shard_map/all_to_all | solution.py:36
  354.0 28.3 %reshape.21 = bf16[1280,7168]{1,0:T(8,128)(2,1)} reshape(bf16[128,10,7168]{2,1,0:T(8,128)(2,1)} %all_to_all.10) | data formatting | bytes 36700160 | tf_op jit(solution)/shard_map/reshape | solution.py:37
  382.3 9.8 %fusion.4 = f32[1280,256]{1,0:T(8,128)S(1)} fusion(bf16[1280,7168]{1,0:T(8,128)(2,1)} %reshape.21, bf16[1,7168,256]{2,1,0:T(8,128)(2,1)} %param.9), kind=kOutput, calls=%fused_computation.8 | convolution fusion | flops 4697620480 | bytes 23330816 | tf_op jit(solution)/shard_map/dot_general | solution.py:8
  392.1 27.2 %convolution_convert_fusion = bf16[1280,7168]{1,0:T(8,128)(2,1)} fusion(bf16[1,256,7168]{2,1,0:T(8,128)(2,1)} %param.11, bf16[1280,7168]{1,0:T(8,128)(2,1)} %reshape.21, bf16[1,7168,256]{2,1,0:T(8,128)(2,1)} %param.10, f32[1280,256]{1,0:T(8,128)S(1)} %fusion.4), kind=kOutput, calls=%fused_computation.1 | convolution fusion | flops 9406382080 | bytes 45350912 | tf_op jit(solution)/shard_map/dot_general | solution.py:11
  419.4 27.7 %reshape.22 = bf16[128,10,7168]{2,1,0:T(8,128)(2,1)} reshape(bf16[1280,7168]{1,0:T(8,128)(2,1)} %convolution_convert_fusion) | data formatting | bytes 36700160 | tf_op jit(solution)/shard_map/reshape | solution.py:38
  447.1 328.4 %all_to_all.11 = bf16[128,10,7168]{2,1,0:T(8,128)(2,1)} all-to-all(bf16[128,10,7168]{2,1,0:T(8,128)(2,1)} %reshape.22), channel_id=1, replica_groups=mesh['group'=16,'inner'=8] {'group','inner'}, dimensions={0} | all-to-all | bytes 36700160 | tf_op jit(solution)/shard_map/all_to_all | solution.py:39
  775.5 0.0 copy-start.1
  775.5 12.9 %bitcast_reduce_fusion = bf16[16,10,7168]{2,1,0:T(8,128)(2,1)} fusion(bf16[128,10,7168]{2,1,0:T(8,128)(2,1)} %all_to_all.11), kind=kLoop, calls=%fused_computation | loop fusion | flops 8028160 | bytes 20643840 | tf_op jit(solution)/shard_map/reduce_sum | solution.py:42
  788.4 0.0 copy-start.2
  788.4 4.5 reshape.24
  792.9 0.0 copy-done.2
  792.9 3.6 fusion
  796.5 0.0 copy-done.1
Async XLA Ops:
  0.0 2.6 copy-start
  775.5 21.0 %copy-start.1 = (bf16[128,7168]{1,0:T(8,128)(2,1)S(1)}, bf16[128,7168]{1,0:T(8,128)(2,1)}, u32[]{:S(2)}) copy-start(bf16[128,7168]{1,0:T(8,128)(2,1)} %param.6) | copy-start | bytes 5505028
  788.4 4.5 copy-start.2
where the time goes:
time: 799 us; the launch traced here: 796 us
  blocking collectives  662 us (83%)
  local copies, waits for them, and re-layouts  76.1 us (10%)
  matrix products  42.7 us (5%)
  other arithmetic  15.4 us (2%)
    all_to_all x1, blocking collectives, body(): lax.all_to_all(copies, ('group', 'inner'), split_axis=0, concat_axis=0, t...  334 us
    all_to_all x1, blocking collectives, body(): lax.all_to_all(partial_value, ('group', 'inner'), split_axis=0, concat_ax...  328 us
    reshape x1, local copies, waits for them, and re-layouts, body(): received.reshape(-1, model_width)  28.3 us
    reshape x1, local copies, waits for them, and re-layouts, body(): partial_value = partial_value.astype(jnp.bfloat16).reshape(received.shape)  27.7 us
    dot_general x1, matrix products, expert_part(): return jnp.dot(hidden, down_mat, preferred_element_type=jnp.float32)  27.2 us

commit v1 on v0

--- a/solution.py
+++ b/solution.py
@@ -25,24 +25,18 @@
         jnp.bfloat16
     )
     outbound = jnp.dot(dispatch, tokens, preferred_element_type=jnp.float32).astype(jnp.bfloat16)
-    gate_mat = gate_weight[0]
-    up_mat = up_weight[0]
-    down_mat = down_weight[0]
-    copies = jnp.broadcast_to(
-        outbound.reshape(groups, 1, capacity, model_width),
-        (groups, inner_size, capacity, model_width),
+    outbound = outbound.reshape(groups, capacity, model_width)
+    received = lax.all_to_all(outbound, "group", 0, 0, tiled=True)
+    gathered = lax.all_gather(received, "inner", axis=0, tiled=False)
+    partial_value = expert_part(
+        gathered.reshape(-1, model_width), gate_weight[0], up_weight[0], down_weight[0]
     )
-    copies = copies.reshape(groups * inner_size, capacity, model_width)
-    received = lax.all_to_all(copies, ("group", "inner"), split_axis=0, concat_axis=0, tiled=True)
-    partial_value = expert_part(received.reshape(-1, model_width), gate_mat, up_mat, down_mat)
-    partial_value = partial_value.astype(jnp.bfloat16).reshape(received.shape)
-    returned = lax.all_to_all(
-        partial_value, ("group", "inner"), split_axis=0, concat_axis=0, tiled=True
+    partial_value = partial_value.astype(jnp.bfloat16).reshape(
+        inner_size, groups, capacity, model_width
     )
-    summed = jnp.sum(
-        returned.reshape(groups, inner_size, capacity, model_width).astype(jnp.float32), axis=1
-    )
-    back_rows = summed.astype(jnp.bfloat16).reshape(slot_count, model_width)
+    pieces = lax.all_to_all(partial_value, "inner", 0, 0, tiled=True)
+    summed = jnp.sum(pieces.astype(jnp.float32), axis=0).astype(jnp.bfloat16)
+    back_rows = lax.all_to_all(summed, "group", 0, 0, tiled=True).reshape(slot_count, model_width)
     expert_out = lax.dot_general(
         dispatch, back_rows, (((0,), (0,)), ((), ())), preferred_element_type=jnp.float32
     )

time: 799 us -> 584 us (0.73)
  blocking collectives: 662 us -> 313 us
  waiting for transfers between devices: 0 us -> 89.2 us
  local copies, waits for them, and re-layouts: 76.1 us -> 109 us
  between operations: 0.03 us -> 13.4 us
    all_to_all x2 -> x3, blocking collectives: 662 us -> 313 us  [the longest x1 208 us: body(): pieces = lax.all_to_all(partial_value, 'inner', 0, 0, tiled=True)]
    all_gather x0 -> x1, waiting for transfers between devices: none -> 89.1 us  [body(): gathered = lax.all_gather(received, 'inner', axis=0, tiled=False)]
    reshape x3 -> x5, local copies, waits for them, and re-layouts: 60.6 us -> 82.1 us  [the longest x2 44.8 us: body(): partial_value.astype(jnp.bfloat16)]
    all_gather x0 -> x1, local copies, waits for them, and re-layouts: none -> 21.5 us  [body(): gathered = lax.all_gather(received, 'inner', axis=0, tiled=False)]
    broadcast_in_dim x2 -> x0, local copies, waits for them, and re-layouts: 15.5 us -> none  [body(): jnp.broadcast_to(outbound.reshape(groups, 1, capacity, model_width), (gro...]
  transfers between devices with their start and end apart: 0 -> 1, of which waited for: 0 -> 1; matrix products, arithmetic and copies ran while one was open for 0% -> 0% of each run, Pallas kernels for 0% -> 0%
where the time goes in v1:
time: 584 us; the launch traced here: 582 us
  blocking collectives  313 us (54%)
  local copies, waits for them, and re-layouts  109 us (19%)
  waiting for transfers between devices  89.2 us (15%)
  matrix products  42.7 us (7%)
  other arithmetic  13.6 us (2%)
  between operations  13.4 us (2%)
    all_to_all x1, blocking collectives, body(): pieces = lax.all_to_all(partial_value, 'inner', 0, 0, tiled=True)  208 us
    all_gather x1, waiting for transfers between devices, body(): gathered = lax.all_gather(received, 'inner', axis=0, tiled=False)  89.1 us
    all_to_all x1, blocking collectives, body(): received = lax.all_to_all(outbound, 'group', 0, 0, tiled=True)  53.4 us
    all_to_all x1, blocking collectives, body(): lax.all_to_all(summed, 'group', 0, 0, tiled=True)  51.9 us
    reshape x2, local copies, waits for them, and re-layouts, body(): partial_value.astype(jnp.bfloat16)  44.8 us
    reshape x1, local copies, waits for them, and re-layouts, body(): gathered.reshape(-1, model_width)  28.2 us
    dot_general x1, matrix products, expert_part(): return jnp.dot(hidden, down_mat, preferred_element_type=jnp.float32)  27.1 us
    all_gather x1, local copies, waits for them, and re-layouts, body(): gathered = lax.all_gather(received, 'inner', axis=0, tiled=False)  21.5 us
  transfers between devices with their start and end apart: 1, of which 1 were waited for; matrix products, arithmetic and copies ran while one was open for 0% of the time, Pallas kernels for 0%

profile of v1, /device:TPU:0, one launch (start us, length us, event | category | flops | bytes accessed | tf_op | source)
XLA Modules:
  0.0 581.5 jit_solution(12582657928746278648)
XLA Ops:
  6.5 0.0 copy-start
  6.5 0.0 all-gather.3.cloned.1.call-start
  6.5 0.9 fusion.18
  7.4 0.2 reduce_window_sum.11
  7.6 0.8 select_reduce_fusion
  8.4 0.7 compare_select_fusion
  9.1 0.0 copy-done
  9.1 2.1 convolution_convert_fusion.1
  11.2 4.5 reshape.15
  15.7 53.4 %all_to_all.15 = bf16[16,10,7168]{2,1,0:T(8,128)(2,1)S(1)} all-to-all(bf16[16,10,7168]{2,1,0:T(8,128)(2,1)} %reshape.15), channel_id=1, replica_groups=mesh['group'=16,'inner'=8] {'group'}, dimensions={0} | all-to-all | bytes 4587520 | tf_op jit(solution)/shard_map/all_to_all | solution.py:29
  69.1 2.6 copy.14
  71.7 0.0 all-gather.3.cloned.1.call-update
  71.7 89.1 %all-gather.3.cloned.1.call-done = bf16[128,10,7168]{2,0,1:T(8,128)(2,1)} async-done(((bf16[16,10,7168]{2,0,1:T(8,128)(2,1)}), bf16[128,10,7168]{2,0,1:T(8,128)(2,1)}) %all-gather.3.cloned.1.call-update) | async-done | bytes 18350096 | tf_op jit(solution)/shard_map/all_gather | solution.py:30
  160.9 21.5 %copy.15 = bf16[128,10,7168]{2,1,0:T(8,128)(2,1)} copy(bf16[128,10,7168]{2,0,1:T(8,128)(2,1)} %all-gather.3.cloned.1.call-done) | data formatting | bytes 36700160 | tf_op jit(solution)/shard_map/all_gather | solution.py:30
  182.4 28.2 %reshape.16 = bf16[1280,7168]{1,0:T(8,128)(2,1)} reshape(bf16[128,10,7168]{2,1,0:T(8,128)(2,1)} %copy.15) | data formatting | bytes 36700160 | tf_op jit(solution)/shard_map/reshape | solution.py:32
  210.6 9.8 %fusion.4 = f32[1280,256]{1,0:T(8,128)S(1)} fusion(bf16[1280,7168]{1,0:T(8,128)(2,1)} %reshape.16, bf16[1,7168,256]{2,1,0:T(8,128)(2,1)} %param.9), kind=kOutput, calls=%fused_computation.7 | convolution fusion | flops 4697620480 | bytes 23330816 | tf_op jit(solution)/shard_map/dot_general | solution.py:8
  220.4 27.1 %convolution_convert_fusion = bf16[1280,7168]{1,0:T(8,128)(2,1)} fusion(bf16[1,256,7168]{2,1,0:T(8,128)(2,1)} %param.11, bf16[1280,7168]{1,0:T(8,128)(2,1)} %reshape.16, bf16[1,7168,256]{2,1,0:T(8,128)(2,1)} %param.10, f32[1280,256]{1,0:T(8,128)S(1)} %fusion.4), kind=kOutput, calls=%fused_computation | convolution fusion | flops 9406382080 | bytes 45350912 | tf_op jit(solution)/shard_map/dot_general | solution.py:11
  247.6 27.7 %reshape.17 = bf16[8,16,10,7168]{3,2,1,0:T(8,128)(2,1)} reshape(bf16[1280,7168]{1,0:T(8,128)(2,1)} %convolution_convert_fusion) | data formatting | bytes 36700160 | tf_op jit(solution)/shard_map/reshape | solution.py:34
  275.2 17.2 %copy.16 = bf16[8,16,10,7168]{3,1,2,0:T(8,128)(2,1)S(1)} copy(bf16[8,16,10,7168]{3,2,1,0:T(8,128)(2,1)} %reshape.17) | data formatting | bytes 36700160 | tf_op jit(solution)/shard_map/reshape | solution.py:34
  292.4 208.1 %all_to_all.16 = bf16[8,16,10,7168]{3,1,2,0:T(8,128)(2,1)} all-to-all(bf16[8,16,10,7168]{3,1,2,0:T(8,128)(2,1)S(1)} %copy.16), channel_id=1, replica_groups=mesh['group'=16,'inner'=8] {'inner'}, dimensions={0} | all-to-all | bytes 36700160 | tf_op jit(solution)/shard_map/all_to_all | solution.py:37
  500.6 11.1 %reduce_sum.22 = bf16[16,10,7168]{2,0,1:T(8,128)(2,1)} reduce(bf16[8,16,10,7168]{3,1,2,0:T(8,128)(2,1)} %all_to_all.16, bf16[]{:T(256)} %constant.17.clone.1), dimensions={0}, to_apply=%region_2.3 | reduce | flops 8028160 | bytes 20643842 | tf_op jit(solution)/shard_map/reduce_sum | solution.py:38
  511.6 3.0 copy.17
  514.7 0.0 copy-start.1
  514.7 51.9 %all_to_all.17 = bf16[16,10,7168]{2,1,0:T(8,128)(2,1)} all-to-all(bf16[16,10,7168]{2,1,0:T(8,128)(2,1)S(1)} %copy.17), channel_id=1, replica_groups=mesh['group'=16,'inner'=8] {'group'}, dimensions={0} | all-to-all | bytes 4587520 | tf_op jit(solution)/shard_map/all_to_all | solution.py:39
  566.6 0.0 copy-start.2
  566.6 4.5 reshape.18
  571.1 0.0 copy-done.2
  571.1 3.6 fusion
  574.7 0.0 copy-done.1
Async XLA Ops:
  6.5 2.6 copy-start
  6.5 154.3 %all-gather.3.cloned.1.call-start = ((), (), s32[]{:S(2)}) async-start(), calls=%async_computation.3 | async-start | bytes 20643840 | tf_op jit(solution)/shard_map/all_gather | solution.py:30
  514.7 60.0 %copy-start.1 = (bf16[128,7168]{1,0:T(8,128)(2,1)S(1)}, bf16[128,7168]{1,0:T(8,128)(2,1)}, u32[]{:S(2)}) copy-start(bf16[128,7168]{1,0:T(8,128)(2,1)} %param.6) | copy-start | bytes 5505028
  566.6 4.5 copy-start.2
Sparse Core Ops, SparseCore 0:
  71.9 88.9 all-gather.2

commit v2 on v1

--- a/solution.py
+++ b/solution.py
@@ -5,10 +5,10 @@
 
 
 def expert_part(rows_in, gate_mat, up_mat, down_mat):
-    gate_pre = jnp.dot(rows_in, gate_mat, preferred_element_type=jnp.float32)
-    up_pre = jnp.dot(rows_in, up_mat, preferred_element_type=jnp.float32)
+    gate_pre = jnp.einsum("abcd,df->abcf", rows_in, gate_mat, preferred_element_type=jnp.float32)
+    up_pre = jnp.einsum("abcd,df->abcf", rows_in, up_mat, preferred_element_type=jnp.float32)
     hidden = (jax.nn.silu(gate_pre) * up_pre).astype(jnp.bfloat16)
-    return jnp.dot(hidden, down_mat, preferred_element_type=jnp.float32)
+    return jnp.einsum("abcf,fd->abcd", hidden, down_mat, preferred_element_type=jnp.float32)
 
 
 def body(tokens, target, gate_scale, gate_weight, up_weight, down_weight):
@@ -28,17 +28,15 @@
     outbound = outbound.reshape(groups, capacity, model_width)
     received = lax.all_to_all(outbound, "group", 0, 0, tiled=True)
     gathered = lax.all_gather(received, "inner", axis=0, tiled=False)
-    partial_value = expert_part(
-        gathered.reshape(-1, model_width), gate_weight[0], up_weight[0], down_weight[0]
-    )
-    partial_value = partial_value.astype(jnp.bfloat16).reshape(
-        inner_size, groups, capacity, model_width
-    )
-    pieces = lax.all_to_all(partial_value, "inner", 0, 0, tiled=True)
-    summed = jnp.sum(pieces.astype(jnp.float32), axis=0).astype(jnp.bfloat16)
-    back_rows = lax.all_to_all(summed, "group", 0, 0, tiled=True).reshape(slot_count, model_width)
-    expert_out = lax.dot_general(
-        dispatch, back_rows, (((0,), (0,)), ((), ())), preferred_element_type=jnp.float32
+    partial_value = expert_part(gathered, gate_weight[0], up_weight[0], down_weight[0])
+    partial_value = partial_value.astype(jnp.bfloat16)
+    summed = lax.psum_scatter(partial_value, "inner", scatter_dimension=0, tiled=False)
+    back_rows = lax.all_to_all(summed, "group", 0, 0, tiled=True)
+    expert_out = jnp.einsum(
+        "gct,gcd->td",
+        dispatch.reshape(groups, capacity, tok_count),
+        back_rows,
+        preferred_element_type=jnp.float32,
     )
     return (gate_scale[:, None] * expert_out).astype(jnp.bfloat16)
 

time: 584 us -> 378 us (0.65)
  blocking collectives: 313 us -> 53.4 us
  waiting for transfers between devices: 89.2 us -> 243 us
  local copies, waits for them, and re-layouts: 109 us -> 12 us
  other arithmetic: 13.6 us -> 2.54 us
  starting transfers between devices: 0.01 us -> 7.2 us
    all_to_all x2 -> x0, blocking collectives: 260 us -> none  [the longest x1 208 us: body(): pieces = lax.all_to_all(partial_value, 'inner', 0, 0, tiled=True)]
    reduce_scatter x0 -> x1, waiting for transfers between devices: none -> 100 us  [body(): lax.psum_scatter(partial_value, 'inner', scatter_dimension=0, tiled=False)]
    reshape x4 -> x0, local copies, waits for them, and re-layouts: 77.6 us -> none  [the longest x2 44.8 us: body(): partial_value.astype(jnp.bfloat16)]
    all_to_all x0 -> x1, waiting for transfers between devices: none -> 53.8 us  [body(): back_rows = lax.all_to_all(summed, 'group', 0, 0, tiled=True)]
    all_gather x1 -> x0, local copies, waits for them, and re-layouts: 21.5 us -> none  [body(): gathered = lax.all_gather(received, 'inner', axis=0, tiled=False)]
    reduce_sum x1 -> x0, other arithmetic: 11.1 us -> none  [body(): summed = jnp.sum(pieces.astype(jnp.float32), axis=0).astype(jnp.bfloat16)]
    all_to_all x0 -> x1, starting transfers between devices: none -> 7.16 us  [body(): back_rows = lax.all_to_all(summed, 'group', 0, 0, tiled=True)]
  transfers between devices with their start and end apart: 1 -> 3, of which waited for: 1 -> 3; matrix products, arithmetic and copies ran while one was open for 0% -> 0% of each run, Pallas kernels for 0% -> 0%
where the time goes in v2:
time: 378 us; the launch traced here: 375 us
  waiting for transfers between devices  243 us (64%)
  blocking collectives  53.4 us (14%)
  matrix products  43.4 us (11%)
  between operations  13.4 us (4%)
  local copies, waits for them, and re-layouts  12 us (3%)
  starting transfers between devices  7.2 us (2%)
    reduce_scatter x1, waiting for transfers between devices, body(): lax.psum_scatter(partial_value, 'inner', scatter_dimension=0, tiled=False)  100 us
    all_gather x1, waiting for transfers between devices, body(): gathered = lax.all_gather(received, 'inner', axis=0, tiled=False)  89.1 us
    all_to_all x1, waiting for transfers between devices, body(): back_rows = lax.all_to_all(summed, 'group', 0, 0, tiled=True)  53.8 us
    all_to_all x1, blocking collectives, body(): received = lax.all_to_all(outbound, 'group', 0, 0, tiled=True)  53.4 us
    dot_general x1, matrix products, expert_part(): jnp.einsum('abcf,fd->abcd', hidden, down_mat, preferred_element_type=jnp....  26.4 us
    dot_general x1, matrix products, expert_part(): jnp.einsum('abcd,df->abcf', rows_in, gate_mat, preferred_element_type=jnp...  9.83 us
  transfers between devices with their start and end apart: 3, of which 3 were waited for; matrix products, arithmetic and copies ran while one was open for 0% of the time, Pallas kernels for 0%

profile of v2, /device:TPU:0, one launch (start us, length us, event | category | flops | bytes accessed | tf_op | source)
XLA Modules:
  0.0 374.9 jit_solution(16346120310350611314)
XLA Ops:
  6.5 0.0 copy-start
  6.5 0.0 all-gather.3.cloned.1.call-start
  6.5 0.9 fusion.31
  7.4 0.2 reduce_window_sum.11
  7.6 0.8 select_reduce_fusion
  8.4 0.7 compare_select_fusion
  9.1 0.0 copy-done
  9.1 2.2 convolution_convert_fusion.1
  11.2 4.5 %reshape.21 = bf16[16,10,7168]{2,1,0:T(8,128)(2,1)} reshape(bf16[160,7168]{1,0:T(8,128)(2,1)} %convolution_convert_fusion.1) | data formatting | bytes 4587520 | tf_op jit(solution)/shard_map/reshape | solution.py:28
  15.7 53.4 %all_to_all.10 = bf16[16,10,7168]{2,1,0:T(8,128)(2,1)S(1)} all-to-all(bf16[16,10,7168]{2,1,0:T(8,128)(2,1)} %reshape.21), channel_id=1, replica_groups=mesh['group'=16,'inner'=8] {'group'}, dimensions={0} | all-to-all | bytes 4587520 | tf_op jit(solution)/shard_map/all_to_all | solution.py:29
  69.1 2.7 copy.9
  71.7 0.0 all-gather.3.cloned.1.call-update
  71.7 0.0 reduce-scatter.2.cloned.1.call-start
  71.8 89.1 %all-gather.3.cloned.1.call-done = bf16[128,10,7168]{2,0,1:T(8,128)(2,1)} async-done(((bf16[16,10,7168]{2,0,1:T(8,128)(2,1)}), bf16[128,10,7168]{2,0,1:T(8,128)(2,1)}) %all-gather.3.cloned.1.call-update) | async-done | bytes 18350096 | tf_op jit(solution)/shard_map/all_gather | solution.py:30
  160.9 9.8 %fusion.2 = f32[8,16,10,256]{3,1,2,0:T(8,128)S(1)} fusion(bf16[8,16,10,7168]{3,1,0,2:T(8,128)(2,1)} %bitcast.37, bf16[1,7168,256]{2,1,0:T(8,128)(2,1)} %param.9), kind=kOutput, calls=%fused_computation.2 | convolution fusion | flops 4697620480 | bytes 23330816 | tf_op jit(solution)/shard_map/abcd,df->abcf/dot_general | solution.py:8
  170.7 26.4 %convolution_convert_fusion = bf16[8,16,10,7168]{3,1,2,0:T(8,128)(2,1)} fusion(bf16[1,256,7168]{2,1,0:T(8,128)(2,1)} %param.11, bf16[1,7168,256]{2,1,0:T(8,128)(2,1)} %param.10, bf16[8,16,10,7168]{3,1,0,2:T(8,128)(2,1)} %bitcast.38, f32[8,16,10,256]{3,1,2,0:T(8,128)S(1)} %fusion.2), kind=kOutput, calls=%fused_computation.4 | convolution fusion | flops 9406382080 | bytes 45350912 | tf_op jit(solution)/shard_map/abcf,fd->abcd/dot_general | solution.py:11
  197.1 0.0 reduce-scatter.2.cloned.1.call-update
  197.1 100.0 %reduce-scatter.2.cloned.1.call-done = bf16[1,16,10,7168]{3,1,2,0:T(8,128)(2,1)} async-done(((bf16[8,16,10,7168]{3,1,2,0:T(8,128)(2,1)}), bf16[1,16,10,7168]{3,1,2,0:T(8,128)(2,1)}) %reduce-scatter.2.cloned.1.call-update) | async-done | bytes 2293776 | tf_op jit(solution)/shard_map/reduce_scatter | solution.py:33
  297.2 4.8 %copy.12 = bf16[16,10,7168]{2,1,0:T(8,128)(2,1)} copy(bf16[16,10,7168]{2,0,1:T(8,128)(2,1)} %bitcast.36) | data formatting | bytes 4587520 | tf_op jit(solution)/shard_map/reduce_scatter | solution.py:33
  302.0 0.0 copy-start.2
  302.0 7.2 %all-to-all-start.1 = ((bf16[16,10,7168]{2,1,0:T(8,128)(2,1)}), bf16[16,10,7168]{2,1,0:T(8,128)(2,1)}, u32[]{:S(2)}, u32[]{:S(2)}) async-start(bf16[16,10,7168]{2,1,0:T(8,128)(2,1)} %copy.12), calls=%async_computation.2 | async-start | bytes 7340032 | tf_op jit(solution)/shard_map/all_to_all | solution.py:34
  309.2 0.0 copy-start.1
  309.2 53.8 %all-to-all-done.1 = bf16[16,10,7168]{2,1,0:T(8,128)(2,1)} async-done(((bf16[16,10,7168]{2,1,0:T(8,128)(2,1)}), bf16[16,10,7168]{2,1,0:T(8,128)(2,1)}, u32[]{:S(2)}, u32[]{:S(2)}) %all-to-all-start.1) | async-done | bytes 2293792 | tf_op jit(solution)/shard_map/all_to_all | solution.py:34
  363.0 0.0 copy-done.2
  363.0 5.0 %fusion.5 = bf16[128,7168]{1,0:T(8,128)(2,1)} fusion(bf16[16,10,7168]{2,1,0:T(8,128)(2,1)} %all-to-all-done.1, f32[128]{0:T(128)S(1)} %copy-done.2, s32[16,10]{0,1:T(8,128)S(1)} %multiply_add_fusion, s32[128]{0:T(128)S(1)} %compare_select_fusion), kind=kOutput, calls=%fused_computation.8 | convolution fusion | flops 295456768 | bytes 4130432 | tf_op jit(solution)/shard_map/gct,gcd->td/dot_general | solution.py:35
  368.1 0.0 copy-done.1
  (1 shorter events, 0.0 us)
Async XLA Ops:
  6.5 2.6 copy-start
  6.5 154.3 %all-gather.3.cloned.1.call-start = ((), (), s32[]{:S(2)}) async-start(), calls=%async_computation.4 | async-start | bytes 20643840 | tf_op jit(solution)/shard_map/all_gather | solution.py:30
  71.7 225.4 %reduce-scatter.2.cloned.1.call-start = ((), (), s32[]{:S(2)}) async-start(), calls=%async_computation.3 | async-start | bytes 20643840 | tf_op jit(solution)/shard_map/reduce_scatter | solution.py:33
  302.0 61.0 %copy-start.2 = (f32[128]{0:T(128)S(1)}, f32[128]{0:T(128)}, u32[]{:S(2)}) copy-start(f32[128]{0:T(128)} %param.8) | copy-start | bytes 1540
  302.0 61.0 %all-to-all-start.1 = ((bf16[16,10,7168]{2,1,0:T(8,128)(2,1)}), bf16[16,10,7168]{2,1,0:T(8,128)(2,1)}, u32[]{:S(2)}, u32[]{:S(2)}) async-start(bf16[16,10,7168]{2,1,0:T(8,128)(2,1)} %copy.12), calls=%async_computation.2 | async-start | bytes 7340032 | tf_op jit(solution)/shard_map/all_to_all | solution.py:34
  309.2 58.9 %copy-start.1 = (bf16[128,7168]{1,0:T(8,128)(2,1)S(1)}, bf16[128,7168]{1,0:T(8,128)(2,1)}, u32[]{:S(2)}) copy-start(bf16[128,7168]{1,0:T(8,128)(2,1)} %param.6) | copy-start | bytes 5505028
Sparse Core Ops, SparseCore 0:
  71.9 88.9 all-gather.2
  197.3 99.8 reduce-scatter.1

commit v3 on v2

--- a/solution.py
+++ b/solution.py
@@ -1,14 +1,73 @@
+import functools
+
 import jax
 import jax.numpy as jnp
 from jax import lax
+from jax.experimental import pallas as pl
+from jax.experimental.pallas import tpu as pltpu
 from jax.sharding import PartitionSpec as P
+
+MESH = pl.DeviceIdType.MESH
+
+
+def exchange_kernel(groups, x_ref, y_ref, local_sem, send_sem, recv_sem):
+    me = lax.axis_index("group")
+    inner = lax.axis_index("inner")
+    barrier = pltpu.get_barrier_semaphore()
+    for k in range(1, groups):
+        peer = lax.rem(me + k, groups)
+        pl.semaphore_signal(barrier, inc=1, device_id=(peer, inner), device_id_type=MESH)
+    pl.semaphore_wait(barrier, groups - 1)
+    local = pltpu.make_async_copy(x_ref.at[me], y_ref.at[me], local_sem)
+    local.start()
+    sends = []
+    for k in range(1, groups):
+        peer = lax.rem(me + k, groups)
+        copy = pltpu.make_async_remote_copy(
+            src_ref=x_ref.at[peer],
+            dst_ref=y_ref.at[me],
+            send_sem=send_sem.at[peer],
+            recv_sem=recv_sem.at[me],
+            device_id=(peer, inner),
+            device_id_type=MESH,
+        )
+        copy.start()
+        sends.append(copy)
+    for k in range(1, groups):
+        source = lax.rem(me + groups - k, groups)
+        sends[k - 1].wait_send()
+        pltpu.make_async_remote_copy(
+            src_ref=x_ref.at[source],
+            dst_ref=y_ref.at[source],
+            send_sem=send_sem.at[source],
+            recv_sem=recv_sem.at[source],
+            device_id=(source, inner),
+            device_id_type=MESH,
+        ).wait_recv()
+    local.wait()
+
+
+def group_exchange(x, collective_id):
+    groups = x.shape[0]
+    return pl.pallas_call(
+        functools.partial(exchange_kernel, groups),
+        out_shape=jax.ShapeDtypeStruct(x.shape, x.dtype),
+        in_specs=[pl.BlockSpec(memory_space=pl.ANY)],
+        out_specs=pl.BlockSpec(memory_space=pl.ANY),
+        scratch_shapes=[
+            pltpu.SemaphoreType.DMA,
+            pltpu.SemaphoreType.DMA((groups,)),
+            pltpu.SemaphoreType.DMA((groups,)),
+        ],
+        compiler_params=pltpu.CompilerParams(collective_id=collective_id, has_side_effects=True),
+    )(x)
 
 
 def expert_part(rows_in, gate_mat, up_mat, down_mat):
-    gate_pre = jnp.einsum("abcd,df->abcf", rows_in, gate_mat, preferred_element_type=jnp.float32)
-    up_pre = jnp.einsum("abcd,df->abcf", rows_in, up_mat, preferred_element_type=jnp.float32)
+    gate_pre = jnp.dot(rows_in, gate_mat, preferred_element_type=jnp.float32)
+    up_pre = jnp.dot(rows_in, up_mat, preferred_element_type=jnp.float32)
     hidden = (jax.nn.silu(gate_pre) * up_pre).astype(jnp.bfloat16)
-    return jnp.einsum("abcf,fd->abcd", hidden, down_mat, preferred_element_type=jnp.float32)
+    return jnp.dot(hidden, down_mat, preferred_element_type=jnp.float32)
 
 
 def body(tokens, target, gate_scale, gate_weight, up_weight, down_weight):
@@ -26,12 +85,12 @@
     )
     outbound = jnp.dot(dispatch, tokens, preferred_element_type=jnp.float32).astype(jnp.bfloat16)
     outbound = outbound.reshape(groups, capacity, model_width)
-    received = lax.all_to_all(outbound, "group", 0, 0, tiled=True)
-    gathered = lax.all_gather(received, "inner", axis=0, tiled=False)
+    received = group_exchange(outbound, 0)
+    gathered = lax.all_gather(received.reshape(slot_count, model_width), "inner", axis=0, tiled=True)
     partial_value = expert_part(gathered, gate_weight[0], up_weight[0], down_weight[0])
     partial_value = partial_value.astype(jnp.bfloat16)
-    summed = lax.psum_scatter(partial_value, "inner", scatter_dimension=0, tiled=False)
-    back_rows = lax.all_to_all(summed, "group", 0, 0, tiled=True)
+    summed = lax.psum_scatter(partial_value, "inner", scatter_dimension=0, tiled=True)
+    back_rows = group_exchange(summed.reshape(groups, capacity, model_width), 1)
     expert_out = jnp.einsum(
         "gct,gcd->td",
         dispatch.reshape(groups, capacity, tok_count),

time: 378 us -> 392 us (1.037); the launches traced: 375 us -> 384 us
  Pallas kernels: 0 us -> 121 us
  blocking collectives: 53.4 us -> 0 us
  waiting for transfers between devices: 243 us -> 190 us
  starting transfers between devices: 7.2 us -> 0.04 us
    pallas_call x0 -> x2, Pallas kernels: none -> 121 us  [group_exchange(): pl.pallas_call(functools.partial(exchange_kernel, groups), out_shape=jax....]
    all_to_all x1 -> x0, waiting for transfers between devices: 53.8 us -> none  [body(): back_rows = lax.all_to_all(summed, 'group', 0, 0, tiled=True)]
    all_to_all x1 -> x0, blocking collectives: 53.4 us -> none  [body(): received = lax.all_to_all(outbound, 'group', 0, 0, tiled=True)]
    reshape x0 -> x2, local copies, waits for them, and re-layouts: none -> 8.99 us  [the longest x1 4.53 us: body(): received.reshape(slot_count, model_width)]
    all_to_all x1 -> x0, starting transfers between devices: 7.16 us -> none  [body(): back_rows = lax.all_to_all(summed, 'group', 0, 0, tiled=True)]
    reduce_scatter x1 -> x0, local copies, waits for them, and re-layouts: 4.84 us -> none  [body(): lax.psum_scatter(partial_value, 'inner', scatter_dimension=0, tiled=False)]
  transfers between devices with their start and end apart: 3 -> 2, of which waited for: 3 -> 2; matrix products, arithmetic and copies ran while one was open for 0% -> 0% of each run, Pallas kernels for 0% -> 0%
where the time goes in v3:
time: 392 us; the launch traced here: 384 us
  waiting for transfers between devices  190 us (48%)
  Pallas kernels  121 us (31%)
  matrix products  44.1 us (11%)
  local copies, waits for them, and re-layouts  13.5 us (3%)
  between operations  13.5 us (3%)
    pallas_call x2, Pallas kernels, group_exchange(): pl.pallas_call(functools.partial(exchange_kernel, groups), out_shape=jax....  121 us
    reduce_scatter x1, waiting for transfers between devices, body(): lax.psum_scatter(partial_value, 'inner', scatter_dimension=0, tiled=True)  100 us
    all_gather x1, waiting for transfers between devices, body(): lax.all_gather(received.reshape(slot_count, model_width), 'inner', axis=0...  89.6 us
    dot_general x1, matrix products, expert_part(): return jnp.dot(hidden, down_mat, preferred_element_type=jnp.float32)  27.1 us
    dot_general x1, matrix products, expert_part(): gate_pre = jnp.dot(rows_in, gate_mat, preferred_element_type=jnp.float32)  9.81 us
  transfers between devices with their start and end apart: 2, of which 2 were waited for; matrix products, arithmetic and copies ran while one was open for 0% of the time, Pallas kernels for 0%

profile of v3, /device:TPU:0, one launch (start us, length us, event | category | flops | bytes accessed | tf_op | source)
XLA Modules:
  0.0 384.5 jit_solution(8161279823710639719)
XLA Ops:
  6.5 0.0 copy-start
  6.5 0.0 all-gather.2.cloned.1.call-start
  6.5 0.9 fusion.21
  7.4 0.2 reduce_window_sum.11
  7.6 0.8 select_reduce_fusion
  8.4 0.7 compare_select_fusion
  9.1 0.0 copy-done
  9.1 2.1 convolution_convert_fusion.1
  11.2 4.5 %reshape.27.x_ref = bf16[16,10,7168]{2,1,0:T(8,128)(2,1)} reshape(bf16[160,7168]{1,0:T(8,128)(2,1)} %convolution_convert_fusion.1) | data formatting | bytes 4587520 | tf_op jit(solution)/shard_map/reshape | solution.py:87
  15.7 63.2 %shard_map.64 = bf16[16,10,7168]{2,1,0:T(8,128)(2,1)} custom-call(bf16[16,10,7168]{2,1,0:T(8,128)(2,1)} %reshape.27.x_ref), custom_call_target="tpu_custom_call" | custom-call | tf_op jit(solution)/shard_map/pallas_call | solution.py:52
  78.9 4.5 %reshape.28 = bf16[160,7168]{1,0:T(8,128)(2,1)} reshape(bf16[16,10,7168]{2,1,0:T(8,128)(2,1)} %shard_map.64) | data formatting | bytes 4587520 | tf_op jit(solution)/shard_map/reshape | solution.py:89
  83.5 0.0 all-gather.2.cloned.1.call-update
  83.5 0.0 reduce-scatter.2.cloned.1.call-start
  83.5 89.6 %all-gather.2.cloned.1.call-done = bf16[1280,7168]{1,0:T(8,128)(2,1)} async-done(((bf16[160,7168]{1,0:T(8,128)(2,1)}), bf16[1280,7168]{1,0:T(8,128)(2,1)}) %all-gather.2.cloned.1.call-update) | async-done | bytes 18350096 | tf_op jit(solution)/shard_map/all_gather | solution.py:89
  173.2 9.8 %fusion.5 = f32[1280,256]{1,0:T(8,128)S(1)} fusion(bf16[1280,7168]{1,0:T(8,128)(2,1)} %all-gather.2.cloned.1.call-done, bf16[1,7168,256]{2,1,0:T(8,128)(2,1)} %param.9), kind=kOutput, calls=%fused_computation.8 | convolution fusion | flops 4697620480 | bytes 23330816 | tf_op jit(solution)/shard_map/dot_general | solution.py:67
  183.0 27.1 %convolution_convert_fusion = bf16[1280,7168]{1,0:T(8,128)(2,1)} fusion(bf16[1,256,7168]{2,1,0:T(8,128)(2,1)} %param.11, bf16[1280,7168]{1,0:T(8,128)(2,1)} %all-gather.2.cloned.1.call-done, bf16[1,7168,256]{2,1,0:T(8,128)(2,1)} %param.10, f32[1280,256]{1,0:T(8,128)S(1)} %fusion.5), kind=kOutput, calls=%fused_computation | convolution fusion | flops 9406382080 | bytes 45350912 | tf_op jit(solution)/shard_map/dot_general | solution.py:70
  210.1 0.0 reduce-scatter.2.cloned.1.call-update
  210.1 100.0 %reduce-scatter.2.cloned.1.call-done = bf16[160,7168]{1,0:T(8,128)(2,1)} async-done(((bf16[1280,7168]{1,0:T(8,128)(2,1)}), bf16[160,7168]{1,0:T(8,128)(2,1)}) %reduce-scatter.2.cloned.1.call-update) | async-done | bytes 2293776 | tf_op jit(solution)/shard_map/reduce_scatter | solution.py:92
  310.1 4.5 %reshape.29.x_ref = bf16[16,10,7168]{2,1,0:T(8,128)(2,1)} reshape(bf16[160,7168]{1,0:T(8,128)(2,1)} %reduce-scatter.2.cloned.1.call-done) | data formatting | bytes 4587520 | tf_op jit(solution)/shard_map/reshape | solution.py:93
  314.6 0.0 copy-start.2
  314.6 0.0 copy-start.1
  314.6 58.0 %shard_map.65 = bf16[16,10,7168]{2,1,0:T(8,128)(2,1)} custom-call(bf16[16,10,7168]{2,1,0:T(8,128)(2,1)} %reshape.29.x_ref), custom_call_target="tpu_custom_call" | custom-call | tf_op jit(solution)/shard_map/pallas_call | solution.py:52
  372.6 0.0 copy-done.2
  372.6 5.0 %fusion.1 = bf16[128,7168]{1,0:T(8,128)(2,1)} fusion(bf16[16,10,7168]{2,1,0:T(8,128)(2,1)} %shard_map.65, f32[128]{0:T(128)S(1)} %copy-done.2, s32[16,10]{0,1:T(8,128)S(1)} %multiply_add_fusion, s32[128]{0:T(128)S(1)} %compare_select_fusion), kind=kOutput, calls=%fused_computation.4 | convolution fusion | flops 295456768 | bytes 4130432 | tf_op jit(solution)/shard_map/gct,gcd->td/dot_general | solution.py:94
  377.6 0.0 copy-done.1
  (1 shorter events, 0.0 us)
Async XLA Ops:
  6.5 2.6 copy-start
  6.5 166.6 %all-gather.2.cloned.1.call-start = ((), (), s32[]{:S(2)}) async-start(), calls=%async_computation.1 | async-start | bytes 20643840 | tf_op jit(solution)/shard_map/all_gather | solution.py:89
  83.5 226.6 %reduce-scatter.2.cloned.1.call-start = ((), (), s32[]{:S(2)}) async-start(), calls=%async_computation.2 | async-start | bytes 20643840 | tf_op jit(solution)/shard_map/reduce_scatter | solution.py:92
  314.6 58.0 %copy-start.2 = (f32[128]{0:T(128)S(1)}, f32[128]{0:T(128)}, u32[]{:S(2)}) copy-start(f32[128]{0:T(128)} %param.8) | copy-start | bytes 1540
  314.6 63.1 %copy-start.1 = (bf16[128,7168]{1,0:T(8,128)(2,1)S(1)}, bf16[128,7168]{1,0:T(8,128)(2,1)}, u32[]{:S(2)}) copy-start(bf16[128,7168]{1,0:T(8,128)(2,1)} %param.6) | copy-start | bytes 5505028
Sparse Core Ops, SparseCore 0:
  83.6 89.5 all-gather.1
  210.2 99.8 reduce-scatter.1

commit v4 on v3

v4 whole, which is shorter than its diff:
```python
import functools

import jax
import jax.numpy as jnp
from jax import lax
from jax.experimental import pallas as pl
from jax.experimental.pallas import tpu as pltpu
from jax.sharding import PartitionSpec as P

MESH = pl.DeviceIdType.MESH


def chunk_orders(groups):
    pairs = [(k, groups - k) for k in range(1, (groups + 1) // 2)]
    first = [0] + ([groups // 2] if groups % 2 == 0 and groups > 1 else [])
    second = []
    for index, pair in enumerate(pairs):
        (first if index < len(pairs) // 2 else second).extend(pair)
    return [first, second] if second else [first]


def exchange_kernel(groups, offsets, src_base, sign, x_ref, y_ref, local_sem, send_sem, recv_sem):
    me = lax.axis_index("group")
    inner = lax.axis_index("inner")
    peers = sorted({k % groups for k in offsets} - {0})
    barrier = pltpu.get_barrier_semaphore()
    for k in peers:
        pl.semaphore_signal(
            barrier, inc=1, device_id=(lax.rem(me + k, groups), inner), device_id_type=MESH
        )
    if peers:
        pl.semaphore_wait(barrier, len(peers))
    local = None
    sends = []
    for i, k in enumerate(offsets):
        if k == 0:
            local = pltpu.make_async_copy(x_ref.at[src_base + i], y_ref.at[i], local_sem)
            local.start()
            continue
        dest = lax.rem(me + sign * k + groups, groups)
        copy = pltpu.make_async_remote_copy(
            src_ref=x_ref.at[src_base + i],
            dst_ref=y_ref.at[i],
            send_sem=send_sem.at[i],
            recv_sem=recv_sem.at[i],
            device_id=(dest, inner),
            device_id_type=MESH,
        )
        copy.start()
        sends.append(copy)
    for copy in sends:
        copy.wait_send()
    for i, k in enumerate(offsets):
        if k == 0:
            continue
        source = lax.rem(me - sign * k + groups, groups)
        pltpu.make_async_remote_copy(
            src_ref=x_ref.at[src_base + i],
            dst_ref=y_ref.at[i],
            send_sem=send_sem.at[i],
            recv_sem=recv_sem.at[i],
            device_id=(source, inner),
            device_id_type=MESH,
        ).wait_recv()
    if local is not None:
        local.wait()


def group_exchange(x, offsets, src_base, sign, collective_id):
    groups = lax.axis_size("group")
    count = len(offsets)
    return pl.pallas_call(
        functools.partial(exchange_kernel, groups, tuple(offsets), src_base, sign),
        out_shape=jax.ShapeDtypeStruct((count,) + x.shape[1:], x.dtype),
        in_specs=[pl.BlockSpec(memory_space=pl.ANY)],
        out_specs=pl.BlockSpec(memory_space=pl.ANY),
        scratch_shapes=[
            pltpu.SemaphoreType.DMA,
            pltpu.SemaphoreType.DMA((count,)),
            pltpu.SemaphoreType.DMA((count,)),
        ],
        compiler_params=pltpu.CompilerParams(collective_id=collective_id, has_side_effects=True),
    )(x)


def expert_part(rows_in, gate_mat, up_mat, down_mat):
    gate_pre = jnp.dot(rows_in, gate_mat, preferred_element_type=jnp.float32)
    up_pre = jnp.dot(rows_in, up_mat, preferred_element_type=jnp.float32)
    hidden = (jax.nn.silu(gate_pre) * up_pre).astype(jnp.bfloat16)
    return jnp.dot(hidden, down_mat, preferred_element_type=jnp.float32)


def body(tokens, target, gate_scale, gate_weight, up_weight, down_weight):
    groups = lax.axis_size("group")
    tok_count = tokens.shape[0]
    model_width = tokens.shape[1]
    capacity = tok_count * 5 // (4 * groups)
    slot_count = groups * capacity
    chunks = chunk_orders(groups)
    order = [k for chunk in chunks for k in chunk]
    position_of = [0] * groups
    for position, k in enumerate(order):
        position_of[k] = position
    me = lax.axis_index("group")
    onehot = (target[:, None] == jnp.arange(groups, dtype=jnp.int32)[None, :]).astype(jnp.int32)
    rank_in = jnp.sum((jnp.cumsum(onehot, axis=0) - onehot) * onehot, axis=1)
    relative = lax.rem(target - me + groups, groups)
    position = jnp.asarray(position_of, dtype=jnp.int32)[relative]
    slot_of = jnp.where(target < groups, position * capacity + rank_in, slot_count)
    dispatch = (slot_of[None, :] == jnp.arange(slot_count, dtype=jnp.int32)[:, None]).astype(
        jnp.bfloat16
    )
    outbound = jnp.dot(dispatch, tokens, preferred_element_type=jnp.float32).astype(jnp.bfloat16)
    outbound = outbound.reshape(groups, capacity, model_width)
    returned = []
    base = 0
    for index, chunk in enumerate(chunks):
        received = group_exchange(outbound, chunk, base, 1, 2 * index)
        base += len(chunk)
        rows = received.reshape(len(chunk) * capacity, model_width)
        gathered = lax.all_gather(rows, "inner", axis=0, tiled=True)
        partial_value = expert_part(gathered, gate_weight[0], up_weight[0], down_weight[0])
        summed = lax.psum_scatter(
            partial_value.astype(jnp.bfloat16), "inner", scatter_dimension=0, tiled=True
        )
        returned.append((summed.reshape(len(chunk), capacity, model_width), chunk, index))
    back = [group_exchange(z, chunk, 0, -1, 2 * index + 1) for z, chunk, index in returned]
    back_rows = jnp.concatenate(back, axis=0) if len(back) > 1 else back[0]
    expert_out = jnp.einsum(
        "gct,gcd->td",
        dispatch.reshape(groups, capacity, tok_count),
        back_rows,
        preferred_element_type=jnp.float32,
    )
    return (gate_scale[:, None] * expert_out).astype(jnp.bfloat16)


def solution(mesh):
    in_specs = (
        P(("group", "inner"), None),
        P(("group", "inner")),
        P(("group", "inner")),
        P("group", None, "inner"),
        P("group", None, "inner"),
        P("group", "inner", None),
    )
    out_specs = P(("group", "inner"), None)
    return jax.shard_map(body, mesh=mesh, in_specs=in_specs, out_specs=out_specs, check_vma=False)
```

time: 392 us -> 330 us (0.84); the launches traced: 384 us -> 328 us
  waiting for transfers between devices: 190 us -> 98.4 us
  Pallas kernels: 121 us -> 138 us
  matrix products: 44.1 us -> 59.1 us
    all_gather x1 -> x2, waiting for transfers between devices: 89.6 us -> 38.8 us  [body(): gathered = lax.all_gather(rows, 'inner', axis=0, tiled=True)]
    reduce_scatter x1 -> x2, waiting for transfers between devices: 100 us -> 59.5 us  [body(): lax.psum_scatter(partial_value.astype(jnp.bfloat16), 'inner', scatter_dim...]
    pallas_call x2 -> x4, Pallas kernels: 121 us -> 138 us  [group_exchange(): pl.pallas_call(functools.partial(exchange_kernel, groups, tuple(offsets),...]
    dot_general x1 -> x2, matrix products: 27.1 us -> 39.6 us  [expert_part(): return jnp.dot(hidden, down_mat, preferred_element_type=jnp.float32)]
    dot_general x1 -> x2, matrix products: 9.81 us -> 14.3 us  [expert_part(): gate_pre = jnp.dot(rows_in, gate_mat, preferred_element_type=jnp.float32)]
    reshape x2 -> x4, local copies, waits for them, and re-layouts: 8.99 us -> 10.1 us  [the longest x2 5.13 us: body(): rows = received.reshape(len(chunk) * capacity, model_width)]
  transfers between devices with their start and end apart: 2 -> 4, of which waited for: 2 -> 4; matrix products, arithmetic and copies ran while one was open for 0% -> 18% of each run, Pallas kernels for 0% -> 21%
where the time goes in v4:
time: 330 us; the launch traced here: 328 us
  Pallas kernels  138 us (42%)
  waiting for transfers between devices  98.4 us (30%)
  matrix products  59.1 us (18%)
  local copies, waits for them, and re-layouts  14.6 us (4%)
  between operations  13.2 us (4%)
  other arithmetic  5.22 us (2%)
    pallas_call x4, Pallas kernels, group_exchange(): pl.pallas_call(functools.partial(exchange_kernel, groups, tuple(offsets),...  138 us
    reduce_scatter x2, waiting for transfers between devices, body(): lax.psum_scatter(partial_value.astype(jnp.bfloat16), 'inner', scatter_dim...  59.5 us
    dot_general x2, matrix products, expert_part(): return jnp.dot(hidden, down_mat, preferred_element_type=jnp.float32)  39.6 us
    all_gather x2, waiting for transfers between devices, body(): gathered = lax.all_gather(rows, 'inner', axis=0, tiled=True)  38.8 us
    dot_general x2, matrix products, expert_part(): gate_pre = jnp.dot(rows_in, gate_mat, preferred_element_type=jnp.float32)  14.3 us
  transfers between devices with their start and end apart: 4, of which 4 were waited for; matrix products, arithmetic and copies ran while one was open for 18% of the time, Pallas kernels for 21%

profile of v4, /device:TPU:0, one launch (start us, length us, event | category | flops | bytes accessed | tf_op | source)
XLA Modules:
  0.0 328.4 jit_solution(6229340563988813142)
XLA Ops:
  6.5 0.9 fusion.42
  7.4 0.2 reduce_window_sum.11
  7.6 0.8 select_reduce_fusion
  8.4 0.7 compare_select_fusion.18
  9.1 2.1 convolution_convert_fusion.2
  11.3 4.5 %reshape.33.x_ref = bf16[16,10,7168]{2,1,0:T(8,128)(2,1)} reshape(bf16[160,7168]{1,0:T(8,128)(2,1)} %convolution_convert_fusion.2) | data formatting | bytes 4587520 | tf_op jit(solution)/shard_map/reshape | solution.py:114
  15.7 28.5 %shard_map.73 = bf16[8,10,7168]{2,1,0:T(8,128)(2,1)} custom-call(bf16[16,10,7168]{2,1,0:T(8,128)(2,1)} %reshape.33.x_ref), custom_call_target="tpu_custom_call" | custom-call | tf_op jit(solution)/shard_map/pallas_call | solution.py:72
  44.3 2.5 reshape.34
  46.8 0.0 all-gather.3.cloned.1.call-update
  46.8 0.0 all-gather.5.cloned.1.call-start
  46.9 40.2 %shard_map.75 = bf16[8,10,7168]{2,1,0:T(8,128)(2,1)} custom-call(bf16[16,10,7168]{2,1,0:T(8,128)(2,1)} %reshape.33.x_ref), custom_call_target="tpu_custom_call" | custom-call | tf_op jit(solution)/shard_map/pallas_call | solution.py:72
  87.0 2.6 reshape.36
  89.7 0.0 all-gather.5.cloned.1.call-update
  89.7 0.0 reduce-scatter.3.cloned.1.call-start
  89.7 11.1 %all-gather.3.cloned.1.call-done = bf16[640,7168]{1,0:T(8,128)(2,1)} async-done(((bf16[80,7168]{1,0:T(8,128)(2,1)}), bf16[640,7168]{1,0:T(8,128)(2,1)}) %all-gather.3.cloned.1.call-update) | async-done | bytes 9175056 | tf_op jit(solution)/shard_map/all_gather | solution.py:121
  100.8 7.2 %fusion.10 = f32[640,256]{1,0:T(8,128)S(1)} fusion(bf16[640,7168]{1,0:T(8,128)(2,1)} %all-gather.3.cloned.1.call-done, bf16[1,7168,256]{2,1,0:T(8,128)(2,1)} %param.10), kind=kOutput, calls=%fused_computation.15 | convolution fusion | flops 2348810240 | bytes 13500416 | tf_op jit(solution)/shard_map/dot_general | solution.py:87
  108.0 19.8 %convolution_convert_fusion.1 = bf16[640,7168]{1,0:T(8,128)(2,1)} fusion(bf16[1,256,7168]{2,1,0:T(8,128)(2,1)} %param.12, bf16[640,7168]{1,0:T(8,128)(2,1)} %all-gather.3.cloned.1.call-done, bf16[1,7168,256]{2,1,0:T(8,128)(2,1)} %param.11, f32[640,256]{1,0:T(8,128)S(1)} %fusion.10), kind=kOutput, calls=%fused_computation.1 | convolution fusion | flops 4703191040 | bytes 26345472 | tf_op jit(solution)/shard_map/dot_general | solution.py:90
  127.8 0.0 reduce-scatter.3.cloned.1.call-update
  127.9 0.2 reduce-scatter.5.cloned.1.call-start
  128.1 27.7 %all-gather.5.cloned.1.call-done = bf16[640,7168]{1,0:T(8,128)(2,1)} async-done(((bf16[80,7168]{1,0:T(8,128)(2,1)}), bf16[640,7168]{1,0:T(8,128)(2,1)}) %all-gather.5.cloned.1.call-update) | async-done | bytes 9175056 | tf_op jit(solution)/shard_map/all_gather | solution.py:121
  155.8 7.2 %fusion.8 = f32[640,256]{1,0:T(8,128)S(1)} fusion(bf16[640,7168]{1,0:T(8,128)(2,1)} %all-gather.5.cloned.1.call-done, bf16[1,7168,256]{2,1,0:T(8,128)(2,1)} %param.10), kind=kOutput, calls=%fused_computation.13 | convolution fusion | flops 2348810240 | bytes 13500416 | tf_op jit(solution)/shard_map/dot_general | solution.py:87
  162.9 19.8 %convolution_convert_fusion = bf16[640,7168]{1,0:T(8,128)(2,1)} fusion(bf16[1,256,7168]{2,1,0:T(8,128)(2,1)} %param.12, bf16[640,7168]{1,0:T(8,128)(2,1)} %all-gather.5.cloned.1.call-done, bf16[1,7168,256]{2,1,0:T(8,128)(2,1)} %param.11, f32[640,256]{1,0:T(8,128)S(1)} %fusion.8), kind=kOutput, calls=%fused_computation | convolution fusion | flops 4703191040 | bytes 26345472 | tf_op jit(solution)/shard_map/dot_general | solution.py:90
  182.7 0.0 reduce-scatter.5.cloned.1.call-update
  182.7 31.9 %reduce-scatter.3.cloned.1.call-done = bf16[80,7168]{1,0:T(8,128)(2,1)} async-done(((bf16[640,7168]{1,0:T(8,128)(2,1)}), bf16[80,7168]{1,0:T(8,128)(2,1)}) %reduce-scatter.3.cloned.1.call-update) | async-done | bytes 1146896 | tf_op jit(solution)/shard_map/reduce_scatter | solution.py:123
  214.6 2.5 reshape.35.x_ref
  217.1 27.9 %shard_map.74 = bf16[8,10,7168]{2,1,0:T(8,128)(2,1)} custom-call(bf16[8,10,7168]{2,1,0:T(8,128)(2,1)} %reshape.35.x_ref), custom_call_target="tpu_custom_call" | custom-call | tf_op jit(solution)/shard_map/pallas_call | solution.py:72
  245.0 27.7 %reduce-scatter.5.cloned.1.call-done = bf16[80,7168]{1,0:T(8,128)(2,1)} async-done(((bf16[640,7168]{1,0:T(8,128)(2,1)}), bf16[80,7168]{1,0:T(8,128)(2,1)}) %reduce-scatter.5.cloned.1.call-update) | async-done | bytes 1146896 | tf_op jit(solution)/shard_map/reduce_scatter | solution.py:123
  272.7 2.5 reshape.37.x_ref
  275.2 41.0 %shard_map.76 = bf16[8,10,7168]{2,1,0:T(8,128)(2,1)} custom-call(bf16[8,10,7168]{2,1,0:T(8,128)(2,1)} %reshape.37.x_ref), custom_call_target="tpu_custom_call" | custom-call | tf_op jit(solution)/shard_map/pallas_call | solution.py:72
  316.2 0.0 copy-start.2
  316.2 2.7 pad_maximum_fusion
  318.9 3.0 fusion.1
  (7 shorter events, 0.0 us)
Async XLA Ops:
  6.5 2.6 copy-start
  6.5 94.3 %all-gather.3.cloned.1.call-start = ((), (), s32[]{:S(2)}) async-start(), calls=%async_computation.2 | async-start | bytes 10321920 | tf_op jit(solution)/shard_map/all_gather | solution.py:121
  46.8 108.9 %all-gather.5.cloned.1.call-start = ((), (), s32[]{:S(2)}) async-start(), calls=%async_computation.4 | async-start | bytes 10321920 | tf_op jit(solution)/shard_map/all_gather | solution.py:121
  89.7 124.9 %reduce-scatter.3.cloned.1.call-start = ((), (), s32[]{:S(2)}) async-start(), calls=%async_computation.3 | async-start | bytes 10321920 | tf_op jit(solution)/shard_map/reduce_scatter | solution.py:123
  127.9 144.8 %reduce-scatter.5.cloned.1.call-start = ((), (), s32[]{:S(2)}) async-start(), calls=%async_computation.5 | async-start | bytes 10321920 | tf_op jit(solution)/shard_map/reduce_scatter | solution.py:123
  316.2 2.7 copy-start.2
  316.2 5.7 %copy-start.1 = (bf16[128,7168]{1,0:T(8,128)(2,1)S(1)}, bf16[128,7168]{1,0:T(8,128)(2,1)}, u32[]{:S(2)}) copy-start(bf16[128,7168]{1,0:T(8,128)(2,1)} %param.7) | copy-start | bytes 5505028
Sparse Core Ops, SparseCore 0:
  46.9 53.8 all-gather.2
  102.5 53.2 all-gather.4
  158.2 56.3 reduce-scatter.2
  216.9 55.7 reduce-scatter.4

commit v5 on v4

--- a/solution.py
+++ b/solution.py
@@ -10,34 +10,54 @@
 MESH = pl.DeviceIdType.MESH
 
 
+def torus_sides(groups):
+    side = 4 if groups % 4 == 0 and groups > 4 else groups
+    return groups // side, side
+
+
 def chunk_orders(groups):
-    pairs = [(k, groups - k) for k in range(1, (groups + 1) // 2)]
-    first = [0] + ([groups // 2] if groups % 2 == 0 and groups > 1 else [])
+    if groups == 16:
+        return [
+            [(0, 0), (0, 1), (0, 3), (2, 0)],
+            [(0, 2), (2, 2), (1, 3), (3, 1)],
+            [(1, 2), (3, 2), (2, 1), (2, 3)],
+            [(1, 0), (3, 0), (1, 1), (3, 3)],
+        ]
+    pairs = [((0, k), (0, groups - k)) for k in range(1, (groups + 1) // 2)]
+    first = [(0, 0)] + ([(0, groups // 2)] if groups % 2 == 0 and groups > 1 else [])
     second = []
     for index, pair in enumerate(pairs):
         (first if index < len(pairs) // 2 else second).extend(pair)
     return [first, second] if second else [first]
 
 
+def peer_of(me, offset, sign, groups):
+    rows, side = torus_sides(groups)
+    dz, dy = offset
+    z = lax.rem(me // side + sign * dz + rows, rows)
+    y = lax.rem(lax.rem(me, side) + sign * dy + side, side)
+    return z * side + y
+
+
 def exchange_kernel(groups, offsets, src_base, sign, x_ref, y_ref, local_sem, send_sem, recv_sem):
     me = lax.axis_index("group")
     inner = lax.axis_index("inner")
-    peers = sorted({k % groups for k in offsets} - {0})
+    peers = [k for k in offsets if k != (0, 0)]
     barrier = pltpu.get_barrier_semaphore()
     for k in peers:
         pl.semaphore_signal(
-            barrier, inc=1, device_id=(lax.rem(me + k, groups), inner), device_id_type=MESH
+            barrier, inc=1, device_id=(peer_of(me, k, 1, groups), inner), device_id_type=MESH
         )
     if peers:
         pl.semaphore_wait(barrier, len(peers))
     local = None
     sends = []
     for i, k in enumerate(offsets):
-        if k == 0:
+        if k == (0, 0):
             local = pltpu.make_async_copy(x_ref.at[src_base + i], y_ref.at[i], local_sem)
             local.start()
             continue
-        dest = lax.rem(me + sign * k + groups, groups)
+        dest = peer_of(me, k, sign, groups)
         copy = pltpu.make_async_remote_copy(
             src_ref=x_ref.at[src_base + i],
             dst_ref=y_ref.at[i],
@@ -51,9 +71,9 @@
     for copy in sends:
         copy.wait_send()
     for i, k in enumerate(offsets):
-        if k == 0:
+        if k == (0, 0):
             continue
-        source = lax.rem(me - sign * k + groups, groups)
+        source = peer_of(me, k, -sign, groups)
         pltpu.make_async_remote_copy(
             src_ref=x_ref.at[src_base + i],
             dst_ref=y_ref.at[i],
@@ -98,13 +118,16 @@
     slot_count = groups * capacity
     chunks = chunk_orders(groups)
     order = [k for chunk in chunks for k in chunk]
+    rows, side = torus_sides(groups)
     position_of = [0] * groups
-    for position, k in enumerate(order):
-        position_of[k] = position
+    for position, (dz, dy) in enumerate(order):
+        position_of[dz * side + dy] = position
     me = lax.axis_index("group")
     onehot = (target[:, None] == jnp.arange(groups, dtype=jnp.int32)[None, :]).astype(jnp.int32)
     rank_in = jnp.sum((jnp.cumsum(onehot, axis=0) - onehot) * onehot, axis=1)
-    relative = lax.rem(target - me + groups, groups)
+    relative_z = lax.rem(target // side - me // side + rows, rows)
+    relative_y = lax.rem(lax.rem(target, side) - lax.rem(me, side) + side, side)
+    relative = jnp.where(target < groups, relative_z * side + relative_y, 0)
     position = jnp.asarray(position_of, dtype=jnp.int32)[relative]
     slot_of = jnp.where(target < groups, position * capacity + rank_in, slot_count)
     dispatch = (slot_of[None, :] == jnp.arange(slot_count, dtype=jnp.int32)[:, None]).astype(

time: 330 us -> 373 us (1.13)
  waiting for transfers between devices: 98.4 us -> 140 us
  matrix products: 59.1 us -> 44.6 us
  local copies, waits for them, and re-layouts: 14.6 us -> 28.7 us
    reduce_scatter x2 -> x4, waiting for transfers between devices: 59.5 us -> 89.5 us  [body(): lax.psum_scatter(partial_value.astype(jnp.bfloat16), 'inner', scatter_dim...]
    dot_general x2 -> x4, matrix products: 39.6 us -> 14 us  [expert_part(): return jnp.dot(hidden, down_mat, preferred_element_type=jnp.float32)]
    all_gather x2 -> x4, waiting for transfers between devices: 38.8 us -> 50 us  [body(): gathered = lax.all_gather(rows, 'inner', axis=0, tiled=True)]
    unnamed x6 -> x32, local copies, waits for them, and re-layouts: 0.02 us -> 6.4 us
    dot_general x0 -> x4, matrix products: none -> 5.66 us  [expert_part(): up_pre = jnp.dot(rows_in, up_mat, preferred_element_type=jnp.float32)]
    dot_general x2 -> x4, matrix products: 14.3 us -> 19.8 us  [expert_part(): gate_pre = jnp.dot(rows_in, gate_mat, preferred_element_type=jnp.float32)]
    reshape x2 -> x4, local copies, waits for them, and re-layouts: 5.13 us -> 9 us  [body(): rows = received.reshape(len(chunk) * capacity, model_width)]
    reshape x2 -> x4, local copies, waits for them, and re-layouts: 5 us -> 8.79 us  [body(): summed.reshape(len(chunk), capacity, model_width)]
  transfers between devices with their start and end apart: 4 -> 8, of which waited for: 4 -> 7; matrix products, arithmetic and copies ran while one was open for 18% -> 14% of each run, Pallas kernels for 21% -> 28%
where the time goes in v5:
time: 373 us; the launch traced here: 372 us
  Pallas kernels  140 us (38%)
  waiting for transfers between devices  140 us (38%)
  matrix products  44.6 us (12%)
  local copies, waits for them, and re-layouts  28.7 us (8%)
  between operations  13.8 us (4%)
  other arithmetic  4.9 us (1%)
    pallas_call x8, Pallas kernels, group_exchange(): pl.pallas_call(functools.partial(exchange_kernel, groups, tuple(offsets),...  140 us
    reduce_scatter x4, waiting for transfers between devices, body(): lax.psum_scatter(partial_value.astype(jnp.bfloat16), 'inner', scatter_dim...  89.5 us
    all_gather x4, waiting for transfers between devices, body(): gathered = lax.all_gather(rows, 'inner', axis=0, tiled=True)  50 us
    dot_general x4, matrix products, expert_part(): gate_pre = jnp.dot(rows_in, gate_mat, preferred_element_type=jnp.float32)  19.8 us
    dot_general x4, matrix products, expert_part(): return jnp.dot(hidden, down_mat, preferred_element_type=jnp.float32)  14 us
    reshape x4, local copies, waits for them, and re-layouts, body(): rows = received.reshape(len(chunk) * capacity, model_width)  9 us
    reshape x4, local copies, waits for them, and re-layouts, body(): summed.reshape(len(chunk), capacity, model_width)  8.79 us
  transfers between devices with their start and end apart: 8, of which 7 were waited for; matrix products, arithmetic and copies ran while one was open for 14% of the time, Pallas kernels for 28%

profile of v5, /device:TPU:0, one launch (start us, length us, event | category | flops | bytes accessed | tf_op | source)
XLA Modules:
  0.0 372.4 jit_solution(12289221575148798428)
XLA Ops:
  11.3 4.5 %reshape.45.x_ref = bf16[16,10,7168]{2,1,0:T(8,128)(2,1)} reshape(bf16[160,7168]{1,0:T(8,128)(2,1)} %convolution_convert_fusion.4) | data formatting | bytes 4587520 | tf_op jit(solution)/shard_map/reshape | solution.py:137
  15.8 23.8 %shard_map.75 = bf16[4,10,7168]{2,1,0:T(8,128)(2,1)} custom-call(bf16[16,10,7168]{2,1,0:T(8,128)(2,1)} %reshape.45.x_ref), custom_call_target="tpu_custom_call" | custom-call | tf_op jit(solution)/shard_map/pallas_call | solution.py:92
  39.6 2.2 reshape.48
  41.9 11.0 %shard_map.73 = bf16[4,10,7168]{2,1,0:T(8,128)(2,1)} custom-call(bf16[16,10,7168]{2,1,0:T(8,128)(2,1)} %reshape.45.x_ref), custom_call_target="tpu_custom_call" | custom-call | tf_op jit(solution)/shard_map/pallas_call | solution.py:92
  52.9 2.3 reshape.46
  55.3 22.1 %shard_map.77 = bf16[4,10,7168]{2,1,0:T(8,128)(2,1)} custom-call(bf16[16,10,7168]{2,1,0:T(8,128)(2,1)} %reshape.45.x_ref), custom_call_target="tpu_custom_call" | custom-call | tf_op jit(solution)/shard_map/pallas_call | solution.py:92
  77.3 2.2 reshape.50
  79.6 15.4 %shard_map.79 = bf16[4,10,7168]{2,1,0:T(8,128)(2,1)} custom-call(bf16[16,10,7168]{2,1,0:T(8,128)(2,1)} %reshape.45.x_ref), custom_call_target="tpu_custom_call" | custom-call | tf_op jit(solution)/shard_map/pallas_call | solution.py:92
  95.0 2.3 reshape.52
  97.4 5.1 %fusion.18 = f32[320,256]{1,0:T(8,128)S(1)} fusion(bf16[320,7168]{1,0:T(8,128)(2,1)} %all-gather.7.cloned.1.call-done, bf16[1,7168,256]{2,1,0:T(8,128)(2,1)} %param.10), kind=kOutput, calls=%fused_computation.25 | convolution fusion | flops 1174405120 | bytes 8585216 | tf_op jit(solution)/shard_map/dot_general | solution.py:107
  105.6 3.5 convolution_convert_fusion.2
  109.2 2.3 all-gather.5.cloned.1.call-done
  111.5 4.9 %fusion.20 = f32[320,256]{1,0:T(8,128)S(1)} fusion(bf16[320,7168]{1,0:T(8,128)(2,1)} %all-gather.5.cloned.1.call-done, bf16[1,7168,256]{2,1,0:T(8,128)(2,1)} %param.10), kind=kOutput, calls=%fused_computation.27 | convolution fusion | flops 1174405120 | bytes 8585216 | tf_op jit(solution)/shard_map/dot_general | solution.py:107
  119.4 3.4 convolution_convert_fusion.3
  123.1 23.8 %all-gather.9.cloned.1.call-done = bf16[320,7168]{1,0:T(8,128)(2,1)} async-done(((bf16[40,7168]{1,0:T(8,128)(2,1)}), bf16[320,7168]{1,0:T(8,128)(2,1)}) %all-gather.9.cloned.1.call-update) | async-done | bytes 4587536 | tf_op jit(solution)/shard_map/all_gather | solution.py:144
  146.9 4.9 %fusion.16 = f32[320,256]{1,0:T(8,128)S(1)} fusion(bf16[320,7168]{1,0:T(8,128)(2,1)} %all-gather.9.cloned.1.call-done, bf16[1,7168,256]{2,1,0:T(8,128)(2,1)} %param.10), kind=kOutput, calls=%fused_computation.23 | convolution fusion | flops 1174405120 | bytes 8585216 | tf_op jit(solution)/shard_map/dot_general | solution.py:107
  154.8 3.5 convolution_convert_fusion.1
  158.4 23.8 %all-gather.11.cloned.1.call-done = bf16[320,7168]{1,0:T(8,128)(2,1)} async-done(((bf16[40,7168]{1,0:T(8,128)(2,1)}), bf16[320,7168]{1,0:T(8,128)(2,1)}) %all-gather.11.cloned.1.call-update) | async-done | bytes 4587536 | tf_op jit(solution)/shard_map/all_gather | solution.py:144
  182.2 4.9 %fusion.14 = f32[320,256]{1,0:T(8,128)S(1)} fusion(bf16[320,7168]{1,0:T(8,128)(2,1)} %all-gather.11.cloned.1.call-done, bf16[1,7168,256]{2,1,0:T(8,128)(2,1)} %param.10), kind=kOutput, calls=%fused_computation.21 | convolution fusion | flops 1174405120 | bytes 8585216 | tf_op jit(solution)/shard_map/dot_general | solution.py:107
  190.1 3.6 convolution_convert_fusion
  193.7 29.4 %reduce-scatter.7.cloned.1.call-done = bf16[40,7168]{1,0:T(8,128)(2,1)} async-done(((bf16[320,7168]{1,0:T(8,128)(2,1)}), bf16[40,7168]{1,0:T(8,128)(2,1)}) %reduce-scatter.7.cloned.1.call-update) | async-done | bytes 573456 | tf_op jit(solution)/shard_map/reduce_scatter | solution.py:146
  223.1 2.2 reshape.49.x_ref
  225.3 19.9 %shard_map.76 = bf16[4,10,7168]{2,1,0:T(8,128)(2,1)} custom-call(bf16[4,10,7168]{2,1,0:T(8,128)(2,1)} %reshape.49.x_ref), custom_call_target="tpu_custom_call" | custom-call | tf_op jit(solution)/shard_map/pallas_call | solution.py:92
  245.2 18.4 %reduce-scatter.5.cloned.1.call-done = bf16[40,7168]{1,0:T(8,128)(2,1)} async-done(((bf16[320,7168]{1,0:T(8,128)(2,1)}), bf16[40,7168]{1,0:T(8,128)(2,1)}) %reduce-scatter.5.cloned.1.call-update) | async-done | bytes 573456 | tf_op jit(solution)/shard_map/reduce_scatter | solution.py:146
  265.8 11.4 %shard_map.74 = bf16[4,10,7168]{2,1,0:T(8,128)(2,1)} custom-call(bf16[4,10,7168]{2,1,0:T(8,128)(2,1)} %reshape.47.x_ref), custom_call_target="tpu_custom_call" | custom-call | tf_op jit(solution)/shard_map/pallas_call | solution.py:92
  277.2 26.5 %reduce-scatter.9.cloned.1.call-done = bf16[40,7168]{1,0:T(8,128)(2,1)} async-done(((bf16[320,7168]{1,0:T(8,128)(2,1)}), bf16[40,7168]{1,0:T(8,128)(2,1)}) %reduce-scatter.9.cloned.1.call-update) | async-done | bytes 573456 | tf_op jit(solution)/shard_map/reduce_scatter | solution.py:146
  305.9 23.3 %shard_map.78 = bf16[4,10,7168]{2,1,0:T(8,128)(2,1)} custom-call(bf16[4,10,7168]{2,1,0:T(8,128)(2,1)} %reshape.51.x_ref), custom_call_target="tpu_custom_call" | custom-call | tf_op jit(solution)/shard_map/pallas_call | solution.py:92
  329.1 15.2 %reduce-scatter.11.cloned.1.call-done = bf16[40,7168]{1,0:T(8,128)(2,1)} async-done(((bf16[320,7168]{1,0:T(8,128)(2,1)}), bf16[40,7168]{1,0:T(8,128)(2,1)}) %reduce-scatter.11.cloned.1.call-update) | async-done | bytes 573456 | tf_op jit(solution)/shard_map/reduce_scatter | solution.py:146
  344.3 2.2 reshape.53.x_ref
  346.5 13.7 %shard_map.80 = bf16[4,10,7168]{2,1,0:T(8,128)(2,1)} custom-call(bf16[4,10,7168]{2,1,0:T(8,128)(2,1)} %reshape.53.x_ref), custom_call_target="tpu_custom_call" | custom-call | tf_op jit(solution)/shard_map/pallas_call | solution.py:92
  360.2 2.3 pad_maximum_fusion
  362.6 3.0 fusion.1
  (61 shorter events, 21.8 us)
Async XLA Ops:
  6.5 2.6 copy-start
  6.5 90.8 %all-gather.7.cloned.1.call-start = ((), (), s32[]{:S(2)}) async-start(), calls=%async_computation.6 | async-start | bytes 5160960 | tf_op jit(solution)/shard_map/all_gather | solution.py:144
  41.9 69.6 %all-gather.5.cloned.1.call-start = ((), (), s32[]{:S(2)}) async-start(), calls=%async_computation.4 | async-start | bytes 5160960 | tf_op jit(solution)/shard_map/all_gather | solution.py:144
  55.2 91.7 %all-gather.9.cloned.1.call-start = ((), (), s32[]{:S(2)}) async-start(), calls=%async_computation.8 | async-start | bytes 5160960 | tf_op jit(solution)/shard_map/all_gather | solution.py:144
  79.6 102.6 %all-gather.11.cloned.1.call-start = ((), (), s32[]{:S(2)}) async-start(), calls=%async_computation.10 | async-start | bytes 5160960 | tf_op jit(solution)/shard_map/all_gather | solution.py:144
  97.3 125.8 %reduce-scatter.7.cloned.1.call-start = ((), (), s32[]{:S(2)}) async-start(), calls=%async_computation.7 | async-start | bytes 5160960 | tf_op jit(solution)/shard_map/reduce_scatter | solution.py:146
  97.4 5.1 %copy-start.10 = (bf16[320,7168]{1,0:T(8,128)(2,1)S(1)}, bf16[320,7168]{1,0:T(8,128)(2,1)}, u32[]{:S(2)}) copy-start(bf16[320,7168]{1,0:T(8,128)(2,1)} %all-gather.7.cloned.1.call-done) | copy-start | bytes 13762564
  97.4 6.1 %copy-start.11 = (bf16[1,7168,256]{2,1,0:T(8,128)(2,1)S(1)}, bf16[1,7168,256]{2,1,0:T(8,128)(2,1)}, u32[]{:S(2)}) copy-start(bf16[1,7168,256]{2,1,0:T(8,128)(2,1)} %param.11) | copy-start | bytes 11010052
  103.5 2.1 copy-start.2
  109.2 154.4 %reduce-scatter.5.cloned.1.call-start = ((), (), s32[]{:S(2)}) async-start(), calls=%async_computation.5 | async-start | bytes 5160960 | tf_op jit(solution)/shard_map/reduce_scatter | solution.py:146
  111.5 4.9 %copy-start.9 = (bf16[320,7168]{1,0:T(8,128)(2,1)S(1)}, bf16[320,7168]{1,0:T(8,128)(2,1)}, u32[]{:S(2)}) copy-start(bf16[320,7168]{1,0:T(8,128)(2,1)} %all-gather.5.cloned.1.call-done) | copy-start | bytes 13762564
  111.5 5.9 %copy-start.12 = (bf16[1,7168,256]{2,1,0:T(8,128)(2,1)S(1)}, bf16[1,7168,256]{2,1,0:T(8,128)(2,1)}, u32[]{:S(2)}) copy-start(bf16[1,7168,256]{2,1,0:T(8,128)(2,1)} %param.11) | copy-start | bytes 11010052
  117.3 2.0 copy-start.3
  122.8 180.8 %reduce-scatter.9.cloned.1.call-start = ((), (), s32[]{:S(2)}) async-start(), calls=%async_computation.9 | async-start | bytes 5160960 | tf_op jit(solution)/shard_map/reduce_scatter | solution.py:146
  146.9 4.9 %copy-start.8 = (bf16[320,7168]{1,0:T(8,128)(2,1)S(1)}, bf16[320,7168]{1,0:T(8,128)(2,1)}, u32[]{:S(2)}) copy-start(bf16[320,7168]{1,0:T(8,128)(2,1)} %all-gather.9.cloned.1.call-done) | copy-start | bytes 13762564
  146.9 5.9 %copy-start.13 = (bf16[1,7168,256]{2,1,0:T(8,128)(2,1)S(1)}, bf16[1,7168,256]{2,1,0:T(8,128)(2,1)}, u32[]{:S(2)}) copy-start(bf16[1,7168,256]{2,1,0:T(8,128)(2,1)} %param.11) | copy-start | bytes 11010052
  152.8 2.0 copy-start.4
  158.3 186.0 %reduce-scatter.11.cloned.1.call-start = ((), (), s32[]{:S(2)}) async-start(), calls=%async_computation.11 | async-start | bytes 5160960 | tf_op jit(solution)/shard_map/reduce_scatter | solution.py:146
  182.2 4.9 %copy-start.7 = (bf16[320,7168]{1,0:T(8,128)(2,1)S(1)}, bf16[320,7168]{1,0:T(8,128)(2,1)}, u32[]{:S(2)}) copy-start(bf16[320,7168]{1,0:T(8,128)(2,1)} %all-gather.11.cloned.1.call-done) | copy-start | bytes 13762564
  182.2 5.9 %copy-start.14 = (bf16[1,7168,256]{2,1,0:T(8,128)(2,1)S(1)}, bf16[1,7168,256]{2,1,0:T(8,128)(2,1)}, u32[]{:S(2)}) copy-start(bf16[1,7168,256]{2,1,0:T(8,128)(2,1)} %param.11) | copy-start | bytes 11010052
  188.1 2.0 copy-start.5
  277.2 83.0 %copy-start.6 = (bf16[4,10,7168]{2,1,0:T(8,128)(2,1)S(1)}, bf16[4,10,7168]{2,1,0:T(8,128)(2,1)}, u32[]{:S(2)}) copy-start(bf16[4,10,7168]{2,1,0:T(8,128)(2,1)} %shard_map.76) | copy-start | bytes 1720324
  360.2 2.4 copy-start.15
  360.2 5.4 %copy-start.1 = (bf16[128,7168]{1,0:T(8,128)(2,1)S(1)}, bf16[128,7168]{1,0:T(8,128)(2,1)}, u32[]{:S(2)}) copy-start(bf16[128,7168]{1,0:T(8,128)(2,1)} %param.7) | copy-start | bytes 5505028
Sparse Core Ops, SparseCore 0:
  42.0 34.0 all-gather.6
  77.7 33.7 all-gather.4
  113.2 33.7 all-gather.8
  148.5 33.7 all-gather.10
  184.5 38.5 reduce-scatter.6
  225.5 38.0 reduce-scatter.4
  266.0 37.5 reduce-scatter.8
  306.2 38.0 reduce-scatter.10

commit v6 on v5

--- a/solution.py
+++ b/solution.py
@@ -18,10 +18,9 @@
 def chunk_orders(groups):
     if groups == 16:
         return [
-            [(0, 0), (0, 1), (0, 3), (2, 0)],
-            [(0, 2), (2, 2), (1, 3), (3, 1)],
-            [(1, 2), (3, 2), (2, 1), (2, 3)],
-            [(1, 0), (3, 0), (1, 1), (3, 3)],
+            [(0, 0), (0, 1), (0, 3), (0, 2)],
+            [(1, 1), (3, 3), (1, 3), (3, 1), (1, 2), (3, 2), (2, 1), (2, 3)],
+            [(1, 0), (3, 0), (2, 0), (2, 2)],
         ]
     pairs = [((0, k), (0, groups - k)) for k in range(1, (groups + 1) // 2)]
     first = [(0, 0)] + ([(0, groups // 2)] if groups % 2 == 0 and groups > 1 else [])
@@ -134,7 +133,9 @@
         jnp.bfloat16
     )
     outbound = jnp.dot(dispatch, tokens, preferred_element_type=jnp.float32).astype(jnp.bfloat16)
-    outbound = outbound.reshape(groups, capacity, model_width)
+    lanes = 128 if (capacity * model_width) % 128 == 0 else model_width
+    slab = (capacity * model_width // lanes, lanes)
+    outbound = outbound.reshape((groups,) + slab)
     returned = []
     base = 0
     for index, chunk in enumerate(chunks):
@@ -146,9 +147,10 @@
         summed = lax.psum_scatter(
             partial_value.astype(jnp.bfloat16), "inner", scatter_dimension=0, tiled=True
         )
-        returned.append((summed.reshape(len(chunk), capacity, model_width), chunk, index))
+        returned.append((summed.reshape((len(chunk),) + slab), chunk, index))
     back = [group_exchange(z, chunk, 0, -1, 2 * index + 1) for z, chunk, index in returned]
     back_rows = jnp.concatenate(back, axis=0) if len(back) > 1 else back[0]
+    back_rows = back_rows.reshape(groups, capacity, model_width)
     expert_out = jnp.einsum(
         "gct,gcd->td",
         dispatch.reshape(groups, capacity, tok_count),

time: 373 us -> 343 us (0.920)
  Pallas kernels: 140 us -> 97.7 us
  matrix products: 44.6 us -> 53.6 us
  waiting for transfers between devices: 140 us -> 144 us
    pallas_call x8 -> x6, Pallas kernels: 140 us -> 97.7 us  [group_exchange(): pl.pallas_call(functools.partial(exchange_kernel, groups, tuple(offsets),...]
    dot_general x4 -> x3, matrix products: 14 us -> 26.4 us  [expert_part(): return jnp.dot(hidden, down_mat, preferred_element_type=jnp.float32)]
    all_gather x4 -> x3, waiting for transfers between devices: 50 us -> 58.7 us  [body(): gathered = lax.all_gather(rows, 'inner', axis=0, tiled=True)]
    reduce_scatter x4 -> x3, waiting for transfers between devices: 89.5 us -> 84.9 us  [body(): lax.psum_scatter(partial_value.astype(jnp.bfloat16), 'inner', scatter_dim...]
    dot_general x4 -> x3, matrix products: 19.8 us -> 17.2 us  [expert_part(): gate_pre = jnp.dot(rows_in, gate_mat, preferred_element_type=jnp.float32)]
    reshape x4 -> x3, local copies, waits for them, and re-layouts: 9 us -> 6.63 us  [body(): rows = received.reshape(len(chunk) * capacity, model_width)]
  transfers between devices with their start and end apart: 8 -> 6, of which waited for: 7 -> 5; matrix products, arithmetic and copies ran while one was open for 14% -> 16% of each run, Pallas kernels for 28% -> 18%
where the time goes in v6:
time: 343 us; the launch traced here: 341 us
  waiting for transfers between devices  144 us (42%)
  Pallas kernels  97.7 us (28%)
  matrix products  53.6 us (16%)
  local copies, waits for them, and re-layouts  26.8 us (8%)
  between operations  13.7 us (4%)
  other arithmetic  5.48 us (2%)
    pallas_call x6, Pallas kernels, group_exchange(): pl.pallas_call(functools.partial(exchange_kernel, groups, tuple(offsets),...  97.7 us
    reduce_scatter x3, waiting for transfers between devices, body(): lax.psum_scatter(partial_value.astype(jnp.bfloat16), 'inner', scatter_dim...  84.9 us
    all_gather x3, waiting for transfers between devices, body(): gathered = lax.all_gather(rows, 'inner', axis=0, tiled=True)  58.7 us
    dot_general x3, matrix products, expert_part(): return jnp.dot(hidden, down_mat, preferred_element_type=jnp.float32)  26.4 us
    dot_general x3, matrix products, expert_part(): gate_pre = jnp.dot(rows_in, gate_mat, preferred_element_type=jnp.float32)  17.2 us
  transfers between devices with their start and end apart: 6, of which 5 were waited for; matrix products, arithmetic and copies ran while one was open for 16% of the time, Pallas kernels for 18%

profile of v6, /device:TPU:0, one launch (start us, length us, event | category | flops | bytes accessed | tf_op | source)
XLA Modules:
  0.0 341.3 jit_solution(14524147567326244)
XLA Ops:
  9.1 2.1 convolution_convert_fusion.3
  11.3 4.3 %reshape.42.x_ref = bf16[16,560,128]{2,1,0:T(8,128)(2,1)} reshape(bf16[160,7168]{1,0:T(8,128)(2,1)} %convolution_convert_fusion.3) | data formatting | bytes 4587520 | tf_op jit(solution)/shard_map/reshape | solution.py:138
  15.6 11.5 %shard_map.73 = bf16[4,560,128]{2,1,0:T(8,128)(2,1)} custom-call(bf16[16,560,128]{2,1,0:T(8,128)(2,1)} %reshape.42.x_ref), custom_call_target="tpu_custom_call" | custom-call | tf_op jit(solution)/shard_map/pallas_call | solution.py:91
  27.1 2.1 reshape.43
  29.3 15.5 %shard_map.77 = bf16[4,560,128]{2,1,0:T(8,128)(2,1)} custom-call(bf16[16,560,128]{2,1,0:T(8,128)(2,1)} %reshape.42.x_ref), custom_call_target="tpu_custom_call" | custom-call | tf_op jit(solution)/shard_map/pallas_call | solution.py:91
  44.8 2.1 reshape.47
  47.0 22.7 %shard_map.75 = bf16[8,560,128]{2,1,0:T(8,128)(2,1)} custom-call(bf16[16,560,128]{2,1,0:T(8,128)(2,1)} %reshape.42.x_ref), custom_call_target="tpu_custom_call" | custom-call | tf_op jit(solution)/shard_map/pallas_call | solution.py:91
  69.7 2.4 reshape.45
  72.2 5.1 %fusion.15 = f32[320,256]{1,0:T(8,128)S(1)} fusion(bf16[320,7168]{1,0:T(8,128)(2,1)} %all-gather.4.cloned.1.call-done, bf16[1,7168,256]{2,1,0:T(8,128)(2,1)} %param.10), kind=kOutput, calls=%fused_computation.20 | convolution fusion | flops 1174405120 | bytes 8585216 | tf_op jit(solution)/shard_map/dot_general | solution.py:106
  77.3 1.5 copy-done.9
  78.8 1.4 fusion.35
  80.8 3.5 %convolution_convert_fusion.2 = bf16[320,7168]{1,0:T(8,128)(2,1)} fusion(bf16[320,256]{1,0:T(8,128)(2,1)S(1)} %fusion.35, bf16[1,256,7168]{2,1,0:T(8,128)(2,1)S(1)} %copy-done.2), kind=kOutput, calls=%fused_computation.2 | convolution fusion | flops 1176698880 | bytes 8421376 | tf_op jit(solution)/shard_map/dot_general | solution.py:109
  84.4 15.6 %all-gather.8.cloned.1.call-done = bf16[320,7168]{1,0:T(8,128)(2,1)} async-done(((bf16[40,7168]{1,0:T(8,128)(2,1)}), bf16[320,7168]{1,0:T(8,128)(2,1)}) %all-gather.8.cloned.1.call-update) | async-done | bytes 4587536 | tf_op jit(solution)/shard_map/all_gather | solution.py:145
  100.0 4.9 %fusion.11 = f32[320,256]{1,0:T(8,128)S(1)} fusion(bf16[320,7168]{1,0:T(8,128)(2,1)} %all-gather.8.cloned.1.call-done, bf16[1,7168,256]{2,1,0:T(8,128)(2,1)} %param.10), kind=kOutput, calls=%fused_computation.16 | convolution fusion | flops 1174405120 | bytes 8585216 | tf_op jit(solution)/shard_map/dot_general | solution.py:106
  104.9 0.9 copy-done.8
  105.8 1.4 fusion.32
  107.9 3.5 %convolution_convert_fusion.1 = bf16[320,7168]{1,0:T(8,128)(2,1)} fusion(bf16[320,256]{1,0:T(8,128)(2,1)S(1)} %fusion.32, bf16[1,256,7168]{2,1,0:T(8,128)(2,1)S(1)} %copy-done.3), kind=kOutput, calls=%fused_computation.1 | convolution fusion | flops 1176698880 | bytes 8421376 | tf_op jit(solution)/shard_map/dot_general | solution.py:109
  111.7 43.0 %all-gather.6.cloned.1.call-done = bf16[640,7168]{1,0:T(8,128)(2,1)} async-done(((bf16[80,7168]{1,0:T(8,128)(2,1)}), bf16[640,7168]{1,0:T(8,128)(2,1)}) %all-gather.6.cloned.1.call-update) | async-done | bytes 9175056 | tf_op jit(solution)/shard_map/all_gather | solution.py:145
  154.7 7.2 %fusion.13 = f32[640,256]{1,0:T(8,128)S(1)} fusion(bf16[640,7168]{1,0:T(8,128)(2,1)} %all-gather.6.cloned.1.call-done, bf16[1,7168,256]{2,1,0:T(8,128)(2,1)} %param.10), kind=kOutput, calls=%fused_computation.18 | convolution fusion | flops 2348810240 | bytes 13500416 | tf_op jit(solution)/shard_map/dot_general | solution.py:106
  161.9 19.4 %convolution_convert_fusion = bf16[640,7168]{1,0:T(8,128)(2,1)} fusion(bf16[1,256,7168]{2,1,0:T(8,128)(2,1)} %param.12, bf16[640,7168]{1,0:T(8,128)(2,1)} %all-gather.6.cloned.1.call-done, bf16[1,7168,256]{2,1,0:T(8,128)(2,1)} %param.11, f32[640,256]{1,0:T(8,128)S(1)} %fusion.13), kind=kOutput, calls=%fused_computation | convolution fusion | flops 4703191040 | bytes 26345472 | tf_op jit(solution)/shard_map/dot_general | solution.py:109
  181.3 14.5 %reduce-scatter.4.cloned.1.call-done = bf16[40,7168]{1,0:T(8,128)(2,1)} async-done(((bf16[320,7168]{1,0:T(8,128)(2,1)}), bf16[40,7168]{1,0:T(8,128)(2,1)}) %reduce-scatter.4.cloned.1.call-update) | async-done | bytes 573456 | tf_op jit(solution)/shard_map/reduce_scatter | solution.py:147
  195.8 2.1 reshape.44.x_ref
  197.9 9.2 %shard_map.74 = bf16[4,560,128]{2,1,0:T(8,128)(2,1)} custom-call(bf16[4,560,128]{2,1,0:T(8,128)(2,1)} %reshape.44.x_ref), custom_call_target="tpu_custom_call" | custom-call | tf_op jit(solution)/shard_map/pallas_call | solution.py:91
  207.1 28.8 %reduce-scatter.8.cloned.1.call-done = bf16[40,7168]{1,0:T(8,128)(2,1)} async-done(((bf16[320,7168]{1,0:T(8,128)(2,1)}), bf16[40,7168]{1,0:T(8,128)(2,1)}) %reduce-scatter.8.cloned.1.call-update) | async-done | bytes 573456 | tf_op jit(solution)/shard_map/reduce_scatter | solution.py:147
  235.9 2.1 reshape.48.x_ref
  238.0 13.9 %shard_map.78 = bf16[4,560,128]{2,1,0:T(8,128)(2,1)} custom-call(bf16[4,560,128]{2,1,0:T(8,128)(2,1)} %reshape.48.x_ref), custom_call_target="tpu_custom_call" | custom-call | tf_op jit(solution)/shard_map/pallas_call | solution.py:91
  252.0 41.6 %reduce-scatter.6.cloned.1.call-done = bf16[80,7168]{1,0:T(8,128)(2,1)} async-done(((bf16[640,7168]{1,0:T(8,128)(2,1)}), bf16[80,7168]{1,0:T(8,128)(2,1)}) %reduce-scatter.6.cloned.1.call-update) | async-done | bytes 1146896 | tf_op jit(solution)/shard_map/reduce_scatter | solution.py:147
  293.5 2.4 reshape.46.x_ref
  295.9 25.0 %shard_map.76 = bf16[8,560,128]{2,1,0:T(8,128)(2,1)} custom-call(bf16[8,560,128]{2,1,0:T(8,128)(2,1)} %reshape.46.x_ref), custom_call_target="tpu_custom_call" | custom-call | tf_op jit(solution)/shard_map/pallas_call | solution.py:91
  320.9 2.9 pad_maximum_fusion
  323.8 5.5 %reshape.49 = bf16[16,10,7168]{2,1,0:T(8,128)(2,1)} reshape(bf16[16,560,128]{2,1,0:T(8,128)(2,1)} %pad_maximum_fusion) | data formatting | bytes 4587520 | tf_op jit(solution)/shard_map/reshape | solution.py:153
  329.4 5.0 %fusion.1 = bf16[128,7168]{1,0:T(8,128)(2,1)} fusion(bf16[16,10,7168]{2,1,0:T(8,128)(2,1)} %reshape.49, f32[128]{0:T(128)S(1)} %copy-done.10, s32[16,10]{0,1:T(8,128)S(1)} %multiply_add_fusion, s32[128]{0:T(128)S(1)} %compare_select_fusion.23), kind=kOutput, calls=%fused_computation.6 | convolution fusion | flops 295456768 | bytes 4130432 | tf_op jit(solution)/shard_map/gct,gcd->td/dot_general | solution.py:154
  (38 shorter events, 4.3 us)
Async XLA Ops:
  6.5 2.6 copy-start
  6.5 65.6 %all-gather.4.cloned.1.call-start = ((), (), s32[]{:S(2)}) async-start(), calls=%async_computation.3 | async-start | bytes 5160960 | tf_op jit(solution)/shard_map/all_gather | solution.py:145
  29.2 70.8 %all-gather.8.cloned.1.call-start = ((), (), s32[]{:S(2)}) async-start(), calls=%async_computation.7 | async-start | bytes 5160960 | tf_op jit(solution)/shard_map/all_gather | solution.py:145
  46.9 107.8 %all-gather.6.cloned.1.call-start = ((), (), s32[]{:S(2)}) async-start(), calls=%async_computation.5 | async-start | bytes 10321920 | tf_op jit(solution)/shard_map/all_gather | solution.py:145
  72.1 123.8 %reduce-scatter.4.cloned.1.call-start = ((), (), s32[]{:S(2)}) async-start(), calls=%async_computation.4 | async-start | bytes 5160960 | tf_op jit(solution)/shard_map/reduce_scatter | solution.py:147
  72.1 5.1 %copy-start.4 = (bf16[1,7168,256]{2,1,0:T(8,128)(2,1)S(1)}, bf16[1,7168,256]{2,1,0:T(8,128)(2,1)}, u32[]{:S(2)}) copy-start(bf16[1,7168,256]{2,1,0:T(8,128)(2,1)} %param.11) | copy-start | bytes 11010052
  72.1 6.6 %copy-start.9 = (bf16[320,7168]{1,0:T(8,128)(2,1)S(1)}, bf16[320,7168]{1,0:T(8,128)(2,1)}, u32[]{:S(2)}) copy-start(bf16[320,7168]{1,0:T(8,128)(2,1)} %all-gather.4.cloned.1.call-done) | copy-start | bytes 13762564
  78.8 2.0 copy-start.2
  84.3 151.6 %reduce-scatter.8.cloned.1.call-start = ((), (), s32[]{:S(2)}) async-start(), calls=%async_computation.8 | async-start | bytes 5160960 | tf_op jit(solution)/shard_map/reduce_scatter | solution.py:147
  100.0 4.9 %copy-start.5 = (bf16[1,7168,256]{2,1,0:T(8,128)(2,1)S(1)}, bf16[1,7168,256]{2,1,0:T(8,128)(2,1)}, u32[]{:S(2)}) copy-start(bf16[1,7168,256]{2,1,0:T(8,128)(2,1)} %param.11) | copy-start | bytes 11010052
  100.0 5.8 %copy-start.8 = (bf16[320,7168]{1,0:T(8,128)(2,1)S(1)}, bf16[320,7168]{1,0:T(8,128)(2,1)}, u32[]{:S(2)}) copy-start(bf16[320,7168]{1,0:T(8,128)(2,1)} %all-gather.8.cloned.1.call-done) | copy-start | bytes 13762564
  105.8 2.0 copy-start.3
  111.4 182.1 %reduce-scatter.6.cloned.1.call-start = ((), (), s32[]{:S(2)}) async-start(), calls=%async_computation.6 | async-start | bytes 10321920 | tf_op jit(solution)/shard_map/reduce_scatter | solution.py:147
  207.1 113.8 %copy-start.6 = (bf16[4,560,128]{2,1,0:T(8,128)(2,1)S(1)}, bf16[4,560,128]{2,1,0:T(8,128)(2,1)}, u32[]{:S(2)}) copy-start(bf16[4,560,128]{2,1,0:T(8,128)(2,1)} %shard_map.74) | copy-start | bytes 1720324
  252.0 69.0 %copy-start.7 = (bf16[4,560,128]{2,1,0:T(8,128)(2,1)S(1)}, bf16[4,560,128]{2,1,0:T(8,128)(2,1)}, u32[]{:S(2)}) copy-start(bf16[4,560,128]{2,1,0:T(8,128)(2,1)} %shard_map.78) | copy-start | bytes 1720324
  323.8 5.6 %copy-start.10 = (f32[128]{0:T(128)S(1)}, f32[128]{0:T(128)}, u32[]{:S(2)}) copy-start(f32[128]{0:T(128)} %param.9) | copy-start | bytes 1540
  323.8 10.6 %copy-start.1 = (bf16[128,7168]{1,0:T(8,128)(2,1)S(1)}, bf16[128,7168]{1,0:T(8,128)(2,1)}, u32[]{:S(2)}) copy-start(bf16[128,7168]{1,0:T(8,128)(2,1)} %param.7) | copy-start | bytes 5505028
Sparse Core Ops, SparseCore 0:
  29.4 35.1 all-gather.3
  66.2 33.7 all-gather.7
  101.7 52.9 all-gather.5
  157.0 38.7 reduce-scatter.3
  198.2 37.6 reduce-scatter.7
  238.2 55.2 reduce-scatter.5

commit v7 on v6

--- a/solution.py
+++ b/solution.py
@@ -18,9 +18,8 @@
 def chunk_orders(groups):
     if groups == 16:
         return [
-            [(0, 0), (0, 1), (0, 3), (0, 2)],
-            [(1, 1), (3, 3), (1, 3), (3, 1), (1, 2), (3, 2), (2, 1), (2, 3)],
-            [(1, 0), (3, 0), (2, 0), (2, 2)],
+            [(0, 0), (0, 1), (0, 3), (1, 0), (3, 0), (1, 2), (3, 2), (2, 2)],
+            [(0, 2), (2, 0), (1, 1), (3, 3), (1, 3), (3, 1), (2, 1), (2, 3)],
         ]
     pairs = [((0, k), (0, groups - k)) for k in range(1, (groups + 1) // 2)]
     first = [(0, 0)] + ([(0, groups // 2)] if groups % 2 == 0 and groups > 1 else [])

time: 343 us -> 310 us (0.904)
  waiting for transfers between devices: 144 us -> 125 us
  Pallas kernels: 97.7 us -> 84.4 us
  matrix products: 53.6 us -> 61.1 us
  local copies, waits for them, and re-layouts: 26.8 us -> 19.5 us
    reduce_scatter x3 -> x2, waiting for transfers between devices: 84.9 us -> 68 us  [body(): lax.psum_scatter(partial_value.astype(jnp.bfloat16), 'inner', scatter_dim...]
    pallas_call x6 -> x4, Pallas kernels: 97.7 us -> 84.4 us  [group_exchange(): pl.pallas_call(functools.partial(exchange_kernel, groups, tuple(offsets),...]
    dot_general x3 -> x2, matrix products: 26.4 us -> 39.6 us  [expert_part(): return jnp.dot(hidden, down_mat, preferred_element_type=jnp.float32)]
    unnamed x22 -> x8, local copies, waits for them, and re-layouts: 3.67 us -> 0.02 us
    dot_general x3 -> x2, matrix products: 17.2 us -> 14.3 us  [expert_part(): gate_pre = jnp.dot(rows_in, gate_mat, preferred_element_type=jnp.float32)]
    all_gather x3 -> x2, waiting for transfers between devices: 58.7 us -> 57.3 us  [body(): gathered = lax.all_gather(rows, 'inner', axis=0, tiled=True)]
  transfers between devices with their start and end apart: 6 -> 4, of which waited for: 5 -> 4; matrix products, arithmetic and copies ran while one was open for 16% -> 19% of each run, Pallas kernels for 18% -> 13%
where the time goes in v7:
time: 310 us; the launch traced here: 309 us
  waiting for transfers between devices  125 us (40%)
  Pallas kernels  84.4 us (27%)
  matrix products  61.1 us (20%)
  local copies, waits for them, and re-layouts  19.5 us (6%)
  between operations  13.2 us (4%)
  other arithmetic  5.42 us (2%)
    pallas_call x4, Pallas kernels, group_exchange(): pl.pallas_call(functools.partial(exchange_kernel, groups, tuple(offsets),...  84.4 us
    reduce_scatter x2, waiting for transfers between devices, body(): lax.psum_scatter(partial_value.astype(jnp.bfloat16), 'inner', scatter_dim...  68 us
    all_gather x2, waiting for transfers between devices, body(): gathered = lax.all_gather(rows, 'inner', axis=0, tiled=True)  57.3 us
    dot_general x2, matrix products, expert_part(): return jnp.dot(hidden, down_mat, preferred_element_type=jnp.float32)  39.6 us
    dot_general x2, matrix products, expert_part(): gate_pre = jnp.dot(rows_in, gate_mat, preferred_element_type=jnp.float32)  14.3 us
  transfers between devices with their start and end apart: 4, of which 4 were waited for; matrix products, arithmetic and copies ran while one was open for 19% of the time, Pallas kernels for 13%

profile of v7, /device:TPU:0, one launch (start us, length us, event | category | flops | bytes accessed | tf_op | source)
XLA Modules:
  0.0 309.3 jit_solution(10974906032434725652)
XLA Ops:
  6.5 0.9 fusion.42
  7.4 0.2 reduce_window_sum.11
  7.6 0.8 select_reduce_fusion
  8.4 0.7 compare_select_fusion.23
  9.1 2.1 convolution_convert_fusion.2
  11.3 4.3 %reshape.36.x_ref = bf16[16,560,128]{2,1,0:T(8,128)(2,1)} reshape(bf16[160,7168]{1,0:T(8,128)(2,1)} %convolution_convert_fusion.2) | data formatting | bytes 4587520 | tf_op jit(solution)/shard_map/reshape | solution.py:137
  15.6 21.5 %shard_map.73 = bf16[8,560,128]{2,1,0:T(8,128)(2,1)} custom-call(bf16[16,560,128]{2,1,0:T(8,128)(2,1)} %reshape.36.x_ref), custom_call_target="tpu_custom_call" | custom-call | tf_op jit(solution)/shard_map/pallas_call | solution.py:90
  37.1 2.4 reshape.37
  39.5 0.0 all-gather.3.cloned.1.call-update
  39.5 0.0 all-gather.5.cloned.1.call-start
  39.5 21.1 %shard_map.75 = bf16[8,560,128]{2,1,0:T(8,128)(2,1)} custom-call(bf16[16,560,128]{2,1,0:T(8,128)(2,1)} %reshape.36.x_ref), custom_call_target="tpu_custom_call" | custom-call | tf_op jit(solution)/shard_map/pallas_call | solution.py:90
  60.6 2.4 reshape.39
  63.1 0.0 all-gather.5.cloned.1.call-update
  63.1 0.0 reduce-scatter.3.cloned.1.call-start
  63.1 29.6 %all-gather.3.cloned.1.call-done = bf16[640,7168]{1,0:T(8,128)(2,1)} async-done(((bf16[80,7168]{1,0:T(8,128)(2,1)}), bf16[640,7168]{1,0:T(8,128)(2,1)}) %all-gather.3.cloned.1.call-update) | async-done | bytes 9175056 | tf_op jit(solution)/shard_map/all_gather | solution.py:144
  92.7 7.2 %fusion.10 = f32[640,256]{1,0:T(8,128)S(1)} fusion(bf16[640,7168]{1,0:T(8,128)(2,1)} %all-gather.3.cloned.1.call-done, bf16[1,7168,256]{2,1,0:T(8,128)(2,1)} %param.10), kind=kOutput, calls=%fused_computation.14 | convolution fusion | flops 2348810240 | bytes 13500416 | tf_op jit(solution)/shard_map/dot_general | solution.py:105
  99.9 19.8 %convolution_convert_fusion.1 = bf16[640,7168]{1,0:T(8,128)(2,1)} fusion(bf16[1,256,7168]{2,1,0:T(8,128)(2,1)} %param.12, bf16[640,7168]{1,0:T(8,128)(2,1)} %all-gather.3.cloned.1.call-done, bf16[1,7168,256]{2,1,0:T(8,128)(2,1)} %param.11, f32[640,256]{1,0:T(8,128)S(1)} %fusion.10), kind=kOutput, calls=%fused_computation.1 | convolution fusion | flops 4703191040 | bytes 26345472 | tf_op jit(solution)/shard_map/dot_general | solution.py:108
  119.7 0.0 reduce-scatter.3.cloned.1.call-update
  119.7 0.2 reduce-scatter.5.cloned.1.call-start
  120.0 27.7 %all-gather.5.cloned.1.call-done = bf16[640,7168]{1,0:T(8,128)(2,1)} async-done(((bf16[80,7168]{1,0:T(8,128)(2,1)}), bf16[640,7168]{1,0:T(8,128)(2,1)}) %all-gather.5.cloned.1.call-update) | async-done | bytes 9175056 | tf_op jit(solution)/shard_map/all_gather | solution.py:144
  147.7 7.2 %fusion.8 = f32[640,256]{1,0:T(8,128)S(1)} fusion(bf16[640,7168]{1,0:T(8,128)(2,1)} %all-gather.5.cloned.1.call-done, bf16[1,7168,256]{2,1,0:T(8,128)(2,1)} %param.10), kind=kOutput, calls=%fused_computation.12 | convolution fusion | flops 2348810240 | bytes 13500416 | tf_op jit(solution)/shard_map/dot_general | solution.py:105
  154.8 19.8 %convolution_convert_fusion = bf16[640,7168]{1,0:T(8,128)(2,1)} fusion(bf16[1,256,7168]{2,1,0:T(8,128)(2,1)} %param.12, bf16[640,7168]{1,0:T(8,128)(2,1)} %all-gather.5.cloned.1.call-done, bf16[1,7168,256]{2,1,0:T(8,128)(2,1)} %param.11, f32[640,256]{1,0:T(8,128)S(1)} %fusion.8), kind=kOutput, calls=%fused_computation | convolution fusion | flops 4703191040 | bytes 26345472 | tf_op jit(solution)/shard_map/dot_general | solution.py:108
  174.6 0.0 reduce-scatter.5.cloned.1.call-update
  174.6 31.9 %reduce-scatter.3.cloned.1.call-done = bf16[80,7168]{1,0:T(8,128)(2,1)} async-done(((bf16[640,7168]{1,0:T(8,128)(2,1)}), bf16[80,7168]{1,0:T(8,128)(2,1)}) %reduce-scatter.3.cloned.1.call-update) | async-done | bytes 1146896 | tf_op jit(solution)/shard_map/reduce_scatter | solution.py:146
  206.5 2.4 reshape.38.x_ref
  208.9 19.6 %shard_map.74 = bf16[8,560,128]{2,1,0:T(8,128)(2,1)} custom-call(bf16[8,560,128]{2,1,0:T(8,128)(2,1)} %reshape.38.x_ref), custom_call_target="tpu_custom_call" | custom-call | tf_op jit(solution)/shard_map/pallas_call | solution.py:90
  228.5 36.1 %reduce-scatter.5.cloned.1.call-done = bf16[80,7168]{1,0:T(8,128)(2,1)} async-done(((bf16[640,7168]{1,0:T(8,128)(2,1)}), bf16[80,7168]{1,0:T(8,128)(2,1)}) %reduce-scatter.5.cloned.1.call-update) | async-done | bytes 1146896 | tf_op jit(solution)/shard_map/reduce_scatter | solution.py:146
  264.6 2.4 reshape.40.x_ref
  267.0 22.3 %shard_map.76 = bf16[8,560,128]{2,1,0:T(8,128)(2,1)} custom-call(bf16[8,560,128]{2,1,0:T(8,128)(2,1)} %reshape.40.x_ref), custom_call_target="tpu_custom_call" | custom-call | tf_op jit(solution)/shard_map/pallas_call | solution.py:90
  289.3 2.9 pad_maximum_fusion
  292.1 5.6 %reshape.41 = bf16[16,10,7168]{2,1,0:T(8,128)(2,1)} reshape(bf16[16,560,128]{2,1,0:T(8,128)(2,1)} %pad_maximum_fusion) | data formatting | bytes 4587520 | tf_op jit(solution)/shard_map/reshape | solution.py:152
  297.7 5.0 %fusion.1 = bf16[128,7168]{1,0:T(8,128)(2,1)} fusion(bf16[16,10,7168]{2,1,0:T(8,128)(2,1)} %reshape.41, f32[128]{0:T(128)S(1)} %copy-done.3, s32[16,10]{0,1:T(8,128)S(1)} %multiply_add_fusion, s32[128]{0:T(128)S(1)} %compare_select_fusion.23), kind=kOutput, calls=%fused_computation.5 | convolution fusion | flops 295456768 | bytes 4130432 | tf_op jit(solution)/shard_map/gct,gcd->td/dot_general | solution.py:153
  (10 shorter events, 0.0 us)
Async XLA Ops:
  6.5 2.6 copy-start
  6.5 86.2 %all-gather.3.cloned.1.call-start = ((), (), s32[]{:S(2)}) async-start(), calls=%async_computation.2 | async-start | bytes 10321920 | tf_op jit(solution)/shard_map/all_gather | solution.py:144
  39.5 108.2 %all-gather.5.cloned.1.call-start = ((), (), s32[]{:S(2)}) async-start(), calls=%async_computation.4 | async-start | bytes 10321920 | tf_op jit(solution)/shard_map/all_gather | solution.py:144
  63.1 143.4 %reduce-scatter.3.cloned.1.call-start = ((), (), s32[]{:S(2)}) async-start(), calls=%async_computation.3 | async-start | bytes 10321920 | tf_op jit(solution)/shard_map/reduce_scatter | solution.py:146
  119.7 144.8 %reduce-scatter.5.cloned.1.call-start = ((), (), s32[]{:S(2)}) async-start(), calls=%async_computation.5 | async-start | bytes 10321920 | tf_op jit(solution)/shard_map/reduce_scatter | solution.py:146
  228.5 60.8 %copy-start.2 = (bf16[8,560,128]{2,1,0:T(8,128)(2,1)S(1)}, bf16[8,560,128]{2,1,0:T(8,128)(2,1)}, u32[]{:S(2)}) copy-start(bf16[8,560,128]{2,1,0:T(8,128)(2,1)} %shard_map.74) | copy-start | bytes 3440644
  292.1 5.6 %copy-start.3 = (f32[128]{0:T(128)S(1)}, f32[128]{0:T(128)}, u32[]{:S(2)}) copy-start(f32[128]{0:T(128)} %param.9) | copy-start | bytes 1540
  292.1 10.6 %copy-start.1 = (bf16[128,7168]{1,0:T(8,128)(2,1)S(1)}, bf16[128,7168]{1,0:T(8,128)(2,1)}, u32[]{:S(2)}) copy-start(bf16[128,7168]{1,0:T(8,128)(2,1)} %param.7) | copy-start | bytes 5505028
Sparse Core Ops, SparseCore 0:
  39.6 53.0 all-gather.2
  94.4 53.2 all-gather.4
  150.1 56.3 reduce-scatter.2
  208.8 55.7 reduce-scatter.4

commit v8 on v7

--- a/solution.py
+++ b/solution.py
@@ -101,6 +101,60 @@
     )(x)
 
 
+def partner_kernel(swap, x_ref, y_ref, local_sem, send_sem, recv_sem):
+    group = lax.axis_index("group")
+    inner = lax.axis_index("inner")
+    core = lax.rem(inner, 2)
+    partner = inner + 1 - 2 * core
+    barrier = pltpu.get_barrier_semaphore()
+    pl.semaphore_signal(barrier, inc=1, device_id=(group, partner), device_id_type=MESH)
+    pl.semaphore_wait(barrier, 1)
+    if swap:
+        src, dst, mine = x_ref.at[1 - core], y_ref, None
+        theirs = y_ref
+    else:
+        src, dst = x_ref, y_ref.at[core]
+        mine = pltpu.make_async_copy(x_ref, y_ref.at[core], local_sem)
+        mine.start()
+        theirs = y_ref.at[1 - core]
+    copy = pltpu.make_async_remote_copy(
+        src_ref=src,
+        dst_ref=dst,
+        send_sem=send_sem,
+        recv_sem=recv_sem,
+        device_id=(group, partner),
+        device_id_type=MESH,
+    )
+    copy.start()
+    copy.wait_send()
+    pltpu.make_async_remote_copy(
+        src_ref=src,
+        dst_ref=theirs,
+        send_sem=send_sem,
+        recv_sem=recv_sem,
+        device_id=(group, partner),
+        device_id_type=MESH,
+    ).wait_recv()
+    if mine is not None:
+        mine.wait()
+
+
+def partner_exchange(x, swap, collective_id):
+    shape = x.shape[1:] if swap else (2,) + x.shape
+    return pl.pallas_call(
+        functools.partial(partner_kernel, swap),
+        out_shape=jax.ShapeDtypeStruct(shape, x.dtype),
+        in_specs=[pl.BlockSpec(memory_space=pl.ANY)],
+        out_specs=pl.BlockSpec(memory_space=pl.ANY),
+        scratch_shapes=[
+            pltpu.SemaphoreType.DMA,
+            pltpu.SemaphoreType.DMA,
+            pltpu.SemaphoreType.DMA,
+        ],
+        compiler_params=pltpu.CompilerParams(collective_id=collective_id, has_side_effects=True),
+    )(x)
+
+
 def expert_part(rows_in, gate_mat, up_mat, down_mat):
     gate_pre = jnp.dot(rows_in, gate_mat, preferred_element_type=jnp.float32)
     up_pre = jnp.dot(rows_in, up_mat, preferred_element_type=jnp.float32)
@@ -110,6 +164,7 @@
 
 def body(tokens, target, gate_scale, gate_weight, up_weight, down_weight):
     groups = lax.axis_size("group")
+    inner_size = lax.axis_size("inner")
     tok_count = tokens.shape[0]
     model_width = tokens.shape[1]
     capacity = tok_count * 5 // (4 * groups)
@@ -141,10 +196,19 @@
         received = group_exchange(outbound, chunk, base, 1, 2 * index)
         base += len(chunk)
         rows = received.reshape(len(chunk) * capacity, model_width)
-        gathered = lax.all_gather(rows, "inner", axis=0, tiled=True)
+        same_core = [list(range(c, inner_size, 2)) for c in range(2)]
+        core = lax.rem(lax.axis_index("inner"), 2)
+        mine = lax.all_gather(rows, "inner", axis=0, tiled=True, axis_index_groups=same_core)
+        gathered = partner_exchange(mine, False, 8 + 4 * index).reshape(-1, model_width)
         partial_value = expert_part(gathered, gate_weight[0], up_weight[0], down_weight[0])
+        partial_value = partial_value.astype(jnp.bfloat16).reshape((2, -1, model_width))
+        received_sum = partner_exchange(partial_value, True, 9 + 4 * index)
+        own_part = lax.dynamic_index_in_dim(partial_value, core, axis=0, keepdims=False)
+        pair_sum = (own_part.astype(jnp.float32) + received_sum.astype(jnp.float32)).astype(
+            jnp.bfloat16
+        )
         summed = lax.psum_scatter(
-            partial_value.astype(jnp.bfloat16), "inner", scatter_dimension=0, tiled=True
+            pair_sum, "inner", scatter_dimension=0, tiled=True, axis_index_groups=same_core
         )
         returned.append((summed.reshape((len(chunk),) + slab), chunk, index))
     back = [group_exchange(z, chunk, 0, -1, 2 * index + 1) for z, chunk, index in returned]

time: 310 us -> 552 us (1.78)
  Pallas kernels: 84.4 us -> 383 us
  waiting for transfers between devices: 125 us -> 55.4 us
  other arithmetic: 5.42 us -> 20.5 us
    pallas_call x0 -> x4, Pallas kernels: none -> 297 us  [partner_exchange(): pl.pallas_call(functools.partial(partner_kernel, swap), out_shape=jax.Sha...]
    reduce_scatter x2, waiting for transfers between devices: 68 us -> 27.4 us  [body(): lax.psum_scatter(pair_sum, 'inner', scatter_dimension=0, tiled=True, axis...]
    all_gather x2, waiting for transfers between devices: 57.3 us -> 28 us  [body(): lax.all_gather(rows, 'inner', axis=0, tiled=True, axis_index_groups=same_...]
    convert_element_type x0 -> x2, other arithmetic: none -> 15.1 us  [body(): (own_part.astype(jnp.float32) + received_sum.astype(jnp.float32)).astype(...]
  transfers between devices with their start and end apart: 4 -> 4, of which waited for: 4 -> 2; matrix products, arithmetic and copies ran while one was open for 19% -> 13% of each run, Pallas kernels for 13% -> 61%
where the time goes in v8:
time: 552 us
  Pallas kernels  383 us (69%)
  matrix products  59.3 us (11%)
  waiting for transfers between devices  55.4 us (10%)
  other arithmetic  20.5 us (4%)
  local copies, waits for them, and re-layouts  19.7 us (4%)
  between operations  13.3 us (2%)
    pallas_call x4, Pallas kernels, partner_exchange(): pl.pallas_call(functools.partial(partner_kernel, swap), out_shape=jax.Sha...  297 us
    pallas_call x4, Pallas kernels, group_exchange(): pl.pallas_call(functools.partial(exchange_kernel, groups, tuple(offsets),...  86.1 us
    dot_general x2, matrix products, expert_part(): return jnp.dot(hidden, down_mat, preferred_element_type=jnp.float32)  37.8 us
    all_gather x2, waiting for transfers between devices, body(): lax.all_gather(rows, 'inner', axis=0, tiled=True, axis_index_groups=same_...  28 us
    reduce_scatter x2, waiting for transfers between devices, body(): lax.psum_scatter(pair_sum, 'inner', scatter_dimension=0, tiled=True, axis...  27.4 us
    convert_element_type x2, other arithmetic, body(): (own_part.astype(jnp.float32) + received_sum.astype(jnp.float32)).astype(...  15.1 us
    dot_general x2, matrix products, expert_part(): gate_pre = jnp.dot(rows_in, gate_mat, preferred_element_type=jnp.float32)  14.3 us
  transfers between devices with their start and end apart: 4, of which 2 were waited for; matrix products, arithmetic and copies ran while one was open for 13% of the time, Pallas kernels for 61%

profile of v8, /device:TPU:0, one launch (start us, length us, event | category | flops | bytes accessed | tf_op | source)
XLA Modules:
  0.0 551.8 jit_solution(2118044938240162074)
XLA Ops:
  6.5 0.9 fusion.44
  7.4 0.2 reduce_window_sum.11
  7.6 0.8 select_reduce_fusion
  8.4 0.7 compare_select_fusion.23
  9.1 2.1 convolution_convert_fusion.2
  11.3 4.3 reshape.52.x_ref
  15.6 21.5 %shard_map.73 = bf16[8,560,128]{2,1,0:T(8,128)(2,1)} custom-call(bf16[16,560,128]{2,1,0:T(8,128)(2,1)} %reshape.52.x_ref), custom_call_target="tpu_custom_call" | custom-call | tf_op jit(solution)/shard_map/pallas_call | solution.py:90
  37.1 2.4 reshape.53
  39.5 0.0 all-gather.5.cloned.1.call-start
  39.6 21.1 %shard_map.77 = bf16[8,560,128]{2,1,0:T(8,128)(2,1)} custom-call(bf16[16,560,128]{2,1,0:T(8,128)(2,1)} %reshape.52.x_ref), custom_call_target="tpu_custom_call" | custom-call | tf_op jit(solution)/shard_map/pallas_call | solution.py:90
  60.7 2.4 reshape.57
  63.1 0.2 reduce-scatter.3.cloned.1.call-start
  63.3 28.0 %all-gather.3.cloned.1.call-done.x_ref = bf16[320,7168]{1,0:T(8,128)(2,1)} async-done(((bf16[80,7168]{1,0:T(8,128)(2,1)}), bf16[320,7168]{1,0:T(8,128)(2,1)}) %all-gather.3.cloned.1.call-update) | async-done | bytes 4587536 | tf_op jit(solution)/shard_map/all_gather | solution.py:201
  91.3 140.1 %shard_map.74 = bf16[2,320,7168]{2,1,0:T(8,128)(2,1)} custom-call(bf16[320,7168]{1,0:T(8,128)(2,1)} %all-gather.3.cloned.1.call-done.x_ref), custom_call_target="tpu_custom_call" | custom-call | tf_op jit(solution)/shard_map/pallas_call | solution.py:144
  231.4 7.2 %fusion.12 = f32[640,256]{1,0:T(8,128)S(1)} fusion(bf16[640,7168]{1,0:T(8,128)(2,1)} %bitcast.52, bf16[1,7168,256]{2,1,0:T(8,128)(2,1)} %param.10), kind=kOutput, calls=%fused_computation.18 | convolution fusion | flops 2348810240 | bytes 13500416 | tf_op jit(solution)/shard_map/dot_general | solution.py:159
  238.5 18.9 %convolution_convert_fusion.1 = bf16[640,7168]{1,0:T(8,128)(2,1)} fusion(bf16[1,256,7168]{2,1,0:T(8,128)(2,1)} %param.12, bf16[640,7168]{1,0:T(8,128)(2,1)} %bitcast.53, bf16[1,7168,256]{2,1,0:T(8,128)(2,1)} %param.11, f32[640,256]{1,0:T(8,128)S(1)} %fusion.12), kind=kOutput, calls=%fused_computation.1 | convolution fusion | flops 4703191040 | bytes 26345472 | tf_op jit(solution)/shard_map/dot_general | solution.py:162
  257.4 8.2 %shard_map.75 = bf16[320,7168]{1,0:T(8,128)(2,1)} custom-call(bf16[2,320,7168]{2,1,0:T(8,128)(2,1)} %bitcast.50), custom_call_target="tpu_custom_call" | custom-call | tf_op jit(solution)/shard_map/pallas_call | solution.py:144
  265.7 7.5 %fusion.1 = bf16[320,7168]{1,0:T(8,128)(2,1)} fusion(bf16[320,7168]{1,0:T(8,128)(2,1)} %shard_map.75, bf16[2,320,7168]{2,1,0:T(8,128)(2,1)} %bitcast.51, s32[]{:T(128)S(6)} %select_n.30), kind=kLoop, calls=%fused_computation.5 | loop fusion | flops 9175040 | bytes 13762564 | tf_op jit(solution)/shard_map/convert_element_type | solution.py:207
  273.2 0.3 reduce-scatter.5.cloned.1.call-start
  273.5 140.5 %shard_map.78 = bf16[2,320,7168]{2,1,0:T(8,128)(2,1)} custom-call(bf16[320,7168]{1,0:T(8,128)(2,1)} %all-gather.5.cloned.1.call-done.x_ref), custom_call_target="tpu_custom_call" | custom-call | tf_op jit(solution)/shard_map/pallas_call | solution.py:144
  414.0 7.2 %fusion.10 = f32[640,256]{1,0:T(8,128)S(1)} fusion(bf16[640,7168]{1,0:T(8,128)(2,1)} %bitcast.54, bf16[1,7168,256]{2,1,0:T(8,128)(2,1)} %param.10), kind=kOutput, calls=%fused_computation.16 | convolution fusion | flops 2348810240 | bytes 13500416 | tf_op jit(solution)/shard_map/dot_general | solution.py:159
  421.1 18.9 %convolution_convert_fusion = bf16[640,7168]{1,0:T(8,128)(2,1)} fusion(bf16[1,256,7168]{2,1,0:T(8,128)(2,1)} %param.12, bf16[640,7168]{1,0:T(8,128)(2,1)} %bitcast.55, bf16[1,7168,256]{2,1,0:T(8,128)(2,1)} %param.11, f32[640,256]{1,0:T(8,128)S(1)} %fusion.10), kind=kOutput, calls=%fused_computation | convolution fusion | flops 4703191040 | bytes 26345472 | tf_op jit(solution)/shard_map/dot_general | solution.py:162
  440.0 8.1 %shard_map.79 = bf16[320,7168]{1,0:T(8,128)(2,1)} custom-call(bf16[2,320,7168]{2,1,0:T(8,128)(2,1)} %bitcast.48), custom_call_target="tpu_custom_call" | custom-call | tf_op jit(solution)/shard_map/pallas_call | solution.py:144
  448.1 7.6 %fusion = bf16[320,7168]{1,0:T(8,128)(2,1)} fusion(bf16[320,7168]{1,0:T(8,128)(2,1)} %shard_map.79, bf16[2,320,7168]{2,1,0:T(8,128)(2,1)} %bitcast.49, s32[]{:T(128)S(6)} %select_n.30), kind=kLoop, calls=%fused_computation.3 | loop fusion | flops 9175040 | bytes 13762564 | tf_op jit(solution)/shard_map/convert_element_type | solution.py:207
  455.8 2.7 reshape.56.x_ref
  458.4 20.4 %shard_map.76 = bf16[8,560,128]{2,1,0:T(8,128)(2,1)} custom-call(bf16[8,560,128]{2,1,0:T(8,128)(2,1)} %reshape.56.x_ref), custom_call_target="tpu_custom_call" | custom-call | tf_op jit(solution)/shard_map/pallas_call | solution.py:90
  478.9 27.4 %reduce-scatter.5.cloned.1.call-done = bf16[80,7168]{1,0:T(8,128)(2,1)} async-done(((bf16[320,7168]{1,0:T(8,128)(2,1)}), bf16[80,7168]{1,0:T(8,128)(2,1)}) %reduce-scatter.5.cloned.1.call-update) | async-done | bytes 1146896 | tf_op jit(solution)/shard_map/reduce_scatter | solution.py:210
  506.3 2.4 reshape.60.x_ref
  508.7 23.1 %shard_map.80 = bf16[8,560,128]{2,1,0:T(8,128)(2,1)} custom-call(bf16[8,560,128]{2,1,0:T(8,128)(2,1)} %reshape.60.x_ref), custom_call_target="tpu_custom_call" | custom-call | tf_op jit(solution)/shard_map/pallas_call | solution.py:90
  531.8 2.9 pad_maximum_fusion
  534.7 5.6 %reshape.61 = bf16[16,10,7168]{2,1,0:T(8,128)(2,1)} reshape(bf16[16,560,128]{2,1,0:T(8,128)(2,1)} %pad_maximum_fusion) | data formatting | bytes 4587520 | tf_op jit(solution)/shard_map/reshape | solution.py:216
  540.2 5.0 fusion.3
  (16 shorter events, 0.1 us)
Async XLA Ops:
  6.5 2.6 copy-start
  6.5 84.7 %all-gather.3.cloned.1.call-start = ((), (), s32[]{:S(2)}) async-start(), calls=%async_computation.2 | async-start | bytes 5734400 | tf_op jit(solution)/shard_map/all_gather | solution.py:201
  39.5 234.0 %all-gather.5.cloned.1.call-start = ((), (), s32[]{:S(2)}) async-start(), calls=%async_computation.4 | async-start | bytes 5734400 | tf_op jit(solution)/shard_map/all_gather | solution.py:201
  63.1 392.7 %reduce-scatter.3.cloned.1.call-start = ((), (), s32[]{:S(2)}) async-start(), calls=%async_computation.3 | async-start | bytes 5734400 | tf_op jit(solution)/shard_map/reduce_scatter | solution.py:210
  273.2 233.1 %reduce-scatter.5.cloned.1.call-start = ((), (), s32[]{:S(2)}) async-start(), calls=%async_computation.5 | async-start | bytes 5734400 | tf_op jit(solution)/shard_map/reduce_scatter | solution.py:210
  478.9 52.9 %copy-start.2 = (bf16[8,560,128]{2,1,0:T(8,128)(2,1)S(1)}, bf16[8,560,128]{2,1,0:T(8,128)(2,1)}, u32[]{:S(2)}) copy-start(bf16[8,560,128]{2,1,0:T(8,128)(2,1)} %shard_map.76) | copy-start | bytes 3440644
  534.7 5.6 %copy-start.3 = (f32[128]{0:T(128)S(1)}, f32[128]{0:T(128)}, u32[]{:S(2)}) copy-start(f32[128]{0:T(128)} %param.9) | copy-start | bytes 1540
  534.7 10.6 %copy-start.1 = (bf16[128,7168]{1,0:T(8,128)(2,1)S(1)}, bf16[128,7168]{1,0:T(8,128)(2,1)}, u32[]{:S(2)}) copy-start(bf16[128,7168]{1,0:T(8,128)(2,1)} %param.7) | copy-start | bytes 5505028
Sparse Core Ops, SparseCore 0:
  39.6 51.5 all-gather.2
  92.9 51.9 all-gather.4
  273.3 50.4 reduce-scatter.2
  455.8 50.3 reduce-scatter.4

commit v9 on v7

--- a/solution.py
+++ b/solution.py
@@ -99,6 +99,74 @@
         ],
         compiler_params=pltpu.CompilerParams(collective_id=collective_id, has_side_effects=True),
     )(x)
+
+
+def gather_kernel(chips, x_ref, y_ref, send_sem, recv_sem):
+    group = lax.axis_index("group")
+    inner = lax.axis_index("inner")
+    core = lax.rem(inner, 2)
+    chip = inner // 2
+    partner = inner + 1 - 2 * core
+    barrier = pltpu.get_barrier_semaphore()
+    others = [lax.rem(chip + d, chips) for d in range(1, chips)]
+    for other in others:
+        pl.semaphore_signal(
+            barrier, inc=1, device_id=(group, 2 * other + core), device_id_type=MESH
+        )
+    pl.semaphore_signal(barrier, inc=1, device_id=(group, partner), device_id_type=MESH)
+    pl.semaphore_wait(barrier, chips)
+
+    def copy_to(src, slot, device, index):
+        return pltpu.make_async_remote_copy(
+            src_ref=src,
+            dst_ref=y_ref.at[slot],
+            send_sem=send_sem.at[index],
+            recv_sem=recv_sem.at[slot],
+            device_id=(group, device),
+            device_id_type=MESH,
+        )
+
+    direct = []
+    for d, other in enumerate(others):
+        copy = copy_to(x_ref, inner, 2 * other + core, d)
+        copy.start()
+        direct.append(copy)
+    to_partner = copy_to(x_ref, inner, partner, chips - 1)
+    to_partner.start()
+    forwards = []
+    for d, other in enumerate(others):
+        slot = 2 * other + core
+        copy_to(x_ref, slot, 2 * other + core, d).wait_recv()
+        forward = copy_to(y_ref.at[slot], slot, partner, chips + d)
+        forward.start()
+        forwards.append(forward)
+    for copy in direct:
+        copy.wait_send()
+    to_partner.wait_send()
+    copy_to(x_ref, partner, partner, chips - 1).wait_recv()
+    for d, other in enumerate(others):
+        slot = 2 * other + 1 - core
+        copy_to(x_ref, slot, partner, chips + d).wait_recv()
+    for forward in forwards:
+        forward.wait_send()
+
+
+def inner_gather(x, collective_id):
+    inner_size = lax.axis_size("inner")
+    chips = inner_size // 2
+    out = pl.pallas_call(
+        functools.partial(gather_kernel, chips),
+        out_shape=jax.ShapeDtypeStruct((inner_size,) + x.shape, x.dtype),
+        in_specs=[pl.BlockSpec(memory_space=pl.ANY)],
+        out_specs=pl.BlockSpec(memory_space=pl.ANY),
+        scratch_shapes=[
+            pltpu.SemaphoreType.DMA((2 * chips,)),
+            pltpu.SemaphoreType.DMA((inner_size,)),
+        ],
+        compiler_params=pltpu.CompilerParams(collective_id=collective_id, has_side_effects=True),
+    )(x)
+    out = lax.dynamic_update_index_in_dim(out, x, lax.axis_index("inner"), axis=0)
+    return out.reshape((-1,) + x.shape[1:])
 
 
 def expert_part(rows_in, gate_mat, up_mat, down_mat):
@@ -141,7 +209,10 @@
         received = group_exchange(outbound, chunk, base, 1, 2 * index)
         base += len(chunk)
         rows = received.reshape(len(chunk) * capacity, model_width)
-        gathered = lax.all_gather(rows, "inner", axis=0, tiled=True)
+        if index == len(chunks) - 1 and lax.axis_size("inner") % 2 == 0:
+            gathered = inner_gather(rows, 8)
+        else:
+            gathered = lax.all_gather(rows, "inner", axis=0, tiled=True)
         partial_value = expert_part(gathered, gate_weight[0], up_weight[0], down_weight[0])
         summed = lax.psum_scatter(
             partial_value.astype(jnp.bfloat16), "inner", scatter_dimension=0, tiled=True

time: 310 us -> 331 us (1.068)
  Pallas kernels: 84.4 us -> 166 us
  waiting for transfers between devices: 125 us -> 63.6 us
    pallas_call x0 -> x1, Pallas kernels: none -> 81.1 us  [inner_gather(): pl.pallas_call(functools.partial(gather_kernel, chips), out_shape=jax.Sha...]
    all_gather x2 -> x1, waiting for transfers between devices: 57.3 us -> 0.02 us  [body(): gathered = lax.all_gather(rows, 'inner', axis=0, tiled=True)]
    reduce_scatter x2, waiting for transfers between devices: 68 us -> 63.5 us  [body(): lax.psum_scatter(partial_value.astype(jnp.bfloat16), 'inner', scatter_dim...]
  transfers between devices with their start and end apart: 4 -> 3, of which waited for: 4 -> 2; matrix products, arithmetic and copies ran while one was open for 19% -> 18% of each run, Pallas kernels for 13% -> 38%
where the time goes in v9:
time: 331 us
  Pallas kernels  166 us (50%)
  waiting for transfers between devices  63.6 us (19%)
  matrix products  60.2 us (18%)
  local copies, waits for them, and re-layouts  22.2 us (7%)
  between operations  13.2 us (4%)
  other arithmetic  5.41 us (2%)
    pallas_call x4, Pallas kernels, group_exchange(): pl.pallas_call(functools.partial(exchange_kernel, groups, tuple(offsets),...  84.4 us
    pallas_call x1, Pallas kernels, inner_gather(): pl.pallas_call(functools.partial(gather_kernel, chips), out_shape=jax.Sha...  81.1 us
    reduce_scatter x2, waiting for transfers between devices, body(): lax.psum_scatter(partial_value.astype(jnp.bfloat16), 'inner', scatter_dim...  63.5 us
    dot_general x2, matrix products, expert_part(): return jnp.dot(hidden, down_mat, preferred_element_type=jnp.float32)  38.8 us
    dot_general x2, matrix products, expert_part(): gate_pre = jnp.dot(rows_in, gate_mat, preferred_element_type=jnp.float32)  14.3 us
  transfers between devices with their start and end apart: 3, of which 2 were waited for; matrix products, arithmetic and copies ran while one was open for 18% of the time, Pallas kernels for 38%

profile of v9, /device:TPU:0, one launch (start us, length us, event | category | flops | bytes accessed | tf_op | source)
XLA Modules:
  0.0 330.5 jit_solution(3400357519436784166)
XLA Ops:
  6.5 0.9 fusion.42
  7.4 0.2 reduce_window_sum.11
  7.6 0.8 select_reduce_fusion
  8.4 0.7 compare_select_fusion.23
  9.1 2.1 convolution_convert_fusion.2
  11.3 4.4 %reshape.40.x_ref = bf16[16,560,128]{2,1,0:T(8,128)(2,1)} reshape(bf16[160,7168]{1,0:T(8,128)(2,1)} %convolution_convert_fusion.2) | data formatting | bytes 4587520 | tf_op jit(solution)/shard_map/reshape | solution.py:205
  15.6 21.5 %shard_map.73 = bf16[8,560,128]{2,1,0:T(8,128)(2,1)} custom-call(bf16[16,560,128]{2,1,0:T(8,128)(2,1)} %reshape.40.x_ref), custom_call_target="tpu_custom_call" | custom-call | tf_op jit(solution)/shard_map/pallas_call | solution.py:90
  37.1 2.4 reshape.41
  39.5 0.0 all-gather.2.cloned.1.call-update
  39.5 0.0 reduce-scatter.5.cloned.1.call-start
  39.6 21.1 %shard_map.75 = bf16[8,560,128]{2,1,0:T(8,128)(2,1)} custom-call(bf16[16,560,128]{2,1,0:T(8,128)(2,1)} %reshape.40.x_ref), custom_call_target="tpu_custom_call" | custom-call | tf_op jit(solution)/shard_map/pallas_call | solution.py:90
  60.7 1.6 broadcast_in_dim.19
  62.3 2.4 reshape.43.x_ref
  64.7 81.1 %shard_map.76 = bf16[8,80,7168]{2,1,0:T(8,128)(2,1)} custom-call(bf16[80,7168]{1,0:T(8,128)(2,1)} %reshape.43.x_ref), custom_call_target="tpu_custom_call" | custom-call | tf_op jit(solution)/shard_map/pallas_call | solution.py:157
  145.8 1.1 constant_dynamic-update-slice_fusion
  146.9 7.2 %fusion.8 = f32[640,256]{1,0:T(8,128)S(1)} fusion(bf16[640,7168]{1,0:T(8,128)(2,1)} %bitcast.39, bf16[1,7168,256]{2,1,0:T(8,128)(2,1)} %param.10), kind=kOutput, calls=%fused_computation.12 | convolution fusion | flops 2348810240 | bytes 13500416 | tf_op jit(solution)/shard_map/dot_general | solution.py:173
  154.0 18.9 %convolution_convert_fusion = bf16[640,7168]{1,0:T(8,128)(2,1)} fusion(bf16[1,256,7168]{2,1,0:T(8,128)(2,1)} %param.12, bf16[640,7168]{1,0:T(8,128)(2,1)} %bitcast.40, bf16[1,7168,256]{2,1,0:T(8,128)(2,1)} %param.11, f32[640,256]{1,0:T(8,128)S(1)} %fusion.8), kind=kOutput, calls=%fused_computation | convolution fusion | flops 4703191040 | bytes 26345472 | tf_op jit(solution)/shard_map/dot_general | solution.py:176
  173.0 0.0 reduce-scatter.5.cloned.1.call-update
  173.0 0.2 reduce-scatter.3.cloned.1.call-start
  173.2 0.0 all-gather.2.cloned.1.call-done
  173.3 7.2 %fusion.10 = f32[640,256]{1,0:T(8,128)S(1)} fusion(bf16[640,7168]{1,0:T(8,128)(2,1)} %all-gather.2.cloned.1.call-done, bf16[1,7168,256]{2,1,0:T(8,128)(2,1)} %param.10), kind=kOutput, calls=%fused_computation.14 | convolution fusion | flops 2348810240 | bytes 13500416 | tf_op jit(solution)/shard_map/dot_general | solution.py:173
  180.4 19.8 %convolution_convert_fusion.1 = bf16[640,7168]{1,0:T(8,128)(2,1)} fusion(bf16[1,256,7168]{2,1,0:T(8,128)(2,1)} %param.12, bf16[640,7168]{1,0:T(8,128)(2,1)} %all-gather.2.cloned.1.call-done, bf16[1,7168,256]{2,1,0:T(8,128)(2,1)} %param.11, f32[640,256]{1,0:T(8,128)S(1)} %fusion.10), kind=kOutput, calls=%fused_computation.1 | convolution fusion | flops 4703191040 | bytes 26345472 | tf_op jit(solution)/shard_map/dot_general | solution.py:176
  200.3 0.0 reduce-scatter.3.cloned.1.call-update
  200.3 30.0 %reduce-scatter.5.cloned.1.call-done = bf16[80,7168]{1,0:T(8,128)(2,1)} async-done(((bf16[640,7168]{1,0:T(8,128)(2,1)}), bf16[80,7168]{1,0:T(8,128)(2,1)}) %reduce-scatter.5.cloned.1.call-update) | async-done | bytes 1146896 | tf_op jit(solution)/shard_map/reduce_scatter | solution.py:217
  230.3 2.4 reshape.45.x_ref
  232.7 22.3 %shard_map.77 = bf16[8,560,128]{2,1,0:T(8,128)(2,1)} custom-call(bf16[8,560,128]{2,1,0:T(8,128)(2,1)} %reshape.45.x_ref), custom_call_target="tpu_custom_call" | custom-call | tf_op jit(solution)/shard_map/pallas_call | solution.py:90
  255.1 33.5 %reduce-scatter.3.cloned.1.call-done = bf16[80,7168]{1,0:T(8,128)(2,1)} async-done(((bf16[640,7168]{1,0:T(8,128)(2,1)}), bf16[80,7168]{1,0:T(8,128)(2,1)}) %reduce-scatter.3.cloned.1.call-update) | async-done | bytes 1146896 | tf_op jit(solution)/shard_map/reduce_scatter | solution.py:217
  288.5 2.4 reshape.42.x_ref
  291.0 19.6 %shard_map.74 = bf16[8,560,128]{2,1,0:T(8,128)(2,1)} custom-call(bf16[8,560,128]{2,1,0:T(8,128)(2,1)} %reshape.42.x_ref), custom_call_target="tpu_custom_call" | custom-call | tf_op jit(solution)/shard_map/pallas_call | solution.py:90
  310.5 2.9 pad_maximum_fusion
  313.4 5.6 %reshape.46 = bf16[16,10,7168]{2,1,0:T(8,128)(2,1)} reshape(bf16[16,560,128]{2,1,0:T(8,128)(2,1)} %pad_maximum_fusion) | data formatting | bytes 4587520 | tf_op jit(solution)/shard_map/reshape | solution.py:223
  319.0 5.0 %fusion.1 = bf16[128,7168]{1,0:T(8,128)(2,1)} fusion(bf16[16,10,7168]{2,1,0:T(8,128)(2,1)} %reshape.46, f32[128]{0:T(128)S(1)} %copy-done.3, s32[16,10]{0,1:T(8,128)S(1)} %multiply_add_fusion, s32[128]{0:T(128)S(1)} %compare_select_fusion.23), kind=kOutput, calls=%fused_computation.5 | convolution fusion | flops 295456768 | bytes 4130432 | tf_op jit(solution)/shard_map/gct,gcd->td/dot_general | solution.py:224
  (10 shorter events, 0.0 us)
Async XLA Ops:
  6.5 2.6 copy-start
  6.5 166.7 %all-gather.2.cloned.1.call-start = ((), (), s32[]{:S(2)}) async-start(), calls=%async_computation.2 | async-start | bytes 10321920 | tf_op jit(solution)/shard_map/all_gather | solution.py:215
  39.5 190.8 %reduce-scatter.5.cloned.1.call-start = ((), (), s32[]{:S(2)}) async-start(), calls=%async_computation.4 | async-start | bytes 10321920 | tf_op jit(solution)/shard_map/reduce_scatter | solution.py:217
  173.0 115.5 %reduce-scatter.3.cloned.1.call-start = ((), (), s32[]{:S(2)}) async-start(), calls=%async_computation.3 | async-start | bytes 10321920 | tf_op jit(solution)/shard_map/reduce_scatter | solution.py:217
  255.0 55.5 %copy-start.2 = (bf16[8,560,128]{2,1,0:T(8,128)(2,1)S(1)}, bf16[8,560,128]{2,1,0:T(8,128)(2,1)}, u32[]{:S(2)}) copy-start(bf16[8,560,128]{2,1,0:T(8,128)(2,1)} %shard_map.77) | copy-start | bytes 3440644
  313.4 5.6 %copy-start.3 = (f32[128]{0:T(128)S(1)}, f32[128]{0:T(128)}, u32[]{:S(2)}) copy-start(f32[128]{0:T(128)} %param.9) | copy-start | bytes 1540
  313.4 10.6 %copy-start.1 = (bf16[128,7168]{1,0:T(8,128)(2,1)S(1)}, bf16[128,7168]{1,0:T(8,128)(2,1)}, u32[]{:S(2)}) copy-start(bf16[128,7168]{1,0:T(8,128)(2,1)} %param.7) | copy-start | bytes 5505028
Sparse Core Ops, SparseCore 0:
  39.6 95.1 all-gather.1
  173.1 57.1 reduce-scatter.4
  232.8 55.7 reduce-scatter.2

commit v10 on v7

--- a/solution.py
+++ b/solution.py
@@ -134,11 +134,11 @@
     outbound = jnp.dot(dispatch, tokens, preferred_element_type=jnp.float32).astype(jnp.bfloat16)
     lanes = 128 if (capacity * model_width) % 128 == 0 else model_width
     slab = (capacity * model_width // lanes, lanes)
-    outbound = outbound.reshape((groups,) + slab)
     returned = []
     base = 0
     for index, chunk in enumerate(chunks):
-        received = group_exchange(outbound, chunk, base, 1, 2 * index)
+        piece = outbound[base * capacity : (base + len(chunk)) * capacity]
+        received = group_exchange(piece.reshape((len(chunk),) + slab), chunk, 0, 1, 2 * index)
         base += len(chunk)
         rows = received.reshape(len(chunk) * capacity, model_width)
         gathered = lax.all_gather(rows, "inner", axis=0, tiled=True)
@@ -147,15 +147,20 @@
             partial_value.astype(jnp.bfloat16), "inner", scatter_dimension=0, tiled=True
         )
         returned.append((summed.reshape((len(chunk),) + slab), chunk, index))
-    back = [group_exchange(z, chunk, 0, -1, 2 * index + 1) for z, chunk, index in returned]
-    back_rows = jnp.concatenate(back, axis=0) if len(back) > 1 else back[0]
-    back_rows = back_rows.reshape(groups, capacity, model_width)
-    expert_out = jnp.einsum(
-        "gct,gcd->td",
-        dispatch.reshape(groups, capacity, tok_count),
-        back_rows,
-        preferred_element_type=jnp.float32,
-    )
+    expert_out = None
+    base = 0
+    for z, chunk, index in returned:
+        back_rows = group_exchange(z, chunk, 0, -1, 2 * index + 1)
+        term = jnp.einsum(
+            "gct,gcd->td",
+            dispatch[base * capacity : (base + len(chunk)) * capacity].reshape(
+                len(chunk), capacity, tok_count
+            ),
+            back_rows.reshape(len(chunk), capacity, model_width),
+            preferred_element_type=jnp.float32,
+        )
+        base += len(chunk)
+        expert_out = term if expert_out is None else expert_out + term
     return (gate_scale[:, None] * expert_out).astype(jnp.bfloat16)
 
 

time: 310 us -> 300 us (0.968)
  waiting for transfers between devices: 125 us -> 120 us
    reduce_scatter x2, waiting for transfers between devices: 68 us -> 64.4 us  [body(): lax.psum_scatter(partial_value.astype(jnp.bfloat16), 'inner', scatter_dim...]
    reshape x2 -> x6, local copies, waits for them, and re-layouts: 9.88 us -> 9.62 us  [the longest x2 6.85 us: body(): back_rows.reshape(len(chunk), capacity, model_width)]
  transfers between devices with their start and end apart: 4 -> 4, of which waited for: 4 -> 4; matrix products, arithmetic and copies ran while one was open for 19% -> 21% of each run, Pallas kernels for 13% -> 14%
where the time goes in v10:
time: 300 us; the launch traced here: 299 us
  waiting for transfers between devices  120 us (40%)
  Pallas kernels  84.4 us (28%)
  matrix products  58.9 us (20%)
  local copies, waits for them, and re-layouts  19.4 us (6%)
  between operations  13.3 us (4%)
    pallas_call x4, Pallas kernels, group_exchange(): pl.pallas_call(functools.partial(exchange_kernel, groups, tuple(offsets),...  84.4 us
    reduce_scatter x2, waiting for transfers between devices, body(): lax.psum_scatter(partial_value.astype(jnp.bfloat16), 'inner', scatter_dim...  64.4 us
    all_gather x2, waiting for transfers between devices, body(): gathered = lax.all_gather(rows, 'inner', axis=0, tiled=True)  55.8 us
    dot_general x2, matrix products, expert_part(): return jnp.dot(hidden, down_mat, preferred_element_type=jnp.float32)  39.6 us
    dot_general x2, matrix products, expert_part(): gate_pre = jnp.dot(rows_in, gate_mat, preferred_element_type=jnp.float32)  14.3 us
    reshape x2, local copies, waits for them, and re-layouts, body(): back_rows.reshape(len(chunk), capacity, model_width)  6.85 us
  transfers between devices with their start and end apart: 4, of which 4 were waited for; matrix products, arithmetic and copies ran while one was open for 21% of the time, Pallas kernels for 14%

profile of v10, /device:TPU:0, one launch (start us, length us, event | category | flops | bytes accessed | tf_op | source)
XLA Modules:
  0.0 299.3 jit_solution(2413167258932084580)
XLA Ops:
  6.5 0.9 fusion.41
  7.4 0.2 reduce_window_sum.11
  7.6 0.8 select_reduce_fusion
  8.4 0.7 compare_select_fusion.23
  9.1 0.7 convolution_convert_fusion.2
  9.9 0.2 fusion.50
  10.0 1.4 reshape.34.x_ref
  11.4 21.5 %shard_map.73 = bf16[8,560,128]{2,1,0:T(8,128)(2,1)} custom-call(bf16[8,560,128]{2,1,0:T(8,128)(2,1)} %reshape.34.x_ref), custom_call_target="tpu_custom_call" | custom-call | tf_op jit(solution)/shard_map/pallas_call | solution.py:90
  32.9 2.4 reshape.35
  35.3 0.0 all-gather.5.cloned.1.call-start
  35.4 1.4 reshape.39.x_ref
  36.7 21.0 %shard_map.75 = bf16[8,560,128]{2,1,0:T(8,128)(2,1)} custom-call(bf16[8,560,128]{2,1,0:T(8,128)(2,1)} %reshape.39.x_ref), custom_call_target="tpu_custom_call" | custom-call | tf_op jit(solution)/shard_map/pallas_call | solution.py:90
  57.8 2.4 reshape.40
  60.2 0.0 all-gather.5.cloned.1.call-update
  60.2 0.2 reduce-scatter.3.cloned.1.call-start
  60.4 28.1 %all-gather.3.cloned.1.call-done = bf16[640,7168]{1,0:T(8,128)(2,1)} async-done(((bf16[80,7168]{1,0:T(8,128)(2,1)}), bf16[640,7168]{1,0:T(8,128)(2,1)}) %all-gather.3.cloned.1.call-update) | async-done | bytes 9175056 | tf_op jit(solution)/shard_map/all_gather | solution.py:144
  88.5 7.2 %fusion.11 = f32[640,256]{1,0:T(8,128)S(1)} fusion(bf16[640,7168]{1,0:T(8,128)(2,1)} %all-gather.3.cloned.1.call-done, bf16[1,7168,256]{2,1,0:T(8,128)(2,1)} %param.10), kind=kOutput, calls=%fused_computation.16 | convolution fusion | flops 2348810240 | bytes 13500416 | tf_op jit(solution)/shard_map/dot_general | solution.py:105
  95.7 19.8 %convolution_convert_fusion.1 = bf16[640,7168]{1,0:T(8,128)(2,1)} fusion(bf16[1,256,7168]{2,1,0:T(8,128)(2,1)} %param.12, bf16[640,7168]{1,0:T(8,128)(2,1)} %all-gather.3.cloned.1.call-done, bf16[1,7168,256]{2,1,0:T(8,128)(2,1)} %param.11, f32[640,256]{1,0:T(8,128)S(1)} %fusion.11), kind=kOutput, calls=%fused_computation.1 | convolution fusion | flops 4703191040 | bytes 26345472 | tf_op jit(solution)/shard_map/dot_general | solution.py:108
  115.6 0.3 reduce-scatter.5.cloned.1.call-start
  115.8 27.6 %all-gather.5.cloned.1.call-done = bf16[640,7168]{1,0:T(8,128)(2,1)} async-done(((bf16[80,7168]{1,0:T(8,128)(2,1)}), bf16[640,7168]{1,0:T(8,128)(2,1)}) %all-gather.5.cloned.1.call-update) | async-done | bytes 9175056 | tf_op jit(solution)/shard_map/all_gather | solution.py:144
  143.5 7.2 %fusion.9 = f32[640,256]{1,0:T(8,128)S(1)} fusion(bf16[640,7168]{1,0:T(8,128)(2,1)} %all-gather.5.cloned.1.call-done, bf16[1,7168,256]{2,1,0:T(8,128)(2,1)} %param.10), kind=kOutput, calls=%fused_computation.14 | convolution fusion | flops 2348810240 | bytes 13500416 | tf_op jit(solution)/shard_map/dot_general | solution.py:105
  150.7 19.8 %convolution_convert_fusion = bf16[640,7168]{1,0:T(8,128)(2,1)} fusion(bf16[1,256,7168]{2,1,0:T(8,128)(2,1)} %param.12, bf16[640,7168]{1,0:T(8,128)(2,1)} %all-gather.5.cloned.1.call-done, bf16[1,7168,256]{2,1,0:T(8,128)(2,1)} %param.11, f32[640,256]{1,0:T(8,128)S(1)} %fusion.9), kind=kOutput, calls=%fused_computation | convolution fusion | flops 4703191040 | bytes 26345472 | tf_op jit(solution)/shard_map/dot_general | solution.py:108
  170.5 31.8 %reduce-scatter.3.cloned.1.call-done = bf16[80,7168]{1,0:T(8,128)(2,1)} async-done(((bf16[640,7168]{1,0:T(8,128)(2,1)}), bf16[80,7168]{1,0:T(8,128)(2,1)}) %reduce-scatter.3.cloned.1.call-update) | async-done | bytes 1146896 | tf_op jit(solution)/shard_map/reduce_scatter | solution.py:146
  202.3 2.4 reshape.36.x_ref
  204.7 19.5 %shard_map.74 = bf16[8,560,128]{2,1,0:T(8,128)(2,1)} custom-call(bf16[8,560,128]{2,1,0:T(8,128)(2,1)} %reshape.36.x_ref), custom_call_target="tpu_custom_call" | custom-call | tf_op jit(solution)/shard_map/pallas_call | solution.py:90
  224.3 3.5 %reshape.37 = bf16[8,10,7168]{2,1,0:T(8,128)(2,1)} reshape(bf16[8,560,128]{2,1,0:T(8,128)(2,1)} %shard_map.74) | data formatting | bytes 2293760 | tf_op jit(solution)/shard_map/reshape | solution.py:159
  227.7 32.6 %reduce-scatter.5.cloned.1.call-done = bf16[80,7168]{1,0:T(8,128)(2,1)} async-done(((bf16[640,7168]{1,0:T(8,128)(2,1)}), bf16[80,7168]{1,0:T(8,128)(2,1)}) %reduce-scatter.5.cloned.1.call-update) | async-done | bytes 1146896 | tf_op jit(solution)/shard_map/reduce_scatter | solution.py:146
  260.4 2.4 reshape.41.x_ref
  262.8 22.3 %shard_map.76 = bf16[8,560,128]{2,1,0:T(8,128)(2,1)} custom-call(bf16[8,560,128]{2,1,0:T(8,128)(2,1)} %reshape.41.x_ref), custom_call_target="tpu_custom_call" | custom-call | tf_op jit(solution)/shard_map/pallas_call | solution.py:90
  285.1 3.4 %reshape.42 = bf16[8,10,7168]{2,1,0:T(8,128)(2,1)} reshape(bf16[8,560,128]{2,1,0:T(8,128)(2,1)} %shard_map.76) | data formatting | bytes 2293760 | tf_op jit(solution)/shard_map/reshape | solution.py:159
  288.5 2.3 convolution_bitcast_fusion
  290.9 1.9 fusion.2
  (16 shorter events, 0.1 us)
Async XLA Ops:
  6.5 2.6 copy-start
  6.5 82.0 %all-gather.3.cloned.1.call-start = ((), (), s32[]{:S(2)}) async-start(), calls=%async_computation.2 | async-start | bytes 10321920 | tf_op jit(solution)/shard_map/all_gather | solution.py:144
  35.3 108.2 %all-gather.5.cloned.1.call-start = ((), (), s32[]{:S(2)}) async-start(), calls=%async_computation.4 | async-start | bytes 10321920 | tf_op jit(solution)/shard_map/all_gather | solution.py:144
  60.2 142.1 %reduce-scatter.3.cloned.1.call-start = ((), (), s32[]{:S(2)}) async-start(), calls=%async_computation.3 | async-start | bytes 10321920 | tf_op jit(solution)/shard_map/reduce_scatter | solution.py:146
  115.6 144.8 %reduce-scatter.5.cloned.1.call-start = ((), (), s32[]{:S(2)}) async-start(), calls=%async_computation.5 | async-start | bytes 10321920 | tf_op jit(solution)/shard_map/reduce_scatter | solution.py:146
  285.1 5.7 %copy-start.3 = (f32[128]{0:T(128)S(1)}, f32[128]{0:T(128)}, u32[]{:S(2)}) copy-start(f32[128]{0:T(128)} %param.9) | copy-start | bytes 1540
  288.5 2.4 copy-start.2
  288.5 4.3 %copy-start.1 = (bf16[128,7168]{1,0:T(8,128)(2,1)S(1)}, bf16[128,7168]{1,0:T(8,128)(2,1)}, u32[]{:S(2)}) copy-start(bf16[128,7168]{1,0:T(8,128)(2,1)} %param.7) | copy-start | bytes 5505028
Sparse Core Ops, SparseCore 0:
  35.4 53.0 all-gather.2
  90.2 53.2 all-gather.4
  145.9 56.3 reduce-scatter.2
  204.6 55.7 reduce-scatter.4

commit v11 on v10

--- a/solution.py
+++ b/solution.py
@@ -101,6 +101,38 @@
     )(x)
 
 
+def swap_kernel(x_ref, y_ref, send_sem, recv_sem):
+    group = lax.axis_index("group")
+    inner = lax.axis_index("inner")
+    core = lax.rem(inner, 2)
+    partner = inner + 1 - 2 * core
+    barrier = pltpu.get_barrier_semaphore()
+    pl.semaphore_signal(barrier, inc=1, device_id=(group, partner), device_id_type=MESH)
+    pl.semaphore_wait(barrier, 1)
+    copy = pltpu.make_async_remote_copy(
+        src_ref=x_ref.at[:, 1 - core],
+        dst_ref=y_ref,
+        send_sem=send_sem,
+        recv_sem=recv_sem,
+        device_id=(group, partner),
+        device_id_type=MESH,
+    )
+    copy.start()
+    copy.wait_send()
+    copy.wait_recv()
+
+
+def partner_swap(x, collective_id):
+    return pl.pallas_call(
+        swap_kernel,
+        out_shape=jax.ShapeDtypeStruct(x.shape[:1] + x.shape[2:], x.dtype),
+        in_specs=[pl.BlockSpec(memory_space=pl.ANY)],
+        out_specs=pl.BlockSpec(memory_space=pl.ANY),
+        scratch_shapes=[pltpu.SemaphoreType.DMA, pltpu.SemaphoreType.DMA],
+        compiler_params=pltpu.CompilerParams(collective_id=collective_id, has_side_effects=True),
+    )(x)
+
+
 def expert_part(rows_in, gate_mat, up_mat, down_mat):
     gate_pre = jnp.dot(rows_in, gate_mat, preferred_element_type=jnp.float32)
     up_pre = jnp.dot(rows_in, up_mat, preferred_element_type=jnp.float32)
@@ -143,9 +175,25 @@
         rows = received.reshape(len(chunk) * capacity, model_width)
         gathered = lax.all_gather(rows, "inner", axis=0, tiled=True)
         partial_value = expert_part(gathered, gate_weight[0], up_weight[0], down_weight[0])
-        summed = lax.psum_scatter(
-            partial_value.astype(jnp.bfloat16), "inner", scatter_dimension=0, tiled=True
-        )
+        inner_size = lax.axis_size("inner")
+        if inner_size % 2 == 0:
+            same_core = [list(range(c, inner_size, 2)) for c in range(2)]
+            core = lax.rem(lax.axis_index("inner"), 2)
+            by_core = partial_value.astype(jnp.bfloat16).reshape(inner_size // 2, 2, -1, model_width)
+            received_sum = partner_swap(by_core, 8 + index)
+            own_part = lax.dynamic_index_in_dim(by_core, core, axis=1, keepdims=False)
+            pair_sum = own_part.astype(jnp.float32) + received_sum.astype(jnp.float32)
+            summed = lax.psum_scatter(
+                pair_sum.astype(jnp.bfloat16).reshape(-1, model_width),
+                "inner",
+                scatter_dimension=0,
+                tiled=True,
+                axis_index_groups=same_core,
+            )
+        else:
+            summed = lax.psum_scatter(
+                partial_value.astype(jnp.bfloat16), "inner", scatter_dimension=0, tiled=True
+            )
         returned.append((summed.reshape((len(chunk),) + slab), chunk, index))
     expert_out = None
     base = 0

time: 300 us -> 288 us (0.960)
  waiting for transfers between devices: 120 us -> 76 us
  Pallas kernels: 84.4 us -> 102 us
  other arithmetic: 2.57 us -> 17.9 us
    reduce_scatter x2, waiting for transfers between devices: 64.4 us -> 36 us  [body(): lax.psum_scatter(pair_sum.astype(jnp.bfloat16).reshape(-1, model_width),...]
    pallas_call x0 -> x2, Pallas kernels: none -> 16.2 us  [partner_swap(): pl.pallas_call(swap_kernel, out_shape=jax.ShapeDtypeStruct(x.shape[:1] +...]
    all_gather x2, waiting for transfers between devices: 55.8 us -> 40 us  [body(): gathered = lax.all_gather(rows, 'inner', axis=0, tiled=True)]
    convert_element_type x0 -> x2, other arithmetic: none -> 15.3 us  [body(): pair_sum.astype(jnp.bfloat16).reshape(-1, model_width)]
  transfers between devices with their start and end apart: 4 -> 4, of which waited for: 4 -> 4; matrix products, arithmetic and copies ran while one was open for 21% -> 27% of each run, Pallas kernels for 14% -> 20%
where the time goes in v11:
time: 288 us
  Pallas kernels  102 us (35%)
  waiting for transfers between devices  76 us (26%)
  matrix products  59 us (20%)
  local copies, waits for them, and re-layouts  19.3 us (7%)
  other arithmetic  17.9 us (6%)
  between operations  13.3 us (5%)
    pallas_call x4, Pallas kernels, group_exchange(): pl.pallas_call(functools.partial(exchange_kernel, groups, tuple(offsets),...  85.8 us
    all_gather x2, waiting for transfers between devices, body(): gathered = lax.all_gather(rows, 'inner', axis=0, tiled=True)  40 us
    dot_general x2, matrix products, expert_part(): return jnp.dot(hidden, down_mat, preferred_element_type=jnp.float32)  39.6 us
    reduce_scatter x2, waiting for transfers between devices, body(): lax.psum_scatter(pair_sum.astype(jnp.bfloat16).reshape(-1, model_width),...  36 us
    pallas_call x2, Pallas kernels, partner_swap(): pl.pallas_call(swap_kernel, out_shape=jax.ShapeDtypeStruct(x.shape[:1] +...  16.2 us
    convert_element_type x2, other arithmetic, body(): pair_sum.astype(jnp.bfloat16).reshape(-1, model_width)  15.3 us
    dot_general x2, matrix products, expert_part(): gate_pre = jnp.dot(rows_in, gate_mat, preferred_element_type=jnp.float32)  14.3 us
    reshape x2, local copies, waits for them, and re-layouts, body(): back_rows.reshape(len(chunk), capacity, model_width)  6.81 us
  transfers between devices with their start and end apart: 4, of which 4 were waited for; matrix products, arithmetic and copies ran while one was open for 27% of the time, Pallas kernels for 20%

profile of v11, /device:TPU:0, one launch (start us, length us, event | category | flops | bytes accessed | tf_op | source)
XLA Modules:
  0.0 288.0 jit_solution(2105986193962966392)
XLA Ops:
  6.5 0.9 fusion.43
  7.6 0.8 select_reduce_fusion
  8.4 0.7 compare_select_fusion.23
  9.1 0.7 convolution_convert_fusion.2
  10.0 1.4 reshape.50.x_ref
  11.4 21.5 %shard_map.73 = bf16[8,560,128]{2,1,0:T(8,128)(2,1)} custom-call(bf16[8,560,128]{2,1,0:T(8,128)(2,1)} %reshape.50.x_ref), custom_call_target="tpu_custom_call" | custom-call | tf_op jit(solution)/shard_map/pallas_call | solution.py:90
  32.9 2.4 reshape.51
  35.4 1.4 reshape.57.x_ref
  36.7 21.0 %shard_map.76 = bf16[8,560,128]{2,1,0:T(8,128)(2,1)} custom-call(bf16[8,560,128]{2,1,0:T(8,128)(2,1)} %reshape.57.x_ref), custom_call_target="tpu_custom_call" | custom-call | tf_op jit(solution)/shard_map/pallas_call | solution.py:90
  57.8 2.4 reshape.58
  60.2 0.2 reduce-scatter.3.cloned.1.call-start
  60.4 28.1 %all-gather.3.cloned.1.call-done = bf16[640,7168]{1,0:T(8,128)(2,1)} async-done(((bf16[80,7168]{1,0:T(8,128)(2,1)}), bf16[640,7168]{1,0:T(8,128)(2,1)}) %all-gather.3.cloned.1.call-update) | async-done | bytes 9175056 | tf_op jit(solution)/shard_map/all_gather | solution.py:176
  88.5 7.2 %fusion.13 = f32[640,256]{1,0:T(8,128)S(1)} fusion(bf16[640,7168]{1,0:T(8,128)(2,1)} %all-gather.3.cloned.1.call-done, bf16[1,7168,256]{2,1,0:T(8,128)(2,1)} %param.10), kind=kOutput, calls=%fused_computation.20 | convolution fusion | flops 2348810240 | bytes 13500416 | tf_op jit(solution)/shard_map/dot_general | solution.py:137
  95.7 19.8 %convolution_convert_fusion.1 = bf16[640,7168]{1,0:T(8,128)(2,1)} fusion(bf16[1,256,7168]{2,1,0:T(8,128)(2,1)} %param.12, bf16[640,7168]{1,0:T(8,128)(2,1)} %all-gather.3.cloned.1.call-done, bf16[1,7168,256]{2,1,0:T(8,128)(2,1)} %param.11, f32[640,256]{1,0:T(8,128)S(1)} %fusion.13), kind=kOutput, calls=%fused_computation.1 | convolution fusion | flops 4703191040 | bytes 26345472 | tf_op jit(solution)/shard_map/dot_general | solution.py:140
  115.5 8.1 %shard_map.74 = bf16[4,80,7168]{2,1,0:T(8,128)(2,1)} custom-call(bf16[4,2,80,7168]{3,2,1,0:T(8,128)(2,1)} %bitcast.58), custom_call_target="tpu_custom_call" | custom-call | tf_op jit(solution)/shard_map/pallas_call | solution.py:126
  123.6 7.7 %fusion.1 = bf16[4,80,7168]{2,1,0:T(8,128)(2,1)} fusion(bf16[4,80,7168]{2,1,0:T(8,128)(2,1)} %shard_map.74, bf16[4,2,80,7168]{3,2,1,0:T(8,128)(2,1)} %bitcast.59, s32[]{:T(128)S(6)} %select_n.30), kind=kLoop, calls=%fused_computation.5 | loop fusion | flops 9175040 | bytes 13762564 | tf_op jit(solution)/shard_map/convert_element_type | solution.py:187
  131.4 0.3 reduce-scatter.5.cloned.1.call-start
  131.6 11.8 %all-gather.5.cloned.1.call-done = bf16[640,7168]{1,0:T(8,128)(2,1)} async-done(((bf16[80,7168]{1,0:T(8,128)(2,1)}), bf16[640,7168]{1,0:T(8,128)(2,1)}) %all-gather.5.cloned.1.call-update) | async-done | bytes 9175056 | tf_op jit(solution)/shard_map/all_gather | solution.py:176
  143.5 7.2 %fusion.11 = f32[640,256]{1,0:T(8,128)S(1)} fusion(bf16[640,7168]{1,0:T(8,128)(2,1)} %all-gather.5.cloned.1.call-done, bf16[1,7168,256]{2,1,0:T(8,128)(2,1)} %param.10), kind=kOutput, calls=%fused_computation.18 | convolution fusion | flops 2348810240 | bytes 13500416 | tf_op jit(solution)/shard_map/dot_general | solution.py:137
  150.7 19.8 %convolution_convert_fusion = bf16[640,7168]{1,0:T(8,128)(2,1)} fusion(bf16[1,256,7168]{2,1,0:T(8,128)(2,1)} %param.12, bf16[640,7168]{1,0:T(8,128)(2,1)} %all-gather.5.cloned.1.call-done, bf16[1,7168,256]{2,1,0:T(8,128)(2,1)} %param.11, f32[640,256]{1,0:T(8,128)S(1)} %fusion.11), kind=kOutput, calls=%fused_computation | convolution fusion | flops 4703191040 | bytes 26345472 | tf_op jit(solution)/shard_map/dot_general | solution.py:140
  170.4 8.1 %shard_map.77 = bf16[4,80,7168]{2,1,0:T(8,128)(2,1)} custom-call(bf16[4,2,80,7168]{3,2,1,0:T(8,128)(2,1)} %bitcast.56), custom_call_target="tpu_custom_call" | custom-call | tf_op jit(solution)/shard_map/pallas_call | solution.py:126
  178.5 7.6 %fusion = bf16[4,80,7168]{2,1,0:T(8,128)(2,1)} fusion(bf16[4,80,7168]{2,1,0:T(8,128)(2,1)} %shard_map.77, bf16[4,2,80,7168]{3,2,1,0:T(8,128)(2,1)} %bitcast.57, s32[]{:T(128)S(6)} %select_n.30), kind=kLoop, calls=%fused_computation.3 | loop fusion | flops 9175040 | bytes 13762564 | tf_op jit(solution)/shard_map/convert_element_type | solution.py:187
  186.2 10.0 %reduce-scatter.3.cloned.1.call-done = bf16[80,7168]{1,0:T(8,128)(2,1)} async-done(((bf16[320,7168]{1,0:T(8,128)(2,1)}), bf16[80,7168]{1,0:T(8,128)(2,1)}) %reduce-scatter.3.cloned.1.call-update) | async-done | bytes 1146896 | tf_op jit(solution)/shard_map/reduce_scatter | solution.py:186
  196.2 2.4 reshape.54.x_ref
  198.6 20.2 %shard_map.75 = bf16[8,560,128]{2,1,0:T(8,128)(2,1)} custom-call(bf16[8,560,128]{2,1,0:T(8,128)(2,1)} %reshape.54.x_ref), custom_call_target="tpu_custom_call" | custom-call | tf_op jit(solution)/shard_map/pallas_call | solution.py:90
  218.8 3.4 %reshape.55 = bf16[8,10,7168]{2,1,0:T(8,128)(2,1)} reshape(bf16[8,560,128]{2,1,0:T(8,128)(2,1)} %shard_map.75) | data formatting | bytes 2293760 | tf_op jit(solution)/shard_map/reshape | solution.py:207
  222.2 26.0 %reduce-scatter.5.cloned.1.call-done = bf16[80,7168]{1,0:T(8,128)(2,1)} async-done(((bf16[320,7168]{1,0:T(8,128)(2,1)}), bf16[80,7168]{1,0:T(8,128)(2,1)}) %reduce-scatter.5.cloned.1.call-update) | async-done | bytes 1146896 | tf_op jit(solution)/shard_map/reduce_scatter | solution.py:186
  248.2 2.4 reshape.61.x_ref
  250.6 23.1 %shard_map.78 = bf16[8,560,128]{2,1,0:T(8,128)(2,1)} custom-call(bf16[8,560,128]{2,1,0:T(8,128)(2,1)} %reshape.61.x_ref), custom_call_target="tpu_custom_call" | custom-call | tf_op jit(solution)/shard_map/pallas_call | solution.py:90
  273.8 3.4 %reshape.62 = bf16[8,10,7168]{2,1,0:T(8,128)(2,1)} reshape(bf16[8,560,128]{2,1,0:T(8,128)(2,1)} %shard_map.78) | data formatting | bytes 2293760 | tf_op jit(solution)/shard_map/reshape | solution.py:207
  277.2 2.3 convolution_bitcast_fusion
  279.5 1.9 fusion.4
  (20 shorter events, 0.5 us)
Async XLA Ops:
  6.5 2.6 copy-start
  6.5 82.0 %all-gather.3.cloned.1.call-start = ((), (), s32[]{:S(2)}) async-start(), calls=%async_computation.2 | async-start | bytes 10321920 | tf_op jit(solution)/shard_map/all_gather | solution.py:176
  35.3 108.2 %all-gather.5.cloned.1.call-start = ((), (), s32[]{:S(2)}) async-start(), calls=%async_computation.4 | async-start | bytes 10321920 | tf_op jit(solution)/shard_map/all_gather | solution.py:176
  60.2 136.0 %reduce-scatter.3.cloned.1.call-start = ((), (), s32[]{:S(2)}) async-start(), calls=%async_computation.3 | async-start | bytes 5734400 | tf_op jit(solution)/shard_map/reduce_scatter | solution.py:186
  131.4 116.8 %reduce-scatter.5.cloned.1.call-start = ((), (), s32[]{:S(2)}) async-start(), calls=%async_computation.5 | async-start | bytes 5734400 | tf_op jit(solution)/shard_map/reduce_scatter | solution.py:186
  273.8 5.7 %copy-start.3 = (f32[128]{0:T(128)S(1)}, f32[128]{0:T(128)}, u32[]{:S(2)}) copy-start(f32[128]{0:T(128)} %param.9) | copy-start | bytes 1540
  277.2 2.4 copy-start.2
  277.2 4.3 %copy-start.1 = (bf16[128,7168]{1,0:T(8,128)(2,1)S(1)}, bf16[128,7168]{1,0:T(8,128)(2,1)}, u32[]{:S(2)}) copy-start(bf16[128,7168]{1,0:T(8,128)(2,1)} %param.7) | copy-start | bytes 5505028
Sparse Core Ops, SparseCore 0:
  35.4 53.0 all-gather.2
  90.2 53.2 all-gather.4
  145.9 50.2 reduce-scatter.2
  198.4 49.7 reduce-scatter.4

commit v12 on v11

--- a/solution.py
+++ b/solution.py
@@ -168,18 +168,34 @@
     slab = (capacity * model_width // lanes, lanes)
     returned = []
     base = 0
+    inner_size = lax.axis_size("inner")
+    weights = (gate_weight[0], up_weight[0], down_weight[0])
     for index, chunk in enumerate(chunks):
-        piece = outbound[base * capacity : (base + len(chunk)) * capacity]
-        received = group_exchange(piece.reshape((len(chunk),) + slab), chunk, 0, 1, 2 * index)
+        local_first = index == 0 and chunk[0] == (0, 0) and inner_size % 2 == 0
+        remote = chunk[1:] if local_first else chunk
+        piece = outbound[(base + len(chunk) - len(remote)) * capacity : (base + len(chunk)) * capacity]
+        received = group_exchange(piece.reshape((len(remote),) + slab), remote, 0, 1, 2 * index)
+        rows = received.reshape(len(remote) * capacity, model_width)
+        gathered = lax.all_gather(rows, "inner", axis=0, tiled=True)
+        partial_value = expert_part(gathered, *weights).astype(jnp.bfloat16)
+        if local_first:
+            local_rows = lax.all_gather(
+                outbound[base * capacity : (base + 1) * capacity], "inner", axis=0, tiled=True
+            )
+            local_value = expert_part(local_rows, *weights).astype(jnp.bfloat16)
+            partial_value = jnp.concatenate(
+                [
+                    local_value.reshape(inner_size, capacity, model_width),
+                    partial_value.reshape(inner_size, len(remote) * capacity, model_width),
+                ],
+                axis=1,
+            )
+        partial_value = partial_value.reshape(-1, model_width)
         base += len(chunk)
-        rows = received.reshape(len(chunk) * capacity, model_width)
-        gathered = lax.all_gather(rows, "inner", axis=0, tiled=True)
-        partial_value = expert_part(gathered, gate_weight[0], up_weight[0], down_weight[0])
-        inner_size = lax.axis_size("inner")
         if inner_size % 2 == 0:
             same_core = [list(range(c, inner_size, 2)) for c in range(2)]
             core = lax.rem(lax.axis_index("inner"), 2)
-            by_core = partial_value.astype(jnp.bfloat16).reshape(inner_size // 2, 2, -1, model_width)
+            by_core = partial_value.reshape(inner_size // 2, 2, -1, model_width)
             received_sum = partner_swap(by_core, 8 + index)
             own_part = lax.dynamic_index_in_dim(by_core, core, axis=1, keepdims=False)
             pair_sum = own_part.astype(jnp.float32) + received_sum.astype(jnp.float32)
@@ -191,9 +207,7 @@
                 axis_index_groups=same_core,
             )
         else:
-            summed = lax.psum_scatter(
-                partial_value.astype(jnp.bfloat16), "inner", scatter_dimension=0, tiled=True
-            )
+            summed = lax.psum_scatter(partial_value, "inner", scatter_dimension=0, tiled=True)
         returned.append((summed.reshape((len(chunk),) + slab), chunk, index))
     expert_out = None
     base = 0

time: 288 us -> 296 us (1.028)
  waiting for transfers between devices: 76 us -> 49.9 us
  local copies, waits for them, and re-layouts: 19.3 us -> 38.5 us
  other arithmetic: 17.9 us -> 27.2 us
  matrix products: 59 us -> 64.3 us
    all_gather x2, waiting for transfers between devices: 40 us -> 16 us  [body(): gathered = lax.all_gather(rows, 'inner', axis=0, tiled=True)]
    unnamed x8 -> x14, local copies, waits for them, and re-layouts: 0.02 us -> 12.8 us
    concatenate x0 -> x1, other arithmetic: none -> 9.6 us  [body(): jnp.concatenate([local_value.reshape(inner_size, capacity, model_width),...]
    concatenate x0 -> x2, local copies, waits for them, and re-layouts: none -> 7.26 us  [body(): jnp.concatenate([local_value.reshape(inner_size, capacity, model_width),...]
    dot_general x2 -> x3, matrix products: 39.6 us -> 42.6 us  [expert_part(): return jnp.dot(hidden, down_mat, preferred_element_type=jnp.float32)]
    dot_general x2 -> x3, matrix products: 14.3 us -> 16.7 us  [expert_part(): gate_pre = jnp.dot(rows_in, gate_mat, preferred_element_type=jnp.float32)]
    reshape x4 -> x3, local copies, waits for them, and re-layouts: 7.5 us -> 5.24 us  [the longest x2 2.87 us: body(): piece.reshape((len(remote),) + slab)]
  transfers between devices with their start and end apart: 4 -> 5, of which waited for: 4 -> 3; matrix products, arithmetic and copies ran while one was open for 27% -> 39% of each run, Pallas kernels for 20% -> 27%
where the time goes in v12:
time: 296 us
  Pallas kernels  102 us (34%)
  matrix products  64.3 us (22%)
  waiting for transfers between devices  49.9 us (17%)
  local copies, waits for them, and re-layouts  38.5 us (13%)
  other arithmetic  27.2 us (9%)
  between operations  13.4 us (5%)
    pallas_call x4, Pallas kernels, group_exchange(): pl.pallas_call(functools.partial(exchange_kernel, groups, tuple(offsets),...  85.8 us
    dot_general x3, matrix products, expert_part(): return jnp.dot(hidden, down_mat, preferred_element_type=jnp.float32)  42.6 us
    reduce_scatter x2, waiting for transfers between devices, body(): lax.psum_scatter(pair_sum.astype(jnp.bfloat16).reshape(-1, model_width),...  33.9 us
    dot_general x3, matrix products, expert_part(): gate_pre = jnp.dot(rows_in, gate_mat, preferred_element_type=jnp.float32)  16.7 us
    pallas_call x2, Pallas kernels, partner_swap(): pl.pallas_call(swap_kernel, out_shape=jax.ShapeDtypeStruct(x.shape[:1] +...  16.4 us
    all_gather x2, waiting for transfers between devices, body(): gathered = lax.all_gather(rows, 'inner', axis=0, tiled=True)  16 us
    convert_element_type x2, other arithmetic, body(): pair_sum.astype(jnp.bfloat16).reshape(-1, model_width)  15.1 us
    unnamed x14, local copies, waits for them, and re-layouts  12.8 us
  transfers between devices with their start and end apart: 5, of which 3 were waited for; matrix products, arithmetic and copies ran while one was open for 39% of the time, Pallas kernels for 27%

profile of v12, /device:TPU:0, one launch (start us, length us, event | category | flops | bytes accessed | tf_op | source)
XLA Modules:
  0.0 295.9 jit_solution(7652457247898832081)
XLA Ops:
  9.9 1.4 copy-done.2
  12.0 1.5 slice.39
  13.6 1.5 reshape.53.x_ref
  15.1 21.5 %shard_map.73 = bf16[7,560,128]{2,1,0:T(8,128)(2,1)} custom-call(bf16[7,560,128]{2,1,0:T(8,128)(2,1)} %reshape.53.x_ref), custom_call_target="tpu_custom_call" | custom-call | tf_op jit(solution)/shard_map/pallas_call | solution.py:90
  36.5 2.3 reshape.93
  40.3 21.0 %shard_map.76 = bf16[8,560,128]{2,1,0:T(8,128)(2,1)} custom-call(bf16[8,560,128]{2,1,0:T(8,128)(2,1)} %reshape.59.x_ref), custom_call_target="tpu_custom_call" | custom-call | tf_op jit(solution)/shard_map/pallas_call | solution.py:90
  61.3 2.4 reshape.60
  64.0 1.8 reshape.92
  65.8 2.8 fusion.20
  68.6 5.5 %convolution_convert_fusion.3 = bf16[80,7168]{1,0:T(8,128)(2,1)S(1)} fusion(bf16[1,256,7168]{2,1,0:T(8,128)(2,1)} %param.12, bf16[80,7168]{1,0:T(8,128)(2,1)S(1)} %reshape.92, bf16[1,7168,256]{2,1,0:T(8,128)(2,1)} %param.11, f32[80,256]{1,0:T(8,128)S(1)} %fusion.20), kind=kOutput, calls=%fused_computation.15 | convolution fusion | flops 587898880 | bytes 9715712 | tf_op jit(solution)/shard_map/dot_general | solution.py:140
  74.5 16.0 %all-gather.10.cloned.1.call-done = bf16[8,70,7168]{2,1,0:T(8,128)(2,1)} async-done(((bf16[1,70,7168]{2,1,0:T(8,128)(2,1)}), bf16[8,70,7168]{2,1,0:T(8,128)(2,1)}) %all-gather.10.cloned.1.call-update) | async-done | bytes 8028176 | tf_op jit(solution)/shard_map/all_gather | solution.py:179
  90.5 6.6 %reshape.94 = bf16[560,7168]{1,0:T(8,128)(2,1)} reshape(bf16[8,70,7168]{2,1,0:T(8,128)(2,1)} %all-gather.10.cloned.1.call-done) | data formatting | bytes 16056320
  97.1 6.7 %fusion.18 = f32[560,256]{1,0:T(8,128)S(1)} fusion(bf16[560,7168]{1,0:T(8,128)(2,1)} %reshape.94, bf16[1,7168,256]{2,1,0:T(8,128)(2,1)} %param.10), kind=kOutput, calls=%fused_computation.29 | convolution fusion | flops 2055208960 | bytes 12271616 | tf_op jit(solution)/shard_map/dot_general | solution.py:137
  103.8 17.4 %convolution_convert_fusion.1 = bf16[560,7168]{1,0:T(8,128)(2,1)} fusion(bf16[1,256,7168]{2,1,0:T(8,128)(2,1)} %param.12, bf16[560,7168]{1,0:T(8,128)(2,1)} %reshape.94, bf16[1,7168,256]{2,1,0:T(8,128)(2,1)} %param.11, f32[560,256]{1,0:T(8,128)S(1)} %fusion.18), kind=kOutput, calls=%fused_computation.3 | convolution fusion | flops 4115292160 | bytes 23969792 | tf_op jit(solution)/shard_map/dot_general | solution.py:140
  121.2 6.8 %concatenate.9 = bf16[4,2,70,7168]{3,2,1,0:T(8,128)(2,1)} reshape(bf16[560,7168]{1,0:T(8,128)(2,1)} %convolution_convert_fusion.1) | data formatting | bytes 16056320 | tf_op jit(solution)/shard_map/concatenate | solution.py:186
  128.0 9.6 %pad_maximum_fusion.x_ref = bf16[4,2,80,7168]{3,2,1,0:T(8,128)(2,1)} fusion(bf16[4,2,10,7168]{3,2,1,0:T(8,128)(2,1)S(1)} %concatenate.8, bf16[4,2,70,7168]{3,2,1,0:T(8,128)(2,1)} %concatenate.9), kind=kLoop, calls=%fused_computation.1 | loop fusion | flops 18350080 | bytes 18350080 | tf_op jit(solution)/shard_map/concatenate | solution.py:186
  137.6 8.3 %shard_map.74 = bf16[4,80,7168]{2,1,0:T(8,128)(2,1)} custom-call(bf16[4,2,80,7168]{3,2,1,0:T(8,128)(2,1)} %pad_maximum_fusion.x_ref), custom_call_target="tpu_custom_call" | custom-call | tf_op jit(solution)/shard_map/pallas_call | solution.py:126
  146.0 7.5 %fusion.1 = bf16[4,80,7168]{2,1,0:T(8,128)(2,1)} fusion(bf16[4,80,7168]{2,1,0:T(8,128)(2,1)} %shard_map.74, s32[]{:T(128)S(6)} %select_n.30, bf16[4,2,70,7168]{3,2,1,0:T(8,128)(2,1)} %concatenate.9, bf16[4,2,10,7168]{3,2,1,0:T(8,128)(2,1)S(1)} %concatenate.8), kind=kLoop, calls=%fused_computation.7 | loop fusion | flops 18350080 | bytes 18350084 | tf_op jit(solution)/shard_map/convert_element_type | solution.py:203
  153.6 7.2 %fusion.16 = f32[640,256]{1,0:T(8,128)S(1)} fusion(bf16[640,7168]{1,0:T(8,128)(2,1)} %all-gather.6.cloned.1.call-done, bf16[1,7168,256]{2,1,0:T(8,128)(2,1)} %param.10), kind=kOutput, calls=%fused_computation.27 | convolution fusion | flops 2348810240 | bytes 13500416 | tf_op jit(solution)/shard_map/dot_general | solution.py:137
  160.8 19.8 %convolution_convert_fusion = bf16[640,7168]{1,0:T(8,128)(2,1)} fusion(bf16[1,256,7168]{2,1,0:T(8,128)(2,1)} %param.12, bf16[640,7168]{1,0:T(8,128)(2,1)} %all-gather.6.cloned.1.call-done, bf16[1,7168,256]{2,1,0:T(8,128)(2,1)} %param.11, f32[640,256]{1,0:T(8,128)S(1)} %fusion.16), kind=kOutput, calls=%fused_computation.2 | convolution fusion | flops 4703191040 | bytes 26345472 | tf_op jit(solution)/shard_map/dot_general | solution.py:140
  180.5 8.1 %shard_map.77 = bf16[4,80,7168]{2,1,0:T(8,128)(2,1)} custom-call(bf16[4,2,80,7168]{3,2,1,0:T(8,128)(2,1)} %bitcast.73), custom_call_target="tpu_custom_call" | custom-call | tf_op jit(solution)/shard_map/pallas_call | solution.py:126
  188.6 7.5 %fusion = bf16[4,80,7168]{2,1,0:T(8,128)(2,1)} fusion(bf16[4,80,7168]{2,1,0:T(8,128)(2,1)} %shard_map.77, bf16[4,2,80,7168]{3,2,1,0:T(8,128)(2,1)} %bitcast.74, s32[]{:T(128)S(6)} %select_n.30), kind=kLoop, calls=%fused_computation.5 | loop fusion | flops 9175040 | bytes 13762564 | tf_op jit(solution)/shard_map/convert_element_type | solution.py:203
  196.3 7.8 %reduce-scatter.3.cloned.1.call-done = bf16[80,7168]{1,0:T(8,128)(2,1)} async-done(((bf16[320,7168]{1,0:T(8,128)(2,1)}), bf16[80,7168]{1,0:T(8,128)(2,1)}) %reduce-scatter.3.cloned.1.call-update) | async-done | bytes 1146896 | tf_op jit(solution)/shard_map/reduce_scatter | solution.py:202
  204.1 2.4 reshape.56.x_ref
  206.5 20.2 %shard_map.75 = bf16[8,560,128]{2,1,0:T(8,128)(2,1)} custom-call(bf16[8,560,128]{2,1,0:T(8,128)(2,1)} %reshape.56.x_ref), custom_call_target="tpu_custom_call" | custom-call | tf_op jit(solution)/shard_map/pallas_call | solution.py:90
  226.7 3.4 %reshape.57 = bf16[8,10,7168]{2,1,0:T(8,128)(2,1)} reshape(bf16[8,560,128]{2,1,0:T(8,128)(2,1)} %shard_map.75) | data formatting | bytes 2293760 | tf_op jit(solution)/shard_map/reshape | solution.py:221
  230.1 26.0 %reduce-scatter.5.cloned.1.call-done = bf16[80,7168]{1,0:T(8,128)(2,1)} async-done(((bf16[320,7168]{1,0:T(8,128)(2,1)}), bf16[80,7168]{1,0:T(8,128)(2,1)}) %reduce-scatter.5.cloned.1.call-update) | async-done | bytes 1146896 | tf_op jit(solution)/shard_map/reduce_scatter | solution.py:202
  256.1 2.4 reshape.63.x_ref
  258.6 23.1 %shard_map.78 = bf16[8,560,128]{2,1,0:T(8,128)(2,1)} custom-call(bf16[8,560,128]{2,1,0:T(8,128)(2,1)} %reshape.63.x_ref), custom_call_target="tpu_custom_call" | custom-call | tf_op jit(solution)/shard_map/pallas_call | solution.py:90
  281.7 3.4 %reshape.64 = bf16[8,10,7168]{2,1,0:T(8,128)(2,1)} reshape(bf16[8,560,128]{2,1,0:T(8,128)(2,1)} %shard_map.78) | data formatting | bytes 2293760 | tf_op jit(solution)/shard_map/reshape | solution.py:221
  285.1 2.3 convolution_bitcast_fusion
  287.4 1.9 fusion.4
  (35 shorter events, 6.4 us)
Async XLA Ops:
  6.5 2.6 copy-start
  6.5 57.4 %all-gather.8.cloned.1.call-start = ((), (), s32[]{:S(2)}) async-start(), calls=%async_computation.5 | async-start | bytes 2064384 | tf_op jit(solution)/shard_map/all_gather | solution.py:182
  9.9 1.4 copy-start.2
  12.0 78.5 %all-gather.10.cloned.1.call-start = ((), (), s32[]{:S(2)}) async-start(), calls=%async_computation.6 | async-start | bytes 9289728 | tf_op jit(solution)/shard_map/all_gather | solution.py:179
  15.1 23.9 %slice-start = ((bf16[160,7168]{1,0:T(8,128)(2,1)}), bf16[80,7168]{1,0:T(8,128)(2,1)S(1)}, s32[]{:S(2)}) async-start(bf16[160,7168]{1,0:T(8,128)(2,1)} %copy-done.2), calls=%async_computation.7 | async-start | bytes 2293760 | tf_op jit(solution)/shard_map/slice | solution.py:176
  38.9 114.7 %all-gather.6.cloned.1.call-start = ((), (), s32[]{:S(2)}) async-start(), calls=%async_computation.3 | async-start | bytes 10321920 | tf_op jit(solution)/shard_map/all_gather | solution.py:179
  63.7 140.4 %reduce-scatter.3.cloned.1.call-start = ((), (), s32[]{:S(2)}) async-start(), calls=%async_computation.2 | async-start | bytes 5734400 | tf_op jit(solution)/shard_map/reduce_scatter | solution.py:202
  153.5 102.6 %reduce-scatter.5.cloned.1.call-start = ((), (), s32[]{:S(2)}) async-start(), calls=%async_computation.4 | async-start | bytes 5734400 | tf_op jit(solution)/shard_map/reduce_scatter | solution.py:202
  281.7 5.7 %copy-start.4 = (f32[128]{0:T(128)S(1)}, f32[128]{0:T(128)}, u32[]{:S(2)}) copy-start(f32[128]{0:T(128)} %param.9) | copy-start | bytes 1540
  285.1 2.4 copy-start.3
  285.1 4.3 %copy-start.1 = (bf16[128,7168]{1,0:T(8,128)(2,1)S(1)}, bf16[128,7168]{1,0:T(8,128)(2,1)}, u32[]{:S(2)}) copy-start(bf16[128,7168]{1,0:T(8,128)(2,1)} %param.7) | copy-start | bytes 5505028
Sparse Core Ops, SparseCore 0:
  12.1 27.3 all-gather.7
  41.2 49.2 all-gather.9
  92.2 54.4 all-gather.5
  153.6 50.4 reduce-scatter.2
  206.4 49.7 reduce-scatter.4

commit v13 on v11

--- a/solution.py
+++ b/solution.py
@@ -184,7 +184,7 @@
             own_part = lax.dynamic_index_in_dim(by_core, core, axis=1, keepdims=False)
             pair_sum = own_part.astype(jnp.float32) + received_sum.astype(jnp.float32)
             summed = lax.psum_scatter(
-                pair_sum.astype(jnp.bfloat16).reshape(-1, model_width),
+                pair_sum.astype(jnp.bfloat16).reshape((-1,) + slab),
                 "inner",
                 scatter_dimension=0,
                 tiled=True,

time: 288 us -> 286 us (level)
  waiting for transfers between devices: 76 us -> 62.9 us
  local copies, waits for them, and re-layouts: 19.3 us -> 29.9 us
    reshape x2, local copies, waits for them, and re-layouts: 4.81 us -> 15.4 us  [body(): pair_sum.astype(jnp.bfloat16).reshape((-1,) + slab)]
    all_gather x2, waiting for transfers between devices: 40 us -> 32.2 us  [body(): gathered = lax.all_gather(rows, 'inner', axis=0, tiled=True)]
    reduce_scatter x2, waiting for transfers between devices: 36 us -> 30.6 us  [body(): lax.psum_scatter(pair_sum.astype(jnp.bfloat16).reshape((-1,) + slab), 'in...]
  transfers between devices with their start and end apart: 4 -> 4, of which waited for: 4 -> 4; matrix products, arithmetic and copies ran while one was open for 27% -> 32% of each run, Pallas kernels for 20% -> 20%
where the time goes in v13:
time: 286 us
  Pallas kernels  102 us (36%)
  waiting for transfers between devices  62.9 us (22%)
  matrix products  59 us (21%)
  local copies, waits for them, and re-layouts  29.9 us (10%)
  other arithmetic  18 us (6%)
  between operations  13.3 us (5%)
    pallas_call x4, Pallas kernels, group_exchange(): pl.pallas_call(functools.partial(exchange_kernel, groups, tuple(offsets),...  85.8 us
    dot_general x2, matrix products, expert_part(): return jnp.dot(hidden, down_mat, preferred_element_type=jnp.float32)  39.6 us
    all_gather x2, waiting for transfers between devices, body(): gathered = lax.all_gather(rows, 'inner', axis=0, tiled=True)  32.2 us
    reduce_scatter x2, waiting for transfers between devices, body(): lax.psum_scatter(pair_sum.astype(jnp.bfloat16).reshape((-1,) + slab), 'in...  30.6 us
    pallas_call x2, Pallas kernels, partner_swap(): pl.pallas_call(swap_kernel, out_shape=jax.ShapeDtypeStruct(x.shape[:1] +...  16.2 us
    convert_element_type x2, other arithmetic, body(): pair_sum.astype(jnp.bfloat16).reshape((-1,) + slab)  15.4 us
    reshape x2, local copies, waits for them, and re-layouts, body(): pair_sum.astype(jnp.bfloat16).reshape((-1,) + slab)  15.4 us
    dot_general x2, matrix products, expert_part(): gate_pre = jnp.dot(rows_in, gate_mat, preferred_element_type=jnp.float32)  14.3 us
  transfers between devices with their start and end apart: 4, of which 4 were waited for; matrix products, arithmetic and copies ran while one was open for 32% of the time, Pallas kernels for 20%

profile of v13, /device:TPU:0, one launch (start us, length us, event | category | flops | bytes accessed | tf_op | source)
XLA Modules:
  0.0 285.6 jit_solution(7468842212754293326)
XLA Ops:
  6.5 0.9 fusion.43
  7.6 0.8 select_reduce_fusion
  8.4 0.7 compare_select_fusion.23
  9.1 0.7 convolution_convert_fusion.2
  10.0 1.4 reshape.44.x_ref
  11.4 21.5 %shard_map.73 = bf16[8,560,128]{2,1,0:T(8,128)(2,1)} custom-call(bf16[8,560,128]{2,1,0:T(8,128)(2,1)} %reshape.44.x_ref), custom_call_target="tpu_custom_call" | custom-call | tf_op jit(solution)/shard_map/pallas_call | solution.py:90
  32.9 2.4 reshape.45
  35.4 1.4 reshape.50.x_ref
  36.7 21.0 %shard_map.76 = bf16[8,560,128]{2,1,0:T(8,128)(2,1)} custom-call(bf16[8,560,128]{2,1,0:T(8,128)(2,1)} %reshape.50.x_ref), custom_call_target="tpu_custom_call" | custom-call | tf_op jit(solution)/shard_map/pallas_call | solution.py:90
  57.8 2.4 reshape.51
  60.2 0.2 reduce-scatter.3.cloned.1.call-start
  60.4 28.1 %all-gather.3.cloned.1.call-done = bf16[640,7168]{1,0:T(8,128)(2,1)} async-done(((bf16[80,7168]{1,0:T(8,128)(2,1)}), bf16[640,7168]{1,0:T(8,128)(2,1)}) %all-gather.3.cloned.1.call-update) | async-done | bytes 9175056 | tf_op jit(solution)/shard_map/all_gather | solution.py:176
  88.5 7.2 %fusion.13 = f32[640,256]{1,0:T(8,128)S(1)} fusion(bf16[640,7168]{1,0:T(8,128)(2,1)} %all-gather.3.cloned.1.call-done, bf16[1,7168,256]{2,1,0:T(8,128)(2,1)} %param.10), kind=kOutput, calls=%fused_computation.20 | convolution fusion | flops 2348810240 | bytes 13500416 | tf_op jit(solution)/shard_map/dot_general | solution.py:137
  95.7 19.8 %convolution_convert_fusion.1 = bf16[640,7168]{1,0:T(8,128)(2,1)} fusion(bf16[1,256,7168]{2,1,0:T(8,128)(2,1)} %param.12, bf16[640,7168]{1,0:T(8,128)(2,1)} %all-gather.3.cloned.1.call-done, bf16[1,7168,256]{2,1,0:T(8,128)(2,1)} %param.11, f32[640,256]{1,0:T(8,128)S(1)} %fusion.13), kind=kOutput, calls=%fused_computation.1 | convolution fusion | flops 4703191040 | bytes 26345472 | tf_op jit(solution)/shard_map/dot_general | solution.py:140
  115.5 8.1 %shard_map.74 = bf16[4,80,7168]{2,1,0:T(8,128)(2,1)} custom-call(bf16[4,2,80,7168]{3,2,1,0:T(8,128)(2,1)} %bitcast.56), custom_call_target="tpu_custom_call" | custom-call | tf_op jit(solution)/shard_map/pallas_call | solution.py:126
  123.6 7.8 %fusion.1 = bf16[4,80,7168]{2,1,0:T(8,128)(2,1)} fusion(bf16[4,80,7168]{2,1,0:T(8,128)(2,1)} %shard_map.74, bf16[4,2,80,7168]{3,2,1,0:T(8,128)(2,1)} %bitcast.57, s32[]{:T(128)S(6)} %select_n.30), kind=kLoop, calls=%fused_computation.5 | loop fusion | flops 9175040 | bytes 13762564 | tf_op jit(solution)/shard_map/convert_element_type | solution.py:187
  131.4 7.7 %reshape.47 = bf16[32,560,128]{2,1,0:T(8,128)(2,1)} reshape(bf16[4,80,7168]{2,1,0:T(8,128)(2,1)} %fusion.1) | data formatting | bytes 9175040 | tf_op jit(solution)/shard_map/reshape | solution.py:187
  139.1 0.3 reduce-scatter.5.cloned.1.call-start
  139.4 4.1 %all-gather.5.cloned.1.call-done = bf16[640,7168]{1,0:T(8,128)(2,1)} async-done(((bf16[80,7168]{1,0:T(8,128)(2,1)}), bf16[640,7168]{1,0:T(8,128)(2,1)}) %all-gather.5.cloned.1.call-update) | async-done | bytes 9175056 | tf_op jit(solution)/shard_map/all_gather | solution.py:176
  143.5 7.2 %fusion.11 = f32[640,256]{1,0:T(8,128)S(1)} fusion(bf16[640,7168]{1,0:T(8,128)(2,1)} %all-gather.5.cloned.1.call-done, bf16[1,7168,256]{2,1,0:T(8,128)(2,1)} %param.10), kind=kOutput, calls=%fused_computation.18 | convolution fusion | flops 2348810240 | bytes 13500416 | tf_op jit(solution)/shard_map/dot_general | solution.py:137
  150.7 19.8 %convolution_convert_fusion = bf16[640,7168]{1,0:T(8,128)(2,1)} fusion(bf16[1,256,7168]{2,1,0:T(8,128)(2,1)} %param.12, bf16[640,7168]{1,0:T(8,128)(2,1)} %all-gather.5.cloned.1.call-done, bf16[1,7168,256]{2,1,0:T(8,128)(2,1)} %param.11, f32[640,256]{1,0:T(8,128)S(1)} %fusion.11), kind=kOutput, calls=%fused_computation | convolution fusion | flops 4703191040 | bytes 26345472 | tf_op jit(solution)/shard_map/dot_general | solution.py:140
  170.4 8.1 %shard_map.77 = bf16[4,80,7168]{2,1,0:T(8,128)(2,1)} custom-call(bf16[4,2,80,7168]{3,2,1,0:T(8,128)(2,1)} %bitcast.54), custom_call_target="tpu_custom_call" | custom-call | tf_op jit(solution)/shard_map/pallas_call | solution.py:126
  178.5 7.6 %fusion = bf16[4,80,7168]{2,1,0:T(8,128)(2,1)} fusion(bf16[4,80,7168]{2,1,0:T(8,128)(2,1)} %shard_map.77, bf16[4,2,80,7168]{3,2,1,0:T(8,128)(2,1)} %bitcast.55, s32[]{:T(128)S(6)} %select_n.30), kind=kLoop, calls=%fused_computation.3 | loop fusion | flops 9175040 | bytes 13762564 | tf_op jit(solution)/shard_map/convert_element_type | solution.py:187
  186.2 7.7 %reshape.53 = bf16[32,560,128]{2,1,0:T(8,128)(2,1)} reshape(bf16[4,80,7168]{2,1,0:T(8,128)(2,1)} %fusion) | data formatting | bytes 9175040 | tf_op jit(solution)/shard_map/reshape | solution.py:187
  194.0 2.2 reduce-scatter.3.cloned.1.call-done.x_ref
  196.2 20.2 %shard_map.75 = bf16[8,560,128]{2,1,0:T(8,128)(2,1)} custom-call(bf16[8,560,128]{2,1,0:T(8,128)(2,1)} %reduce-scatter.3.cloned.1.call-done.x_ref), custom_call_target="tpu_custom_call" | custom-call | tf_op jit(solution)/shard_map/pallas_call | solution.py:90
  216.4 3.4 %reshape.48 = bf16[8,10,7168]{2,1,0:T(8,128)(2,1)} reshape(bf16[8,560,128]{2,1,0:T(8,128)(2,1)} %shard_map.75) | data formatting | bytes 2293760 | tf_op jit(solution)/shard_map/reshape | solution.py:207
  219.8 28.4 %reduce-scatter.5.cloned.1.call-done.x_ref = bf16[8,560,128]{2,1,0:T(8,128)(2,1)} async-done(((bf16[32,560,128]{2,1,0:T(8,128)(2,1)}), bf16[8,560,128]{2,1,0:T(8,128)(2,1)}) %reduce-scatter.5.cloned.1.call-update) | async-done | bytes 1146896 | tf_op jit(solution)/shard_map/reduce_scatter | solution.py:186
  248.2 23.1 %shard_map.78 = bf16[8,560,128]{2,1,0:T(8,128)(2,1)} custom-call(bf16[8,560,128]{2,1,0:T(8,128)(2,1)} %reduce-scatter.5.cloned.1.call-done.x_ref), custom_call_target="tpu_custom_call" | custom-call | tf_op jit(solution)/shard_map/pallas_call | solution.py:90
  271.4 3.4 %reshape.54 = bf16[8,10,7168]{2,1,0:T(8,128)(2,1)} reshape(bf16[8,560,128]{2,1,0:T(8,128)(2,1)} %shard_map.78) | data formatting | bytes 2293760 | tf_op jit(solution)/shard_map/reshape | solution.py:207
  274.8 2.3 convolution_bitcast_fusion
  277.1 1.9 fusion.4
  (20 shorter events, 0.5 us)
Async XLA Ops:
  6.5 2.6 copy-start
  6.5 82.0 %all-gather.3.cloned.1.call-start = ((), (), s32[]{:S(2)}) async-start(), calls=%async_computation.2 | async-start | bytes 10321920 | tf_op jit(solution)/shard_map/all_gather | solution.py:176
  35.3 108.2 %all-gather.5.cloned.1.call-start = ((), (), s32[]{:S(2)}) async-start(), calls=%async_computation.4 | async-start | bytes 10321920 | tf_op jit(solution)/shard_map/all_gather | solution.py:176
  60.2 136.0 %reduce-scatter.3.cloned.1.call-start = ((), (), s32[]{:S(2)}) async-start(), calls=%async_computation.3 | async-start | bytes 5734400 | tf_op jit(solution)/shard_map/reduce_scatter | solution.py:186
  139.1 109.1 %reduce-scatter.5.cloned.1.call-start = ((), (), s32[]{:S(2)}) async-start(), calls=%async_computation.5 | async-start | bytes 5734400 | tf_op jit(solution)/shard_map/reduce_scatter | solution.py:186
  271.4 5.7 %copy-start.3 = (f32[128]{0:T(128)S(1)}, f32[128]{0:T(128)}, u32[]{:S(2)}) copy-start(f32[128]{0:T(128)} %param.9) | copy-start | bytes 1540
  274.8 2.4 copy-start.2
  274.8 4.3 %copy-start.1 = (bf16[128,7168]{1,0:T(8,128)(2,1)S(1)}, bf16[128,7168]{1,0:T(8,128)(2,1)}, u32[]{:S(2)}) copy-start(bf16[128,7168]{1,0:T(8,128)(2,1)} %param.7) | copy-start | bytes 5505028
Sparse Core Ops, SparseCore 0:
  35.4 53.0 all-gather.2
  90.2 53.2 all-gather.4
  145.9 50.2 reduce-scatter.2
  198.4 49.7 reduce-scatter.4

commit v14 on v13

--- a/solution.py
+++ b/solution.py
@@ -172,8 +172,8 @@
         piece = outbound[base * capacity : (base + len(chunk)) * capacity]
         received = group_exchange(piece.reshape((len(chunk),) + slab), chunk, 0, 1, 2 * index)
         base += len(chunk)
-        rows = received.reshape(len(chunk) * capacity, model_width)
-        gathered = lax.all_gather(rows, "inner", axis=0, tiled=True)
+        gathered = lax.all_gather(received, "inner", axis=0, tiled=True)
+        gathered = gathered.reshape(-1, model_width)
         partial_value = expert_part(gathered, gate_weight[0], up_weight[0], down_weight[0])
         inner_size = lax.axis_size("inner")
         if inner_size % 2 == 0:

time: 286 us -> 304 us (1.063)
  local copies, waits for them, and re-layouts: 29.9 us -> 53.1 us
  waiting for transfers between devices: 62.9 us -> 56.6 us
    reshape x2, local copies, waits for them, and re-layouts: 4.77 us -> 28.1 us  [body(): gathered = gathered.reshape(-1, model_width)]
    reduce_scatter x2, waiting for transfers between devices: 30.6 us -> 26 us  [body(): lax.psum_scatter(pair_sum.astype(jnp.bfloat16).reshape((-1,) + slab), 'in...]
  transfers between devices with their start and end apart: 4 -> 4, of which waited for: 4 -> 2; matrix products, arithmetic and copies ran while one was open for 32% -> 38% of each run, Pallas kernels for 20% -> 19%
where the time goes in v14:
time: 304 us; the launch traced here: 303 us
  Pallas kernels  104 us (34%)
  matrix products  57.9 us (19%)
  waiting for transfers between devices  56.6 us (19%)
  local copies, waits for them, and re-layouts  53.1 us (17%)
  other arithmetic  17.9 us (6%)
  between operations  13.3 us (4%)
    pallas_call x4, Pallas kernels, group_exchange(): pl.pallas_call(functools.partial(exchange_kernel, groups, tuple(offsets),...  87 us
    dot_general x2, matrix products, expert_part(): return jnp.dot(hidden, down_mat, preferred_element_type=jnp.float32)  38.3 us
    all_gather x2, waiting for transfers between devices, body(): gathered = lax.all_gather(received, 'inner', axis=0, tiled=True)  30.5 us
    reshape x2, local copies, waits for them, and re-layouts, body(): gathered = gathered.reshape(-1, model_width)  28.1 us
    reduce_scatter x2, waiting for transfers between devices, body(): lax.psum_scatter(pair_sum.astype(jnp.bfloat16).reshape((-1,) + slab), 'in...  26 us
    pallas_call x2, Pallas kernels, partner_swap(): pl.pallas_call(swap_kernel, out_shape=jax.ShapeDtypeStruct(x.shape[:1] +...  16.5 us
    convert_element_type x2, other arithmetic, body(): pair_sum.astype(jnp.bfloat16).reshape((-1,) + slab)  15.4 us
    reshape x2, local copies, waits for them, and re-layouts, body(): pair_sum.astype(jnp.bfloat16).reshape((-1,) + slab)  15.3 us
  transfers between devices with their start and end apart: 4, of which 2 were waited for; matrix products, arithmetic and copies ran while one was open for 38% of the time, Pallas kernels for 19%

profile of v14, /device:TPU:0, one launch (start us, length us, event | category | flops | bytes accessed | tf_op | source)
XLA Modules:
  0.0 303.0 jit_solution(18083259412583478603)
XLA Ops:
  6.5 0.9 fusion.43
  7.4 0.2 reduce_window_sum.11
  7.6 0.8 select_reduce_fusion
  8.4 0.7 compare_select_fusion.23
  9.1 0.7 convolution_convert_fusion.2
  9.9 0.2 fusion.52
  10.0 1.4 reshape.44.x_ref
  11.4 21.5 %shard_map.73 = bf16[8,560,128]{2,1,0:T(8,128)(2,1)} custom-call(bf16[8,560,128]{2,1,0:T(8,128)(2,1)} %reshape.44.x_ref), custom_call_target="tpu_custom_call" | custom-call | tf_op jit(solution)/shard_map/pallas_call | solution.py:90
  33.0 1.4 reshape.50.x_ref
  34.4 21.0 %shard_map.76 = bf16[8,560,128]{2,1,0:T(8,128)(2,1)} custom-call(bf16[8,560,128]{2,1,0:T(8,128)(2,1)} %reshape.50.x_ref), custom_call_target="tpu_custom_call" | custom-call | tf_op jit(solution)/shard_map/pallas_call | solution.py:90
  55.4 0.2 reduce-scatter.3.cloned.1.call-start
  55.6 30.5 %all-gather.3.cloned.1.call-done = bf16[64,560,128]{2,1,0:T(8,128)(2,1)} async-done(((bf16[8,560,128]{2,1,0:T(8,128)(2,1)}), bf16[64,560,128]{2,1,0:T(8,128)(2,1)}) %all-gather.3.cloned.1.call-update) | async-done | bytes 9175056 | tf_op jit(solution)/shard_map/all_gather | solution.py:175
  86.2 14.0 %reshape.45 = bf16[640,7168]{1,0:T(8,128)(2,1)} reshape(bf16[64,560,128]{2,1,0:T(8,128)(2,1)} %all-gather.3.cloned.1.call-done) | data formatting | bytes 18350080 | tf_op jit(solution)/shard_map/reshape | solution.py:176
  100.2 7.3 %fusion.13 = f32[640,256]{1,0:T(8,128)S(1)} fusion(bf16[640,7168]{1,0:T(8,128)(2,1)} %reshape.45, bf16[1,7168,256]{2,1,0:T(8,128)(2,1)} %param.10), kind=kOutput, calls=%fused_computation.20 | convolution fusion | flops 2348810240 | bytes 13500416 | tf_op jit(solution)/shard_map/dot_general | solution.py:137
  107.5 19.2 %convolution_convert_fusion.1 = bf16[640,7168]{1,0:T(8,128)(2,1)} fusion(bf16[1,256,7168]{2,1,0:T(8,128)(2,1)} %param.12, bf16[640,7168]{1,0:T(8,128)(2,1)} %reshape.45, bf16[1,7168,256]{2,1,0:T(8,128)(2,1)} %param.11, f32[640,256]{1,0:T(8,128)S(1)} %fusion.13), kind=kOutput, calls=%fused_computation.1 | convolution fusion | flops 4703191040 | bytes 26345472 | tf_op jit(solution)/shard_map/dot_general | solution.py:140
  126.7 8.4 %shard_map.74 = bf16[4,80,7168]{2,1,0:T(8,128)(2,1)} custom-call(bf16[4,2,80,7168]{3,2,1,0:T(8,128)(2,1)} %bitcast.56), custom_call_target="tpu_custom_call" | custom-call | tf_op jit(solution)/shard_map/pallas_call | solution.py:126
  135.2 7.6 %fusion.1 = bf16[4,80,7168]{2,1,0:T(8,128)(2,1)} fusion(bf16[4,80,7168]{2,1,0:T(8,128)(2,1)} %shard_map.74, bf16[4,2,80,7168]{3,2,1,0:T(8,128)(2,1)} %bitcast.57, s32[]{:T(128)S(6)} %select_n.30), kind=kLoop, calls=%fused_computation.5 | loop fusion | flops 9175040 | bytes 13762564 | tf_op jit(solution)/shard_map/convert_element_type | solution.py:187
  142.8 7.6 %reshape.47 = bf16[32,560,128]{2,1,0:T(8,128)(2,1)} reshape(bf16[4,80,7168]{2,1,0:T(8,128)(2,1)} %fusion.1) | data formatting | bytes 9175040 | tf_op jit(solution)/shard_map/reshape | solution.py:187
  150.5 0.3 reduce-scatter.5.cloned.1.call-start
  150.8 14.0 %reshape.51 = bf16[640,7168]{1,0:T(8,128)(2,1)} reshape(bf16[64,560,128]{2,1,0:T(8,128)(2,1)} %all-gather.5.cloned.1.call-done) | data formatting | bytes 18350080 | tf_op jit(solution)/shard_map/reshape | solution.py:176
  164.8 7.3 %fusion.11 = f32[640,256]{1,0:T(8,128)S(1)} fusion(bf16[640,7168]{1,0:T(8,128)(2,1)} %reshape.51, bf16[1,7168,256]{2,1,0:T(8,128)(2,1)} %param.10), kind=kOutput, calls=%fused_computation.18 | convolution fusion | flops 2348810240 | bytes 13500416 | tf_op jit(solution)/shard_map/dot_general | solution.py:137
  172.1 19.1 %convolution_convert_fusion = bf16[640,7168]{1,0:T(8,128)(2,1)} fusion(bf16[1,256,7168]{2,1,0:T(8,128)(2,1)} %param.12, bf16[640,7168]{1,0:T(8,128)(2,1)} %reshape.51, bf16[1,7168,256]{2,1,0:T(8,128)(2,1)} %param.11, f32[640,256]{1,0:T(8,128)S(1)} %fusion.11), kind=kOutput, calls=%fused_computation | convolution fusion | flops 4703191040 | bytes 26345472 | tf_op jit(solution)/shard_map/dot_general | solution.py:140
  191.2 8.1 %shard_map.77 = bf16[4,80,7168]{2,1,0:T(8,128)(2,1)} custom-call(bf16[4,2,80,7168]{3,2,1,0:T(8,128)(2,1)} %bitcast.54), custom_call_target="tpu_custom_call" | custom-call | tf_op jit(solution)/shard_map/pallas_call | solution.py:126
  199.3 7.7 %fusion = bf16[4,80,7168]{2,1,0:T(8,128)(2,1)} fusion(bf16[4,80,7168]{2,1,0:T(8,128)(2,1)} %shard_map.77, bf16[4,2,80,7168]{3,2,1,0:T(8,128)(2,1)} %bitcast.55, s32[]{:T(128)S(6)} %select_n.30), kind=kLoop, calls=%fused_computation.3 | loop fusion | flops 9175040 | bytes 13762564 | tf_op jit(solution)/shard_map/convert_element_type | solution.py:187
  207.0 7.7 %reshape.53 = bf16[32,560,128]{2,1,0:T(8,128)(2,1)} reshape(bf16[4,80,7168]{2,1,0:T(8,128)(2,1)} %fusion) | data formatting | bytes 9175040 | tf_op jit(solution)/shard_map/reshape | solution.py:187
  214.8 21.4 %shard_map.75 = bf16[8,560,128]{2,1,0:T(8,128)(2,1)} custom-call(bf16[8,560,128]{2,1,0:T(8,128)(2,1)} %reduce-scatter.3.cloned.1.call-done.x_ref), custom_call_target="tpu_custom_call" | custom-call | tf_op jit(solution)/shard_map/pallas_call | solution.py:90
  236.2 3.4 %reshape.48 = bf16[8,10,7168]{2,1,0:T(8,128)(2,1)} reshape(bf16[8,560,128]{2,1,0:T(8,128)(2,1)} %shard_map.75) | data formatting | bytes 2293760 | tf_op jit(solution)/shard_map/reshape | solution.py:207
  239.6 26.0 %reduce-scatter.5.cloned.1.call-done.x_ref = bf16[8,560,128]{2,1,0:T(8,128)(2,1)} async-done(((bf16[32,560,128]{2,1,0:T(8,128)(2,1)}), bf16[8,560,128]{2,1,0:T(8,128)(2,1)}) %reduce-scatter.5.cloned.1.call-update) | async-done | bytes 1146896 | tf_op jit(solution)/shard_map/reduce_scatter | solution.py:186
  265.6 23.1 %shard_map.78 = bf16[8,560,128]{2,1,0:T(8,128)(2,1)} custom-call(bf16[8,560,128]{2,1,0:T(8,128)(2,1)} %reduce-scatter.5.cloned.1.call-done.x_ref), custom_call_target="tpu_custom_call" | custom-call | tf_op jit(solution)/shard_map/pallas_call | solution.py:90
  288.7 3.4 %reshape.54 = bf16[8,10,7168]{2,1,0:T(8,128)(2,1)} reshape(bf16[8,560,128]{2,1,0:T(8,128)(2,1)} %shard_map.78) | data formatting | bytes 2293760 | tf_op jit(solution)/shard_map/reshape | solution.py:207
  292.1 2.3 convolution_bitcast_fusion
  294.5 1.9 fusion.4
  (20 shorter events, 0.2 us)
Async XLA Ops:
  6.5 2.6 copy-start
  6.5 79.6 %all-gather.3.cloned.1.call-start = ((), (), s32[]{:S(2)}) async-start(), calls=%async_computation.2 | async-start | bytes 10321920 | tf_op jit(solution)/shard_map/all_gather | solution.py:175
  32.9 117.8 %all-gather.5.cloned.1.call-start = ((), (), s32[]{:S(2)}) async-start(), calls=%async_computation.4 | async-start | bytes 10321920 | tf_op jit(solution)/shard_map/all_gather | solution.py:175
  55.4 159.4 %reduce-scatter.3.cloned.1.call-start = ((), (), s32[]{:S(2)}) async-start(), calls=%async_computation.3 | async-start | bytes 5734400 | tf_op jit(solution)/shard_map/reduce_scatter | solution.py:186
  150.5 115.1 %reduce-scatter.5.cloned.1.call-start = ((), (), s32[]{:S(2)}) async-start(), calls=%async_computation.5 | async-start | bytes 5734400 | tf_op jit(solution)/shard_map/reduce_scatter | solution.py:186
  288.7 5.7 %copy-start.3 = (f32[128]{0:T(128)S(1)}, f32[128]{0:T(128)}, u32[]{:S(2)}) copy-start(f32[128]{0:T(128)} %param.9) | copy-start | bytes 1540
  292.1 2.4 copy-start.2
  292.1 4.3 %copy-start.1 = (bf16[128,7168]{1,0:T(8,128)(2,1)S(1)}, bf16[128,7168]{1,0:T(8,128)(2,1)}, u32[]{:S(2)}) copy-start(bf16[128,7168]{1,0:T(8,128)(2,1)} %param.7) | copy-start | bytes 5505028
Sparse Core Ops, SparseCore 0:
  33.1 53.0 all-gather.2
  87.8 53.2 all-gather.4
  150.6 50.8 reduce-scatter.2
  214.8 50.7 reduce-scatter.4

commit v15 on v13

--- a/solution.py
+++ b/solution.py
@@ -18,8 +18,8 @@
 def chunk_orders(groups):
     if groups == 16:
         return [
-            [(0, 0), (0, 1), (0, 3), (1, 0), (3, 0), (1, 2), (3, 2), (2, 2)],
-            [(0, 2), (2, 0), (1, 1), (3, 3), (1, 3), (3, 1), (2, 1), (2, 3)],
+            [(0, 0), (0, 2), (2, 0), (2, 2), (1, 2), (3, 2), (2, 1), (2, 3)],
+            [(0, 1), (0, 3), (1, 0), (3, 0), (1, 1), (3, 3), (1, 3), (3, 1)],
         ]
     pairs = [((0, k), (0, groups - k)) for k in range(1, (groups + 1) // 2)]
     first = [(0, 0)] + ([(0, groups // 2)] if groups % 2 == 0 and groups > 1 else [])

time: 286 us -> 285 us (level)
    reduce_scatter x2, waiting for transfers between devices: 30.6 us -> 24.2 us  [body(): lax.psum_scatter(pair_sum.astype(jnp.bfloat16).reshape((-1,) + slab), 'in...]
    all_gather x2, waiting for transfers between devices: 32.2 us -> 38.5 us  [body(): gathered = lax.all_gather(rows, 'inner', axis=0, tiled=True)]
where the time goes in v15:
time: 285 us; the launch traced here: 284 us
  Pallas kernels  101 us (35%)
  waiting for transfers between devices  62.7 us (22%)
  matrix products  59 us (21%)
  local copies, waits for them, and re-layouts  29.9 us (10%)
  other arithmetic  18 us (6%)
  between operations  13.3 us (5%)
    pallas_call x4, Pallas kernels, group_exchange(): pl.pallas_call(functools.partial(exchange_kernel, groups, tuple(offsets),...  84.8 us
    dot_general x2, matrix products, expert_part(): return jnp.dot(hidden, down_mat, preferred_element_type=jnp.float32)  39.6 us
    all_gather x2, waiting for transfers between devices, body(): gathered = lax.all_gather(rows, 'inner', axis=0, tiled=True)  38.5 us
    reduce_scatter x2, waiting for transfers between devices, body(): lax.psum_scatter(pair_sum.astype(jnp.bfloat16).reshape((-1,) + slab), 'in...  24.2 us
    pallas_call x2, Pallas kernels, partner_swap(): pl.pallas_call(swap_kernel, out_shape=jax.ShapeDtypeStruct(x.shape[:1] +...  16.2 us
    convert_element_type x2, other arithmetic, body(): pair_sum.astype(jnp.bfloat16).reshape((-1,) + slab)  15.4 us
    reshape x2, local copies, waits for them, and re-layouts, body(): pair_sum.astype(jnp.bfloat16).reshape((-1,) + slab)  15.4 us
    dot_general x2, matrix products, expert_part(): gate_pre = jnp.dot(rows_in, gate_mat, preferred_element_type=jnp.float32)  14.3 us
  transfers between devices with their start and end apart: 4, of which 4 were waited for; matrix products, arithmetic and copies ran while one was open for 32% of the time, Pallas kernels for 20%

profile of v15, /device:TPU:0, one launch (start us, length us, event | category | flops | bytes accessed | tf_op | source)
XLA Modules:
  0.0 284.3 jit_solution(9898751849035281882)
XLA Ops:
  6.5 0.9 fusion.43
  7.6 0.8 select_reduce_fusion
  8.4 0.7 compare_select_fusion.23
  9.1 0.7 convolution_convert_fusion.2
  10.0 1.4 reshape.44.x_ref
  11.4 26.4 %shard_map.73 = bf16[8,560,128]{2,1,0:T(8,128)(2,1)} custom-call(bf16[8,560,128]{2,1,0:T(8,128)(2,1)} %reshape.44.x_ref), custom_call_target="tpu_custom_call" | custom-call | tf_op jit(solution)/shard_map/pallas_call | solution.py:90
  37.8 2.4 reshape.45
  40.2 1.4 reshape.50.x_ref
  41.6 15.4 %shard_map.76 = bf16[8,560,128]{2,1,0:T(8,128)(2,1)} custom-call(bf16[8,560,128]{2,1,0:T(8,128)(2,1)} %reshape.50.x_ref), custom_call_target="tpu_custom_call" | custom-call | tf_op jit(solution)/shard_map/pallas_call | solution.py:90
  57.0 2.4 reshape.51
  59.4 0.2 reduce-scatter.3.cloned.1.call-start
  59.7 34.4 %all-gather.3.cloned.1.call-done = bf16[640,7168]{1,0:T(8,128)(2,1)} async-done(((bf16[80,7168]{1,0:T(8,128)(2,1)}), bf16[640,7168]{1,0:T(8,128)(2,1)}) %all-gather.3.cloned.1.call-update) | async-done | bytes 9175056 | tf_op jit(solution)/shard_map/all_gather | solution.py:176
  94.0 7.2 %fusion.13 = f32[640,256]{1,0:T(8,128)S(1)} fusion(bf16[640,7168]{1,0:T(8,128)(2,1)} %all-gather.3.cloned.1.call-done, bf16[1,7168,256]{2,1,0:T(8,128)(2,1)} %param.10), kind=kOutput, calls=%fused_computation.20 | convolution fusion | flops 2348810240 | bytes 13500416 | tf_op jit(solution)/shard_map/dot_general | solution.py:137
  101.2 19.8 %convolution_convert_fusion.1 = bf16[640,7168]{1,0:T(8,128)(2,1)} fusion(bf16[1,256,7168]{2,1,0:T(8,128)(2,1)} %param.12, bf16[640,7168]{1,0:T(8,128)(2,1)} %all-gather.3.cloned.1.call-done, bf16[1,7168,256]{2,1,0:T(8,128)(2,1)} %param.11, f32[640,256]{1,0:T(8,128)S(1)} %fusion.13), kind=kOutput, calls=%fused_computation.1 | convolution fusion | flops 4703191040 | bytes 26345472 | tf_op jit(solution)/shard_map/dot_general | solution.py:140
  121.1 8.1 %shard_map.74 = bf16[4,80,7168]{2,1,0:T(8,128)(2,1)} custom-call(bf16[4,2,80,7168]{3,2,1,0:T(8,128)(2,1)} %bitcast.56), custom_call_target="tpu_custom_call" | custom-call | tf_op jit(solution)/shard_map/pallas_call | solution.py:126
  129.1 7.8 %fusion.1 = bf16[4,80,7168]{2,1,0:T(8,128)(2,1)} fusion(bf16[4,80,7168]{2,1,0:T(8,128)(2,1)} %shard_map.74, bf16[4,2,80,7168]{3,2,1,0:T(8,128)(2,1)} %bitcast.57, s32[]{:T(128)S(6)} %select_n.30), kind=kLoop, calls=%fused_computation.5 | loop fusion | flops 9175040 | bytes 13762564 | tf_op jit(solution)/shard_map/convert_element_type | solution.py:187
  136.9 7.7 %reshape.47 = bf16[32,560,128]{2,1,0:T(8,128)(2,1)} reshape(bf16[4,80,7168]{2,1,0:T(8,128)(2,1)} %fusion.1) | data formatting | bytes 9175040 | tf_op jit(solution)/shard_map/reshape | solution.py:187
  144.6 0.3 reduce-scatter.5.cloned.1.call-start
  144.9 4.1 %all-gather.5.cloned.1.call-done = bf16[640,7168]{1,0:T(8,128)(2,1)} async-done(((bf16[80,7168]{1,0:T(8,128)(2,1)}), bf16[640,7168]{1,0:T(8,128)(2,1)}) %all-gather.5.cloned.1.call-update) | async-done | bytes 9175056 | tf_op jit(solution)/shard_map/all_gather | solution.py:176
  149.0 7.2 %fusion.11 = f32[640,256]{1,0:T(8,128)S(1)} fusion(bf16[640,7168]{1,0:T(8,128)(2,1)} %all-gather.5.cloned.1.call-done, bf16[1,7168,256]{2,1,0:T(8,128)(2,1)} %param.10), kind=kOutput, calls=%fused_computation.18 | convolution fusion | flops 2348810240 | bytes 13500416 | tf_op jit(solution)/shard_map/dot_general | solution.py:137
  156.2 19.8 %convolution_convert_fusion = bf16[640,7168]{1,0:T(8,128)(2,1)} fusion(bf16[1,256,7168]{2,1,0:T(8,128)(2,1)} %param.12, bf16[640,7168]{1,0:T(8,128)(2,1)} %all-gather.5.cloned.1.call-done, bf16[1,7168,256]{2,1,0:T(8,128)(2,1)} %param.11, f32[640,256]{1,0:T(8,128)S(1)} %fusion.11), kind=kOutput, calls=%fused_computation | convolution fusion | flops 4703191040 | bytes 26345472 | tf_op jit(solution)/shard_map/dot_general | solution.py:140
  175.9 8.1 %shard_map.77 = bf16[4,80,7168]{2,1,0:T(8,128)(2,1)} custom-call(bf16[4,2,80,7168]{3,2,1,0:T(8,128)(2,1)} %bitcast.54), custom_call_target="tpu_custom_call" | custom-call | tf_op jit(solution)/shard_map/pallas_call | solution.py:126
  184.0 7.6 %fusion = bf16[4,80,7168]{2,1,0:T(8,128)(2,1)} fusion(bf16[4,80,7168]{2,1,0:T(8,128)(2,1)} %shard_map.77, bf16[4,2,80,7168]{3,2,1,0:T(8,128)(2,1)} %bitcast.55, s32[]{:T(128)S(6)} %select_n.30), kind=kLoop, calls=%fused_computation.3 | loop fusion | flops 9175040 | bytes 13762564 | tf_op jit(solution)/shard_map/convert_element_type | solution.py:187
  191.6 7.7 %reshape.53 = bf16[32,560,128]{2,1,0:T(8,128)(2,1)} reshape(bf16[4,80,7168]{2,1,0:T(8,128)(2,1)} %fusion) | data formatting | bytes 9175040 | tf_op jit(solution)/shard_map/reshape | solution.py:187
  199.4 2.2 reduce-scatter.3.cloned.1.call-done.x_ref
  201.7 26.7 %shard_map.75 = bf16[8,560,128]{2,1,0:T(8,128)(2,1)} custom-call(bf16[8,560,128]{2,1,0:T(8,128)(2,1)} %reduce-scatter.3.cloned.1.call-done.x_ref), custom_call_target="tpu_custom_call" | custom-call | tf_op jit(solution)/shard_map/pallas_call | solution.py:90
  228.4 3.4 %reshape.48 = bf16[8,10,7168]{2,1,0:T(8,128)(2,1)} reshape(bf16[8,560,128]{2,1,0:T(8,128)(2,1)} %shard_map.75) | data formatting | bytes 2293760 | tf_op jit(solution)/shard_map/reshape | solution.py:207
  231.8 21.9 %reduce-scatter.5.cloned.1.call-done.x_ref = bf16[8,560,128]{2,1,0:T(8,128)(2,1)} async-done(((bf16[32,560,128]{2,1,0:T(8,128)(2,1)}), bf16[8,560,128]{2,1,0:T(8,128)(2,1)}) %reduce-scatter.5.cloned.1.call-update) | async-done | bytes 1146896 | tf_op jit(solution)/shard_map/reduce_scatter | solution.py:186
  253.7 16.3 %shard_map.78 = bf16[8,560,128]{2,1,0:T(8,128)(2,1)} custom-call(bf16[8,560,128]{2,1,0:T(8,128)(2,1)} %reduce-scatter.5.cloned.1.call-done.x_ref), custom_call_target="tpu_custom_call" | custom-call | tf_op jit(solution)/shard_map/pallas_call | solution.py:90
  270.0 3.4 %reshape.54 = bf16[8,10,7168]{2,1,0:T(8,128)(2,1)} reshape(bf16[8,560,128]{2,1,0:T(8,128)(2,1)} %shard_map.78) | data formatting | bytes 2293760 | tf_op jit(solution)/shard_map/reshape | solution.py:207
  273.4 2.3 convolution_bitcast_fusion
  275.8 1.9 fusion.4
  (20 shorter events, 0.5 us)
Async XLA Ops:
  6.5 2.6 copy-start
  6.5 87.5 %all-gather.3.cloned.1.call-start = ((), (), s32[]{:S(2)}) async-start(), calls=%async_computation.2 | async-start | bytes 10321920 | tf_op jit(solution)/shard_map/all_gather | solution.py:176
  40.2 108.8 %all-gather.5.cloned.1.call-start = ((), (), s32[]{:S(2)}) async-start(), calls=%async_computation.4 | async-start | bytes 10321920 | tf_op jit(solution)/shard_map/all_gather | solution.py:176
  59.4 142.2 %reduce-scatter.3.cloned.1.call-start = ((), (), s32[]{:S(2)}) async-start(), calls=%async_computation.3 | async-start | bytes 5734400 | tf_op jit(solution)/shard_map/reduce_scatter | solution.py:186
  144.6 109.1 %reduce-scatter.5.cloned.1.call-start = ((), (), s32[]{:S(2)}) async-start(), calls=%async_computation.5 | async-start | bytes 5734400 | tf_op jit(solution)/shard_map/reduce_scatter | solution.py:186
  270.0 5.7 %copy-start.3 = (f32[128]{0:T(128)S(1)}, f32[128]{0:T(128)}, u32[]{:S(2)}) copy-start(f32[128]{0:T(128)} %param.9) | copy-start | bytes 1540
  273.4 2.4 copy-start.2
  273.4 4.3 %copy-start.1 = (bf16[128,7168]{1,0:T(8,128)(2,1)S(1)}, bf16[128,7168]{1,0:T(8,128)(2,1)}, u32[]{:S(2)}) copy-start(bf16[128,7168]{1,0:T(8,128)(2,1)} %param.7) | copy-start | bytes 5505028
Sparse Core Ops, SparseCore 0:
  40.3 53.6 all-gather.2
  95.7 53.2 all-gather.4
  151.4 50.2 reduce-scatter.2
  203.9 49.7 reduce-scatter.4

commit v16 on v15

--- a/solution.py
+++ b/solution.py
@@ -198,6 +198,8 @@
     expert_out = None
     base = 0
     for z, chunk, index in returned:
+        if expert_out is not None:
+            z, expert_out = lax.optimization_barrier((z, expert_out))
         back_rows = group_exchange(z, chunk, 0, -1, 2 * index + 1)
         term = jnp.einsum(
             "gct,gcd->td",

time: 285 us -> 285 us (level)
  transfers between devices with their start and end apart: 4 -> 4, of which waited for: 4 -> 4; matrix products, arithmetic and copies ran while one was open for 32% -> 33% of each run, Pallas kernels for 20% -> 20%
where the time goes in v16:
time: 285 us
  Pallas kernels  101 us (35%)
  matrix products  61.7 us (22%)
  waiting for transfers between devices  61.2 us (21%)
  local copies, waits for them, and re-layouts  29 us (10%)
  other arithmetic  18 us (6%)
  between operations  13.3 us (5%)
    pallas_call x4, Pallas kernels, group_exchange(): pl.pallas_call(functools.partial(exchange_kernel, groups, tuple(offsets),...  84.8 us
    dot_general x2, matrix products, expert_part(): return jnp.dot(hidden, down_mat, preferred_element_type=jnp.float32)  39.6 us
    all_gather x2, waiting for transfers between devices, body(): gathered = lax.all_gather(rows, 'inner', axis=0, tiled=True)  38.5 us
    reduce_scatter x2, waiting for transfers between devices, body(): lax.psum_scatter(pair_sum.astype(jnp.bfloat16).reshape((-1,) + slab), 'in...  22.6 us
    pallas_call x2, Pallas kernels, partner_swap(): pl.pallas_call(swap_kernel, out_shape=jax.ShapeDtypeStruct(x.shape[:1] +...  16.2 us
    convert_element_type x2, other arithmetic, body(): pair_sum.astype(jnp.bfloat16).reshape((-1,) + slab)  15.4 us
    reshape x2, local copies, waits for them, and re-layouts, body(): pair_sum.astype(jnp.bfloat16).reshape((-1,) + slab)  15.3 us
    dot_general x2, matrix products, expert_part(): gate_pre = jnp.dot(rows_in, gate_mat, preferred_element_type=jnp.float32)  14.4 us
  transfers between devices with their start and end apart: 4, of which 4 were waited for; matrix products, arithmetic and copies ran while one was open for 33% of the time, Pallas kernels for 20%

profile of v16, /device:TPU:0, one launch (start us, length us, event | category | flops | bytes accessed | tf_op | source)
XLA Modules:
  0.0 284.6 jit_solution(7775100218284492850)
XLA Ops:
  6.5 0.9 fusion.43
  7.6 0.8 select_reduce_fusion
  8.4 0.7 compare_select_fusion.23
  9.1 0.7 convolution_convert_fusion.2
  10.0 1.4 reshape.48.x_ref
  11.4 26.4 %shard_map.75 = bf16[8,560,128]{2,1,0:T(8,128)(2,1)} custom-call(bf16[8,560,128]{2,1,0:T(8,128)(2,1)} %reshape.48.x_ref), custom_call_target="tpu_custom_call" | custom-call | tf_op jit(solution)/shard_map/pallas_call | solution.py:90
  37.8 2.4 reshape.49
  40.2 1.4 reshape.43.x_ref
  41.6 15.4 %shard_map.73 = bf16[8,560,128]{2,1,0:T(8,128)(2,1)} custom-call(bf16[8,560,128]{2,1,0:T(8,128)(2,1)} %reshape.43.x_ref), custom_call_target="tpu_custom_call" | custom-call | tf_op jit(solution)/shard_map/pallas_call | solution.py:90
  57.1 2.4 reshape.44
  59.5 0.2 reduce-scatter.5.cloned.1.call-start
  59.7 34.3 %all-gather.5.cloned.1.call-done = bf16[640,7168]{1,0:T(8,128)(2,1)} async-done(((bf16[80,7168]{1,0:T(8,128)(2,1)}), bf16[640,7168]{1,0:T(8,128)(2,1)}) %all-gather.5.cloned.1.call-update) | async-done | bytes 9175056 | tf_op jit(solution)/shard_map/all_gather | solution.py:176
  94.0 7.2 %fusion.11 = f32[640,256]{1,0:T(8,128)S(1)} fusion(bf16[640,7168]{1,0:T(8,128)(2,1)} %all-gather.5.cloned.1.call-done, bf16[1,7168,256]{2,1,0:T(8,128)(2,1)} %param.10), kind=kOutput, calls=%fused_computation.18 | convolution fusion | flops 2348810240 | bytes 13500416 | tf_op jit(solution)/shard_map/dot_general | solution.py:137
  101.2 19.8 %convolution_convert_fusion = bf16[640,7168]{1,0:T(8,128)(2,1)} fusion(bf16[1,256,7168]{2,1,0:T(8,128)(2,1)} %param.12, bf16[640,7168]{1,0:T(8,128)(2,1)} %all-gather.5.cloned.1.call-done, bf16[1,7168,256]{2,1,0:T(8,128)(2,1)} %param.11, f32[640,256]{1,0:T(8,128)S(1)} %fusion.11), kind=kOutput, calls=%fused_computation | convolution fusion | flops 4703191040 | bytes 26345472 | tf_op jit(solution)/shard_map/dot_general | solution.py:140
  121.0 8.1 %shard_map.76 = bf16[4,80,7168]{2,1,0:T(8,128)(2,1)} custom-call(bf16[4,2,80,7168]{3,2,1,0:T(8,128)(2,1)} %bitcast.56), custom_call_target="tpu_custom_call" | custom-call | tf_op jit(solution)/shard_map/pallas_call | solution.py:126
  129.1 7.8 %fusion = bf16[4,80,7168]{2,1,0:T(8,128)(2,1)} fusion(bf16[4,80,7168]{2,1,0:T(8,128)(2,1)} %shard_map.76, bf16[4,2,80,7168]{3,2,1,0:T(8,128)(2,1)} %bitcast.57, s32[]{:T(128)S(6)} %select_n.30), kind=kLoop, calls=%fused_computation.3 | loop fusion | flops 9175040 | bytes 13762564 | tf_op jit(solution)/shard_map/convert_element_type | solution.py:187
  136.9 7.7 %reshape.51 = bf16[32,560,128]{2,1,0:T(8,128)(2,1)} reshape(bf16[4,80,7168]{2,1,0:T(8,128)(2,1)} %fusion) | data formatting | bytes 9175040 | tf_op jit(solution)/shard_map/reshape | solution.py:187
  144.6 0.3 reduce-scatter.3.cloned.1.call-start
  144.9 4.1 %all-gather.3.cloned.1.call-done = bf16[640,7168]{1,0:T(8,128)(2,1)} async-done(((bf16[80,7168]{1,0:T(8,128)(2,1)}), bf16[640,7168]{1,0:T(8,128)(2,1)}) %all-gather.3.cloned.1.call-update) | async-done | bytes 9175056 | tf_op jit(solution)/shard_map/all_gather | solution.py:176
  149.0 7.2 %fusion.13 = f32[640,256]{1,0:T(8,128)S(1)} fusion(bf16[640,7168]{1,0:T(8,128)(2,1)} %all-gather.3.cloned.1.call-done, bf16[1,7168,256]{2,1,0:T(8,128)(2,1)} %param.10), kind=kOutput, calls=%fused_computation.20 | convolution fusion | flops 2348810240 | bytes 13500416 | tf_op jit(solution)/shard_map/dot_general | solution.py:137
  156.1 19.8 %convolution_convert_fusion.1 = bf16[640,7168]{1,0:T(8,128)(2,1)} fusion(bf16[1,256,7168]{2,1,0:T(8,128)(2,1)} %param.12, bf16[640,7168]{1,0:T(8,128)(2,1)} %all-gather.3.cloned.1.call-done, bf16[1,7168,256]{2,1,0:T(8,128)(2,1)} %param.11, f32[640,256]{1,0:T(8,128)S(1)} %fusion.13), kind=kOutput, calls=%fused_computation.1 | convolution fusion | flops 4703191040 | bytes 26345472 | tf_op jit(solution)/shard_map/dot_general | solution.py:140
  175.9 8.1 %shard_map.74 = bf16[4,80,7168]{2,1,0:T(8,128)(2,1)} custom-call(bf16[4,2,80,7168]{3,2,1,0:T(8,128)(2,1)} %bitcast.54), custom_call_target="tpu_custom_call" | custom-call | tf_op jit(solution)/shard_map/pallas_call | solution.py:126
  184.0 7.6 %fusion.1 = bf16[4,80,7168]{2,1,0:T(8,128)(2,1)} fusion(bf16[4,80,7168]{2,1,0:T(8,128)(2,1)} %shard_map.74, bf16[4,2,80,7168]{3,2,1,0:T(8,128)(2,1)} %bitcast.55, s32[]{:T(128)S(6)} %select_n.30), kind=kLoop, calls=%fused_computation.5 | loop fusion | flops 9175040 | bytes 13762564 | tf_op jit(solution)/shard_map/convert_element_type | solution.py:187
  191.7 7.7 %reshape.46 = bf16[32,560,128]{2,1,0:T(8,128)(2,1)} reshape(bf16[4,80,7168]{2,1,0:T(8,128)(2,1)} %fusion.1) | data formatting | bytes 9175040 | tf_op jit(solution)/shard_map/reshape | solution.py:187
  199.4 2.2 reduce-scatter.5.cloned.1.call-done.x_ref
  201.7 26.7 %shard_map.77 = bf16[8,560,128]{2,1,0:T(8,128)(2,1)} custom-call(bf16[8,560,128]{2,1,0:T(8,128)(2,1)} %reduce-scatter.5.cloned.1.call-done.x_ref), custom_call_target="tpu_custom_call" | custom-call | tf_op jit(solution)/shard_map/pallas_call | solution.py:90
  228.3 2.4 reshape.52
  230.8 2.5 convolution_bitcast_fusion.1
  233.3 20.4 %reduce-scatter.3.cloned.1.call-done.x_ref = bf16[8,560,128]{2,1,0:T(8,128)(2,1)} async-done(((bf16[32,560,128]{2,1,0:T(8,128)(2,1)}), bf16[8,560,128]{2,1,0:T(8,128)(2,1)}) %reduce-scatter.3.cloned.1.call-update) | async-done | bytes 1146896 | tf_op jit(solution)/shard_map/reduce_scatter | solution.py:186
  253.7 16.3 %shard_map.78 = bf16[8,560,128]{2,1,0:T(8,128)(2,1)} custom-call(bf16[8,560,128]{2,1,0:T(8,128)(2,1)} %reduce-scatter.3.cloned.1.call-done.x_ref), custom_call_target="tpu_custom_call" | custom-call | tf_op jit(solution)/shard_map/pallas_call | solution.py:90
  270.0 3.5 %reshape.54 = bf16[8,10,7168]{2,1,0:T(8,128)(2,1)} reshape(bf16[8,560,128]{2,1,0:T(8,128)(2,1)} %shard_map.78) | data formatting | bytes 2293760 | tf_op jit(solution)/shard_map/reshape | solution.py:209
  273.5 4.5 %fusion.4 = bf16[128,7168]{1,0:T(8,128)(2,1)} fusion(f32[128,7168]{1,0:T(8,128)} %convolution_bitcast_fusion.1, pred[8,10,128]{2,1,0:T(8,128)(4,1)S(1)} %reshape.53, bf16[8,10,7168]{2,1,0:T(8,128)(2,1)} %reshape.54, f32[128]{0:T(128)S(1)} %copy-done.2), kind=kOutput, calls=%fused_computation.11 | convolution fusion | flops 149553152 | bytes 6662656 | tf_op jit(solution)/shard_map/gct,gcd->td/dot_general | solution.py:204
  (18 shorter events, 0.5 us)
Async XLA Ops:
  6.5 2.6 copy-start
  6.5 87.5 %all-gather.5.cloned.1.call-start = ((), (), s32[]{:S(2)}) async-start(), calls=%async_computation.4 | async-start | bytes 10321920 | tf_op jit(solution)/shard_map/all_gather | solution.py:176
  40.2 108.8 %all-gather.3.cloned.1.call-start = ((), (), s32[]{:S(2)}) async-start(), calls=%async_computation.2 | async-start | bytes 10321920 | tf_op jit(solution)/shard_map/all_gather | solution.py:176
  59.5 142.2 %reduce-scatter.5.cloned.1.call-start = ((), (), s32[]{:S(2)}) async-start(), calls=%async_computation.5 | async-start | bytes 5734400 | tf_op jit(solution)/shard_map/reduce_scatter | solution.py:186
  144.6 109.1 %reduce-scatter.3.cloned.1.call-start = ((), (), s32[]{:S(2)}) async-start(), calls=%async_computation.3 | async-start | bytes 5734400 | tf_op jit(solution)/shard_map/reduce_scatter | solution.py:186
  233.3 40.3 %copy-start.2 = (f32[128]{0:T(128)S(1)}, f32[128]{0:T(128)}, u32[]{:S(2)}) copy-start(f32[128]{0:T(128)} %param.9) | copy-start | bytes 1540
  270.0 8.1 %copy-start.1 = (bf16[128,7168]{1,0:T(8,128)(2,1)S(1)}, bf16[128,7168]{1,0:T(8,128)(2,1)}, u32[]{:S(2)}) copy-start(bf16[128,7168]{1,0:T(8,128)(2,1)} %param.7) | copy-start | bytes 5505028
Sparse Core Ops, SparseCore 0:
  40.3 53.6 all-gather.4
  95.7 53.2 all-gather.2
  151.4 50.2 reduce-scatter.4
  203.9 49.7 reduce-scatter.2

commit v17 on v15

--- a/solution.py
+++ b/solution.py
@@ -48,12 +48,9 @@
         )
     if peers:
         pl.semaphore_wait(barrier, len(peers))
-    local = None
     sends = []
     for i, k in enumerate(offsets):
         if k == (0, 0):
-            local = pltpu.make_async_copy(x_ref.at[src_base + i], y_ref.at[i], local_sem)
-            local.start()
             continue
         dest = peer_of(me, k, sign, groups)
         copy = pltpu.make_async_remote_copy(
@@ -80,14 +77,12 @@
             device_id=(source, inner),
             device_id_type=MESH,
         ).wait_recv()
-    if local is not None:
-        local.wait()
 
 
 def group_exchange(x, offsets, src_base, sign, collective_id):
     groups = lax.axis_size("group")
     count = len(offsets)
-    return pl.pallas_call(
+    out = pl.pallas_call(
         functools.partial(exchange_kernel, groups, tuple(offsets), src_base, sign),
         out_shape=jax.ShapeDtypeStruct((count,) + x.shape[1:], x.dtype),
         in_specs=[pl.BlockSpec(memory_space=pl.ANY)],
@@ -99,6 +94,10 @@
         ],
         compiler_params=pltpu.CompilerParams(collective_id=collective_id, has_side_effects=True),
     )(x)
+    for i, k in enumerate(offsets):
+        if k == (0, 0):
+            out = out.at[i].set(x[src_base + i])
+    return out
 
 
 def swap_kernel(x_ref, y_ref, send_sem, recv_sem):

time: 285 us -> 287 us (level)
  local copies, waits for them, and re-layouts: 29.9 us -> 33.4 us
  transfers between devices with their start and end apart: 4 -> 4, of which waited for: 4 -> 4; matrix products, arithmetic and copies ran while one was open for 32% -> 33% of each run, Pallas kernels for 20% -> 20%
where the time goes in v17:
time: 287 us; the launch traced here: 286 us
  Pallas kernels  101 us (35%)
  waiting for transfers between devices  61.2 us (21%)
  matrix products  59 us (21%)
  local copies, waits for them, and re-layouts  33.4 us (12%)
  other arithmetic  17.9 us (6%)
  between operations  13.3 us (5%)
    pallas_call x4, Pallas kernels, group_exchange(): pl.pallas_call(functools.partial(exchange_kernel, groups, tuple(offsets),...  84.8 us
    dot_general x2, matrix products, expert_part(): return jnp.dot(hidden, down_mat, preferred_element_type=jnp.float32)  39.6 us
    all_gather x2, waiting for transfers between devices, body(): gathered = lax.all_gather(rows, 'inner', axis=0, tiled=True)  38.5 us
    reduce_scatter x2, waiting for transfers between devices, body(): lax.psum_scatter(pair_sum.astype(jnp.bfloat16).reshape((-1,) + slab), 'in...  22.7 us
    pallas_call x2, Pallas kernels, partner_swap(): pl.pallas_call(swap_kernel, out_shape=jax.ShapeDtypeStruct(x.shape[:1] +...  16.2 us
    convert_element_type x2, other arithmetic, body(): pair_sum.astype(jnp.bfloat16).reshape((-1,) + slab)  15.4 us
    reshape x2, local copies, waits for them, and re-layouts, body(): pair_sum.astype(jnp.bfloat16).reshape((-1,) + slab)  15.3 us
    dot_general x2, matrix products, expert_part(): gate_pre = jnp.dot(rows_in, gate_mat, preferred_element_type=jnp.float32)  14.3 us
  transfers between devices with their start and end apart: 4, of which 4 were waited for; matrix products, arithmetic and copies ran while one was open for 33% of the time, Pallas kernels for 20%

profile of v17, /device:TPU:0, one launch (start us, length us, event | category | flops | bytes accessed | tf_op | source)
XLA Modules:
  0.0 286.3 jit_solution(2732987737540051230)
XLA Ops:
  6.5 0.9 fusion.43
  7.6 0.8 select_reduce_fusion
  8.4 0.7 compare_select_fusion.23
  9.1 0.7 convolution_convert_fusion.2
  10.1 1.2 copy-done.2
  11.3 1.3 reshape.106.x_ref
  12.6 26.4 %shard_map.73 = bf16[8,560,128]{2,1,0:T(8,128)(2,1)} custom-call(bf16[8,560,128]{2,1,0:T(8,128)(2,1)} %reshape.106.x_ref), custom_call_target="tpu_custom_call" | custom-call | tf_op jit(solution)/shard_map/pallas_call | solution.py:85
  39.8 2.4 reshape.108
  42.2 1.4 reshape.113.x_ref
  43.6 15.4 %shard_map.76 = bf16[8,560,128]{2,1,0:T(8,128)(2,1)} custom-call(bf16[8,560,128]{2,1,0:T(8,128)(2,1)} %reshape.113.x_ref), custom_call_target="tpu_custom_call" | custom-call | tf_op jit(solution)/shard_map/pallas_call | solution.py:85
  59.0 2.4 reshape.114
  61.7 34.4 %all-gather.3.cloned.1.call-done = bf16[640,7168]{1,0:T(8,128)(2,1)} async-done(((bf16[80,7168]{1,0:T(8,128)(2,1)}), bf16[640,7168]{1,0:T(8,128)(2,1)}) %all-gather.3.cloned.1.call-update) | async-done | bytes 9175056 | tf_op jit(solution)/shard_map/all_gather | solution.py:175
  96.0 7.2 %fusion.13 = f32[640,256]{1,0:T(8,128)S(1)} fusion(bf16[640,7168]{1,0:T(8,128)(2,1)} %all-gather.3.cloned.1.call-done, bf16[1,7168,256]{2,1,0:T(8,128)(2,1)} %param.14), kind=kOutput, calls=%fused_computation.20 | convolution fusion | flops 2348810240 | bytes 13500416 | tf_op jit(solution)/shard_map/dot_general | solution.py:136
  103.2 19.8 %convolution_convert_fusion.1 = bf16[640,7168]{1,0:T(8,128)(2,1)} fusion(bf16[1,256,7168]{2,1,0:T(8,128)(2,1)} %param.16, bf16[640,7168]{1,0:T(8,128)(2,1)} %all-gather.3.cloned.1.call-done, bf16[1,7168,256]{2,1,0:T(8,128)(2,1)} %param.15, f32[640,256]{1,0:T(8,128)S(1)} %fusion.13), kind=kOutput, calls=%fused_computation.1 | convolution fusion | flops 4703191040 | bytes 26345472 | tf_op jit(solution)/shard_map/dot_general | solution.py:139
  123.1 8.1 %shard_map.74 = bf16[4,80,7168]{2,1,0:T(8,128)(2,1)} custom-call(bf16[4,2,80,7168]{3,2,1,0:T(8,128)(2,1)} %bitcast.56), custom_call_target="tpu_custom_call" | custom-call | tf_op jit(solution)/shard_map/pallas_call | solution.py:125
  131.2 7.8 %fusion.1 = bf16[4,80,7168]{2,1,0:T(8,128)(2,1)} fusion(bf16[4,80,7168]{2,1,0:T(8,128)(2,1)} %shard_map.74, bf16[4,2,80,7168]{3,2,1,0:T(8,128)(2,1)} %bitcast.57, s32[]{:T(128)S(6)} %select_n.30), kind=kLoop, calls=%fused_computation.5 | loop fusion | flops 9175040 | bytes 13762564 | tf_op jit(solution)/shard_map/convert_element_type | solution.py:186
  138.9 7.7 %reshape.110 = bf16[32,560,128]{2,1,0:T(8,128)(2,1)} reshape(bf16[4,80,7168]{2,1,0:T(8,128)(2,1)} %fusion.1) | data formatting | bytes 9175040 | tf_op jit(solution)/shard_map/reshape | solution.py:186
  146.9 4.1 %all-gather.5.cloned.1.call-done = bf16[640,7168]{1,0:T(8,128)(2,1)} async-done(((bf16[80,7168]{1,0:T(8,128)(2,1)}), bf16[640,7168]{1,0:T(8,128)(2,1)}) %all-gather.5.cloned.1.call-update) | async-done | bytes 9175056 | tf_op jit(solution)/shard_map/all_gather | solution.py:175
  151.0 7.2 %fusion.11 = f32[640,256]{1,0:T(8,128)S(1)} fusion(bf16[640,7168]{1,0:T(8,128)(2,1)} %all-gather.5.cloned.1.call-done, bf16[1,7168,256]{2,1,0:T(8,128)(2,1)} %param.14), kind=kOutput, calls=%fused_computation.18 | convolution fusion | flops 2348810240 | bytes 13500416 | tf_op jit(solution)/shard_map/dot_general | solution.py:136
  158.2 19.8 %convolution_convert_fusion = bf16[640,7168]{1,0:T(8,128)(2,1)} fusion(bf16[1,256,7168]{2,1,0:T(8,128)(2,1)} %param.16, bf16[640,7168]{1,0:T(8,128)(2,1)} %all-gather.5.cloned.1.call-done, bf16[1,7168,256]{2,1,0:T(8,128)(2,1)} %param.15, f32[640,256]{1,0:T(8,128)S(1)} %fusion.11), kind=kOutput, calls=%fused_computation | convolution fusion | flops 4703191040 | bytes 26345472 | tf_op jit(solution)/shard_map/dot_general | solution.py:139
  177.9 8.1 %shard_map.77 = bf16[4,80,7168]{2,1,0:T(8,128)(2,1)} custom-call(bf16[4,2,80,7168]{3,2,1,0:T(8,128)(2,1)} %bitcast.54), custom_call_target="tpu_custom_call" | custom-call | tf_op jit(solution)/shard_map/pallas_call | solution.py:125
  186.0 7.6 %fusion = bf16[4,80,7168]{2,1,0:T(8,128)(2,1)} fusion(bf16[4,80,7168]{2,1,0:T(8,128)(2,1)} %shard_map.77, bf16[4,2,80,7168]{3,2,1,0:T(8,128)(2,1)} %bitcast.55, s32[]{:T(128)S(6)} %select_n.30), kind=kLoop, calls=%fused_computation.3 | loop fusion | flops 9175040 | bytes 13762564 | tf_op jit(solution)/shard_map/convert_element_type | solution.py:186
  193.6 7.7 %reshape.116 = bf16[32,560,128]{2,1,0:T(8,128)(2,1)} reshape(bf16[4,80,7168]{2,1,0:T(8,128)(2,1)} %fusion) | data formatting | bytes 9175040 | tf_op jit(solution)/shard_map/reshape | solution.py:186
  201.4 2.3 reduce-scatter.3.cloned.1.call-done.x_ref
  203.7 26.7 %shard_map.75 = bf16[8,560,128]{2,1,0:T(8,128)(2,1)} custom-call(bf16[8,560,128]{2,1,0:T(8,128)(2,1)} %reduce-scatter.3.cloned.1.call-done.x_ref), custom_call_target="tpu_custom_call" | custom-call | tf_op jit(solution)/shard_map/pallas_call | solution.py:85
  230.4 1.6 slice_dynamic-update-slice_fusion
  231.9 3.4 %reshape.111 = bf16[8,10,7168]{2,1,0:T(8,128)(2,1)} reshape(bf16[8,560,128]{2,1,0:T(8,128)(2,1)} %slice_dynamic-update-slice_fusion) | data formatting | bytes 2293760 | tf_op jit(solution)/shard_map/reshape | solution.py:206
  235.3 20.4 %reduce-scatter.5.cloned.1.call-done.x_ref = bf16[8,560,128]{2,1,0:T(8,128)(2,1)} async-done(((bf16[32,560,128]{2,1,0:T(8,128)(2,1)}), bf16[8,560,128]{2,1,0:T(8,128)(2,1)}) %reduce-scatter.5.cloned.1.call-update) | async-done | bytes 1146896 | tf_op jit(solution)/shard_map/reduce_scatter | solution.py:185
  255.7 16.3 %shard_map.78 = bf16[8,560,128]{2,1,0:T(8,128)(2,1)} custom-call(bf16[8,560,128]{2,1,0:T(8,128)(2,1)} %reduce-scatter.5.cloned.1.call-done.x_ref), custom_call_target="tpu_custom_call" | custom-call | tf_op jit(solution)/shard_map/pallas_call | solution.py:85
  272.0 3.4 %reshape.117 = bf16[8,10,7168]{2,1,0:T(8,128)(2,1)} reshape(bf16[8,560,128]{2,1,0:T(8,128)(2,1)} %shard_map.78) | data formatting | bytes 2293760 | tf_op jit(solution)/shard_map/reshape | solution.py:206
  275.4 2.3 convolution_bitcast_fusion
  277.8 1.9 fusion.4
  (27 shorter events, 1.8 us)
Async XLA Ops:
  6.5 2.6 copy-start
  6.5 89.5 %all-gather.3.cloned.1.call-start = ((), (), s32[]{:S(2)}) async-start(), calls=%async_computation.2 | async-start | bytes 10321920 | tf_op jit(solution)/shard_map/all_gather | solution.py:175
  9.9 1.4 copy-start.2
  11.3 27.7 %slice-start = ((bf16[160,7168]{1,0:T(8,128)(2,1)}), bf16[10,7168]{1,0:T(8,128)(2,1)S(1)}, s32[]{:S(2)}) async-start(bf16[160,7168]{1,0:T(8,128)(2,1)} %copy-done.2), calls=%async_computation.6 | async-start | bytes 458752 | tf_op jit(solution)/shard_map/slice | solution.py:99
  42.2 108.8 %all-gather.5.cloned.1.call-start = ((), (), s32[]{:S(2)}) async-start(), calls=%async_computation.4 | async-start | bytes 10321920 | tf_op jit(solution)/shard_map/all_gather | solution.py:175
  61.4 142.2 %reduce-scatter.3.cloned.1.call-start = ((), (), s32[]{:S(2)}) async-start(), calls=%async_computation.3 | async-start | bytes 5734400 | tf_op jit(solution)/shard_map/reduce_scatter | solution.py:185
  146.6 109.1 %reduce-scatter.5.cloned.1.call-start = ((), (), s32[]{:S(2)}) async-start(), calls=%async_computation.5 | async-start | bytes 5734400 | tf_op jit(solution)/shard_map/reduce_scatter | solution.py:185
  272.0 5.7 %copy-start.4 = (f32[128]{0:T(128)S(1)}, f32[128]{0:T(128)}, u32[]{:S(2)}) copy-start(f32[128]{0:T(128)} %param.13) | copy-start | bytes 1540
  275.4 2.4 copy-start.3
  275.4 4.3 %copy-start.1 = (bf16[128,7168]{1,0:T(8,128)(2,1)S(1)}, bf16[128,7168]{1,0:T(8,128)(2,1)}, u32[]{:S(2)}) copy-start(bf16[128,7168]{1,0:T(8,128)(2,1)} %param.11) | copy-start | bytes 5505028
Sparse Core Ops, SparseCore 0:
  42.3 53.6 all-gather.2
  97.7 53.2 all-gather.4
  153.4 50.2 reduce-scatter.2
  206.0 49.7 reduce-scatter.4

commit v18 on v15

--- a/solution.py
+++ b/solution.py
@@ -154,7 +154,11 @@
         position_of[dz * side + dy] = position
     me = lax.axis_index("group")
     onehot = (target[:, None] == jnp.arange(groups, dtype=jnp.int32)[None, :]).astype(jnp.int32)
-    rank_in = jnp.sum((jnp.cumsum(onehot, axis=0) - onehot) * onehot, axis=1)
+    earlier = (
+        jnp.arange(tok_count, dtype=jnp.int32)[:, None] > jnp.arange(tok_count, dtype=jnp.int32)[None, :]
+    ).astype(jnp.bfloat16)
+    before = jnp.dot(earlier, onehot.astype(jnp.bfloat16), preferred_element_type=jnp.float32)
+    rank_in = jnp.sum(before * onehot, axis=1).astype(jnp.int32)
     relative_z = lax.rem(target // side - me // side + rows, rows)
     relative_y = lax.rem(lax.rem(target, side) - lax.rem(me, side) + side, side)
     relative = jnp.where(target < groups, relative_z * side + relative_y, 0)

time: 285 us -> 284 us (level)
  transfers between devices with their start and end apart: 4 -> 4, of which waited for: 4 -> 4; matrix products, arithmetic and copies ran while one was open for 32% -> 32% of each run, Pallas kernels for 20% -> 21%
where the time goes in v18:
time: 284 us; the launch traced here: 283 us
  Pallas kernels  101 us (36%)
  waiting for transfers between devices  62.7 us (22%)
  matrix products  59.9 us (21%)
  local copies, waits for them, and re-layouts  29.8 us (10%)
  other arithmetic  16.1 us (6%)
  between operations  13.3 us (5%)
    pallas_call x4, Pallas kernels, group_exchange(): pl.pallas_call(functools.partial(exchange_kernel, groups, tuple(offsets),...  84.8 us
    dot_general x2, matrix products, expert_part(): return jnp.dot(hidden, down_mat, preferred_element_type=jnp.float32)  39.6 us
    all_gather x2, waiting for transfers between devices, body(): gathered = lax.all_gather(rows, 'inner', axis=0, tiled=True)  38.5 us
    reduce_scatter x2, waiting for transfers between devices, body(): lax.psum_scatter(pair_sum.astype(jnp.bfloat16).reshape((-1,) + slab), 'in...  24.2 us
    pallas_call x2, Pallas kernels, partner_swap(): pl.pallas_call(swap_kernel, out_shape=jax.ShapeDtypeStruct(x.shape[:1] +...  16.2 us
    convert_element_type x2, other arithmetic, body(): pair_sum.astype(jnp.bfloat16).reshape((-1,) + slab)  15.4 us
    reshape x2, local copies, waits for them, and re-layouts, body(): pair_sum.astype(jnp.bfloat16).reshape((-1,) + slab)  15.3 us
    dot_general x2, matrix products, expert_part(): gate_pre = jnp.dot(rows_in, gate_mat, preferred_element_type=jnp.float32)  14.3 us
  transfers between devices with their start and end apart: 4, of which 4 were waited for; matrix products, arithmetic and copies ran while one was open for 32% of the time, Pallas kernels for 21%

profile of v18, /device:TPU:0, one launch (start us, length us, event | category | flops | bytes accessed | tf_op | source)
XLA Modules:
  0.0 283.3 jit_solution(334880875270168348)
XLA Ops:
  6.5 1.0 fusion.31
  7.5 0.7 compare_select_fusion.23
  8.2 0.7 convolution_convert_fusion.2
  9.0 0.2 fusion.53
  9.1 1.4 reshape.44.x_ref
  10.5 26.4 %shard_map.73 = bf16[8,560,128]{2,1,0:T(8,128)(2,1)} custom-call(bf16[8,560,128]{2,1,0:T(8,128)(2,1)} %reshape.44.x_ref), custom_call_target="tpu_custom_call" | custom-call | tf_op jit(solution)/shard_map/pallas_call | solution.py:90
  36.9 2.4 reshape.45
  39.3 1.4 reshape.50.x_ref
  40.7 15.4 %shard_map.76 = bf16[8,560,128]{2,1,0:T(8,128)(2,1)} custom-call(bf16[8,560,128]{2,1,0:T(8,128)(2,1)} %reshape.50.x_ref), custom_call_target="tpu_custom_call" | custom-call | tf_op jit(solution)/shard_map/pallas_call | solution.py:90
  56.1 2.4 reshape.51
  58.5 0.2 reduce-scatter.3.cloned.1.call-start
  58.8 34.4 %all-gather.3.cloned.1.call-done = bf16[640,7168]{1,0:T(8,128)(2,1)} async-done(((bf16[80,7168]{1,0:T(8,128)(2,1)}), bf16[640,7168]{1,0:T(8,128)(2,1)}) %all-gather.3.cloned.1.call-update) | async-done | bytes 9175056 | tf_op jit(solution)/shard_map/all_gather | solution.py:180
  93.1 7.2 %fusion.13 = f32[640,256]{1,0:T(8,128)S(1)} fusion(bf16[640,7168]{1,0:T(8,128)(2,1)} %all-gather.3.cloned.1.call-done, bf16[1,7168,256]{2,1,0:T(8,128)(2,1)} %param.10), kind=kOutput, calls=%fused_computation.20 | convolution fusion | flops 2348810240 | bytes 13500416 | tf_op jit(solution)/shard_map/dot_general | solution.py:137
  100.3 19.8 %convolution_convert_fusion.1 = bf16[640,7168]{1,0:T(8,128)(2,1)} fusion(bf16[1,256,7168]{2,1,0:T(8,128)(2,1)} %param.12, bf16[640,7168]{1,0:T(8,128)(2,1)} %all-gather.3.cloned.1.call-done, bf16[1,7168,256]{2,1,0:T(8,128)(2,1)} %param.11, f32[640,256]{1,0:T(8,128)S(1)} %fusion.13), kind=kOutput, calls=%fused_computation.1 | convolution fusion | flops 4703191040 | bytes 26345472 | tf_op jit(solution)/shard_map/dot_general | solution.py:140
  120.1 8.1 %shard_map.74 = bf16[4,80,7168]{2,1,0:T(8,128)(2,1)} custom-call(bf16[4,2,80,7168]{3,2,1,0:T(8,128)(2,1)} %bitcast.56), custom_call_target="tpu_custom_call" | custom-call | tf_op jit(solution)/shard_map/pallas_call | solution.py:126
  128.2 7.8 %fusion.1 = bf16[4,80,7168]{2,1,0:T(8,128)(2,1)} fusion(bf16[4,80,7168]{2,1,0:T(8,128)(2,1)} %shard_map.74, bf16[4,2,80,7168]{3,2,1,0:T(8,128)(2,1)} %bitcast.57, s32[]{:T(128)S(6)} %select_n.30), kind=kLoop, calls=%fused_computation.5 | loop fusion | flops 9175040 | bytes 13762564 | tf_op jit(solution)/shard_map/convert_element_type | solution.py:191
  136.0 7.7 %reshape.47 = bf16[32,560,128]{2,1,0:T(8,128)(2,1)} reshape(bf16[4,80,7168]{2,1,0:T(8,128)(2,1)} %fusion.1) | data formatting | bytes 9175040 | tf_op jit(solution)/shard_map/reshape | solution.py:191
  143.7 0.3 reduce-scatter.5.cloned.1.call-start
  143.9 4.1 %all-gather.5.cloned.1.call-done = bf16[640,7168]{1,0:T(8,128)(2,1)} async-done(((bf16[80,7168]{1,0:T(8,128)(2,1)}), bf16[640,7168]{1,0:T(8,128)(2,1)}) %all-gather.5.cloned.1.call-update) | async-done | bytes 9175056 | tf_op jit(solution)/shard_map/all_gather | solution.py:180
  148.1 7.2 %fusion.11 = f32[640,256]{1,0:T(8,128)S(1)} fusion(bf16[640,7168]{1,0:T(8,128)(2,1)} %all-gather.5.cloned.1.call-done, bf16[1,7168,256]{2,1,0:T(8,128)(2,1)} %param.10), kind=kOutput, calls=%fused_computation.18 | convolution fusion | flops 2348810240 | bytes 13500416 | tf_op jit(solution)/shard_map/dot_general | solution.py:137
  155.2 19.8 %convolution_convert_fusion = bf16[640,7168]{1,0:T(8,128)(2,1)} fusion(bf16[1,256,7168]{2,1,0:T(8,128)(2,1)} %param.12, bf16[640,7168]{1,0:T(8,128)(2,1)} %all-gather.5.cloned.1.call-done, bf16[1,7168,256]{2,1,0:T(8,128)(2,1)} %param.11, f32[640,256]{1,0:T(8,128)S(1)} %fusion.11), kind=kOutput, calls=%fused_computation | convolution fusion | flops 4703191040 | bytes 26345472 | tf_op jit(solution)/shard_map/dot_general | solution.py:140
  175.0 8.1 %shard_map.77 = bf16[4,80,7168]{2,1,0:T(8,128)(2,1)} custom-call(bf16[4,2,80,7168]{3,2,1,0:T(8,128)(2,1)} %bitcast.54), custom_call_target="tpu_custom_call" | custom-call | tf_op jit(solution)/shard_map/pallas_call | solution.py:126
  183.1 7.6 %fusion = bf16[4,80,7168]{2,1,0:T(8,128)(2,1)} fusion(bf16[4,80,7168]{2,1,0:T(8,128)(2,1)} %shard_map.77, bf16[4,2,80,7168]{3,2,1,0:T(8,128)(2,1)} %bitcast.55, s32[]{:T(128)S(6)} %select_n.30), kind=kLoop, calls=%fused_computation.3 | loop fusion | flops 9175040 | bytes 13762564 | tf_op jit(solution)/shard_map/convert_element_type | solution.py:191
  190.7 7.7 %reshape.53 = bf16[32,560,128]{2,1,0:T(8,128)(2,1)} reshape(bf16[4,80,7168]{2,1,0:T(8,128)(2,1)} %fusion) | data formatting | bytes 9175040 | tf_op jit(solution)/shard_map/reshape | solution.py:191
  198.5 2.3 reduce-scatter.3.cloned.1.call-done.x_ref
  200.7 26.7 %shard_map.75 = bf16[8,560,128]{2,1,0:T(8,128)(2,1)} custom-call(bf16[8,560,128]{2,1,0:T(8,128)(2,1)} %reduce-scatter.3.cloned.1.call-done.x_ref), custom_call_target="tpu_custom_call" | custom-call | tf_op jit(solution)/shard_map/pallas_call | solution.py:90
  227.4 3.4 %reshape.48 = bf16[8,10,7168]{2,1,0:T(8,128)(2,1)} reshape(bf16[8,560,128]{2,1,0:T(8,128)(2,1)} %shard_map.75) | data formatting | bytes 2293760 | tf_op jit(solution)/shard_map/reshape | solution.py:211
  230.8 21.9 %reduce-scatter.5.cloned.1.call-done.x_ref = bf16[8,560,128]{2,1,0:T(8,128)(2,1)} async-done(((bf16[32,560,128]{2,1,0:T(8,128)(2,1)}), bf16[8,560,128]{2,1,0:T(8,128)(2,1)}) %reduce-scatter.5.cloned.1.call-update) | async-done | bytes 1146896 | tf_op jit(solution)/shard_map/reduce_scatter | solution.py:190
  252.8 16.3 %shard_map.78 = bf16[8,560,128]{2,1,0:T(8,128)(2,1)} custom-call(bf16[8,560,128]{2,1,0:T(8,128)(2,1)} %reduce-scatter.5.cloned.1.call-done.x_ref), custom_call_target="tpu_custom_call" | custom-call | tf_op jit(solution)/shard_map/pallas_call | solution.py:90
  269.1 3.4 %reshape.54 = bf16[8,10,7168]{2,1,0:T(8,128)(2,1)} reshape(bf16[8,560,128]{2,1,0:T(8,128)(2,1)} %shard_map.78) | data formatting | bytes 2293760 | tf_op jit(solution)/shard_map/reshape | solution.py:211
  272.5 2.3 convolution_bitcast_fusion
  274.9 1.9 fusion.4
  (18 shorter events, 0.2 us)
Async XLA Ops:
  6.5 1.7 copy-start
  6.5 86.6 %all-gather.3.cloned.1.call-start = ((), (), s32[]{:S(2)}) async-start(), calls=%async_computation.2 | async-start | bytes 10321920 | tf_op jit(solution)/shard_map/all_gather | solution.py:180
  39.3 108.8 %all-gather.5.cloned.1.call-start = ((), (), s32[]{:S(2)}) async-start(), calls=%async_computation.4 | async-start | bytes 10321920 | tf_op jit(solution)/shard_map/all_gather | solution.py:180
  58.5 142.2 %reduce-scatter.3.cloned.1.call-start = ((), (), s32[]{:S(2)}) async-start(), calls=%async_computation.3 | async-start | bytes 5734400 | tf_op jit(solution)/shard_map/reduce_scatter | solution.py:190
  143.7 109.1 %reduce-scatter.5.cloned.1.call-start = ((), (), s32[]{:S(2)}) async-start(), calls=%async_computation.5 | async-start | bytes 5734400 | tf_op jit(solution)/shard_map/reduce_scatter | solution.py:190
  269.1 5.7 %copy-start.3 = (f32[128]{0:T(128)S(1)}, f32[128]{0:T(128)}, u32[]{:S(2)}) copy-start(f32[128]{0:T(128)} %param.9) | copy-start | bytes 1540
  272.5 2.4 copy-start.2
  272.5 4.3 %copy-start.1 = (bf16[128,7168]{1,0:T(8,128)(2,1)S(1)}, bf16[128,7168]{1,0:T(8,128)(2,1)}, u32[]{:S(2)}) copy-start(bf16[128,7168]{1,0:T(8,128)(2,1)} %param.7) | copy-start | bytes 5505028
Sparse Core Ops, SparseCore 0:
  39.4 53.6 all-gather.2
  94.8 53.2 all-gather.4
  150.5 50.2 reduce-scatter.2
  203.0 49.7 reduce-scatter.4

commit v19 on v18

--- a/solution.py
+++ b/solution.py
@@ -167,13 +167,16 @@
     dispatch = (slot_of[None, :] == jnp.arange(slot_count, dtype=jnp.int32)[:, None]).astype(
         jnp.bfloat16
     )
-    outbound = jnp.dot(dispatch, tokens, preferred_element_type=jnp.float32).astype(jnp.bfloat16)
     lanes = 128 if (capacity * model_width) % 128 == 0 else model_width
     slab = (capacity * model_width // lanes, lanes)
     returned = []
     base = 0
     for index, chunk in enumerate(chunks):
-        piece = outbound[base * capacity : (base + len(chunk)) * capacity]
+        piece = jnp.dot(
+            dispatch[base * capacity : (base + len(chunk)) * capacity],
+            tokens,
+            preferred_element_type=jnp.float32,
+        ).astype(jnp.bfloat16)
         received = group_exchange(piece.reshape((len(chunk),) + slab), chunk, 0, 1, 2 * index)
         base += len(chunk)
         rows = received.reshape(len(chunk) * capacity, model_width)

time: 284 us -> 283 us (level)
  transfers between devices with their start and end apart: 4 -> 4, of which waited for: 4 -> 4; matrix products, arithmetic and copies ran while one was open for 32% -> 33% of each run, Pallas kernels for 21% -> 21%
where the time goes in v19:
time: 283 us
  Pallas kernels  101 us (36%)
  waiting for transfers between devices  62.3 us (22%)
  matrix products  60.1 us (21%)
  local copies, waits for them, and re-layouts  29.7 us (10%)
  other arithmetic  16.1 us (6%)
  between operations  13.3 us (5%)
    pallas_call x4, Pallas kernels, group_exchange(): pl.pallas_call(functools.partial(exchange_kernel, groups, tuple(offsets),...  84.8 us
    dot_general x2, matrix products, expert_part(): return jnp.dot(hidden, down_mat, preferred_element_type=jnp.float32)  39.6 us
    all_gather x2, waiting for transfers between devices, body(): gathered = lax.all_gather(rows, 'inner', axis=0, tiled=True)  38 us
    reduce_scatter x2, waiting for transfers between devices, body(): lax.psum_scatter(pair_sum.astype(jnp.bfloat16).reshape((-1,) + slab), 'in...  24.2 us
    pallas_call x2, Pallas kernels, partner_swap(): pl.pallas_call(swap_kernel, out_shape=jax.ShapeDtypeStruct(x.shape[:1] +...  16.2 us
    convert_element_type x2, other arithmetic, body(): pair_sum.astype(jnp.bfloat16).reshape((-1,) + slab)  15.4 us
    reshape x2, local copies, waits for them, and re-layouts, body(): pair_sum.astype(jnp.bfloat16).reshape((-1,) + slab)  15.3 us
    dot_general x2, matrix products, expert_part(): gate_pre = jnp.dot(rows_in, gate_mat, preferred_element_type=jnp.float32)  14.3 us
  transfers between devices with their start and end apart: 4, of which 4 were waited for; matrix products, arithmetic and copies ran while one was open for 33% of the time, Pallas kernels for 21%

profile of v19, /device:TPU:0, one launch (start us, length us, event | category | flops | bytes accessed | tf_op | source)
XLA Modules:
  0.0 282.9 jit_solution(3646562520167278933)
XLA Ops:
  6.5 1.0 fusion.31
  7.5 0.7 compare_select_fusion.23
  8.2 0.5 convolution_convert_fusion.3
  8.7 1.4 reshape.44.x_ref
  10.1 26.4 %shard_map.73 = bf16[8,560,128]{2,1,0:T(8,128)(2,1)} custom-call(bf16[8,560,128]{2,1,0:T(8,128)(2,1)} %reshape.44.x_ref), custom_call_target="tpu_custom_call" | custom-call | tf_op jit(solution)/shard_map/pallas_call | solution.py:90
  36.4 2.4 reshape.45
  38.9 0.5 convolution_convert_fusion.2
  39.3 1.4 reshape.50.x_ref
  40.7 15.4 %shard_map.76 = bf16[8,560,128]{2,1,0:T(8,128)(2,1)} custom-call(bf16[8,560,128]{2,1,0:T(8,128)(2,1)} %reshape.50.x_ref), custom_call_target="tpu_custom_call" | custom-call | tf_op jit(solution)/shard_map/pallas_call | solution.py:90
  56.1 2.4 reshape.51
  58.5 0.2 reduce-scatter.3.cloned.1.call-start
  58.8 33.9 %all-gather.3.cloned.1.call-done = bf16[640,7168]{1,0:T(8,128)(2,1)} async-done(((bf16[80,7168]{1,0:T(8,128)(2,1)}), bf16[640,7168]{1,0:T(8,128)(2,1)}) %all-gather.3.cloned.1.call-update) | async-done | bytes 9175056 | tf_op jit(solution)/shard_map/all_gather | solution.py:183
  92.7 7.2 %fusion.13 = f32[640,256]{1,0:T(8,128)S(1)} fusion(bf16[640,7168]{1,0:T(8,128)(2,1)} %all-gather.3.cloned.1.call-done, bf16[1,7168,256]{2,1,0:T(8,128)(2,1)} %param.10), kind=kOutput, calls=%fused_computation.21 | convolution fusion | flops 2348810240 | bytes 13500416 | tf_op jit(solution)/shard_map/dot_general | solution.py:137
  99.9 19.8 %convolution_convert_fusion.1 = bf16[640,7168]{1,0:T(8,128)(2,1)} fusion(bf16[1,256,7168]{2,1,0:T(8,128)(2,1)} %param.12, bf16[640,7168]{1,0:T(8,128)(2,1)} %all-gather.3.cloned.1.call-done, bf16[1,7168,256]{2,1,0:T(8,128)(2,1)} %param.11, f32[640,256]{1,0:T(8,128)S(1)} %fusion.13), kind=kOutput, calls=%fused_computation.1 | convolution fusion | flops 4703191040 | bytes 26345472 | tf_op jit(solution)/shard_map/dot_general | solution.py:140
  119.7 8.1 %shard_map.74 = bf16[4,80,7168]{2,1,0:T(8,128)(2,1)} custom-call(bf16[4,2,80,7168]{3,2,1,0:T(8,128)(2,1)} %bitcast.57), custom_call_target="tpu_custom_call" | custom-call | tf_op jit(solution)/shard_map/pallas_call | solution.py:126
  127.8 7.8 %fusion.1 = bf16[4,80,7168]{2,1,0:T(8,128)(2,1)} fusion(bf16[4,80,7168]{2,1,0:T(8,128)(2,1)} %shard_map.74, bf16[4,2,80,7168]{3,2,1,0:T(8,128)(2,1)} %bitcast.58, s32[]{:T(128)S(6)} %select_n.30), kind=kLoop, calls=%fused_computation.5 | loop fusion | flops 9175040 | bytes 13762564 | tf_op jit(solution)/shard_map/convert_element_type | solution.py:194
  135.6 7.7 %reshape.47 = bf16[32,560,128]{2,1,0:T(8,128)(2,1)} reshape(bf16[4,80,7168]{2,1,0:T(8,128)(2,1)} %fusion.1) | data formatting | bytes 9175040 | tf_op jit(solution)/shard_map/reshape | solution.py:194
  143.3 0.3 reduce-scatter.5.cloned.1.call-start
  143.5 4.1 %all-gather.5.cloned.1.call-done = bf16[640,7168]{1,0:T(8,128)(2,1)} async-done(((bf16[80,7168]{1,0:T(8,128)(2,1)}), bf16[640,7168]{1,0:T(8,128)(2,1)}) %all-gather.5.cloned.1.call-update) | async-done | bytes 9175056 | tf_op jit(solution)/shard_map/all_gather | solution.py:183
  147.6 7.2 %fusion.11 = f32[640,256]{1,0:T(8,128)S(1)} fusion(bf16[640,7168]{1,0:T(8,128)(2,1)} %all-gather.5.cloned.1.call-done, bf16[1,7168,256]{2,1,0:T(8,128)(2,1)} %param.10), kind=kOutput, calls=%fused_computation.19 | convolution fusion | flops 2348810240 | bytes 13500416 | tf_op jit(solution)/shard_map/dot_general | solution.py:137
  154.8 19.8 %convolution_convert_fusion = bf16[640,7168]{1,0:T(8,128)(2,1)} fusion(bf16[1,256,7168]{2,1,0:T(8,128)(2,1)} %param.12, bf16[640,7168]{1,0:T(8,128)(2,1)} %all-gather.5.cloned.1.call-done, bf16[1,7168,256]{2,1,0:T(8,128)(2,1)} %param.11, f32[640,256]{1,0:T(8,128)S(1)} %fusion.11), kind=kOutput, calls=%fused_computation | convolution fusion | flops 4703191040 | bytes 26345472 | tf_op jit(solution)/shard_map/dot_general | solution.py:140
  174.6 8.1 %shard_map.77 = bf16[4,80,7168]{2,1,0:T(8,128)(2,1)} custom-call(bf16[4,2,80,7168]{3,2,1,0:T(8,128)(2,1)} %bitcast.55), custom_call_target="tpu_custom_call" | custom-call | tf_op jit(solution)/shard_map/pallas_call | solution.py:126
  182.7 7.6 %fusion = bf16[4,80,7168]{2,1,0:T(8,128)(2,1)} fusion(bf16[4,80,7168]{2,1,0:T(8,128)(2,1)} %shard_map.77, bf16[4,2,80,7168]{3,2,1,0:T(8,128)(2,1)} %bitcast.56, s32[]{:T(128)S(6)} %select_n.30), kind=kLoop, calls=%fused_computation.3 | loop fusion | flops 9175040 | bytes 13762564 | tf_op jit(solution)/shard_map/convert_element_type | solution.py:194
  190.3 7.7 %reshape.53 = bf16[32,560,128]{2,1,0:T(8,128)(2,1)} reshape(bf16[4,80,7168]{2,1,0:T(8,128)(2,1)} %fusion) | data formatting | bytes 9175040 | tf_op jit(solution)/shard_map/reshape | solution.py:194
  198.0 2.3 reduce-scatter.3.cloned.1.call-done.x_ref
  200.3 26.7 %shard_map.75 = bf16[8,560,128]{2,1,0:T(8,128)(2,1)} custom-call(bf16[8,560,128]{2,1,0:T(8,128)(2,1)} %reduce-scatter.3.cloned.1.call-done.x_ref), custom_call_target="tpu_custom_call" | custom-call | tf_op jit(solution)/shard_map/pallas_call | solution.py:90
  227.0 3.4 %reshape.48 = bf16[8,10,7168]{2,1,0:T(8,128)(2,1)} reshape(bf16[8,560,128]{2,1,0:T(8,128)(2,1)} %shard_map.75) | data formatting | bytes 2293760 | tf_op jit(solution)/shard_map/reshape | solution.py:214
  230.4 21.9 %reduce-scatter.5.cloned.1.call-done.x_ref = bf16[8,560,128]{2,1,0:T(8,128)(2,1)} async-done(((bf16[32,560,128]{2,1,0:T(8,128)(2,1)}), bf16[8,560,128]{2,1,0:T(8,128)(2,1)}) %reduce-scatter.5.cloned.1.call-update) | async-done | bytes 1146896 | tf_op jit(solution)/shard_map/reduce_scatter | solution.py:193
  252.4 16.3 %shard_map.78 = bf16[8,560,128]{2,1,0:T(8,128)(2,1)} custom-call(bf16[8,560,128]{2,1,0:T(8,128)(2,1)} %reduce-scatter.5.cloned.1.call-done.x_ref), custom_call_target="tpu_custom_call" | custom-call | tf_op jit(solution)/shard_map/pallas_call | solution.py:90
  268.7 3.4 %reshape.54 = bf16[8,10,7168]{2,1,0:T(8,128)(2,1)} reshape(bf16[8,560,128]{2,1,0:T(8,128)(2,1)} %shard_map.78) | data formatting | bytes 2293760 | tf_op jit(solution)/shard_map/reshape | solution.py:214
  272.1 2.3 convolution_bitcast_fusion
  274.4 1.9 fusion.4
  (18 shorter events, 0.2 us)
Async XLA Ops:
  6.5 1.7 copy-start
  6.5 86.2 %all-gather.3.cloned.1.call-start = ((), (), s32[]{:S(2)}) async-start(), calls=%async_computation.2 | async-start | bytes 10321920 | tf_op jit(solution)/shard_map/all_gather | solution.py:183
  38.8 108.8 %all-gather.5.cloned.1.call-start = ((), (), s32[]{:S(2)}) async-start(), calls=%async_computation.4 | async-start | bytes 10321920 | tf_op jit(solution)/shard_map/all_gather | solution.py:183
  58.5 141.8 %reduce-scatter.3.cloned.1.call-start = ((), (), s32[]{:S(2)}) async-start(), calls=%async_computation.3 | async-start | bytes 5734400 | tf_op jit(solution)/shard_map/reduce_scatter | solution.py:193
  143.3 109.1 %reduce-scatter.5.cloned.1.call-start = ((), (), s32[]{:S(2)}) async-start(), calls=%async_computation.5 | async-start | bytes 5734400 | tf_op jit(solution)/shard_map/reduce_scatter | solution.py:193
  268.7 5.7 %copy-start.3 = (f32[128]{0:T(128)S(1)}, f32[128]{0:T(128)}, u32[]{:S(2)}) copy-start(f32[128]{0:T(128)} %param.9) | copy-start | bytes 1540
  272.1 2.4 copy-start.2
  272.1 4.3 %copy-start.1 = (bf16[128,7168]{1,0:T(8,128)(2,1)S(1)}, bf16[128,7168]{1,0:T(8,128)(2,1)}, u32[]{:S(2)}) copy-start(bf16[128,7168]{1,0:T(8,128)(2,1)} %param.7) | copy-start | bytes 5505028
Sparse Core Ops, SparseCore 0:
  39.0 53.6 all-gather.2
  94.4 53.2 all-gather.4
  150.1 50.2 reduce-scatter.2
  202.6 49.7 reduce-scatter.4
